TPU v7x, 32 devices: a whole 2x2x4 slice. The times are simulated.
32 devices in a mesh: macro: 4 (over y, x), micro: 8 (over z, core).
Axes of the slice: x: 2, y: 2, z: 4, core: 2. Of those that a mesh axis runs over, the one named last changes fastest.
Arguments:
- displacement: float32 [3, 8, 16, 256], P(None, 'macro', 'micro'), may hold values from -6 to 6
- load: float32 [3, 8, 16, 256], P(None, 'macro', 'micro'), may hold values from -6 to 6
- routes: int32 [4, 8, 1024, 1], P('macro', 'micro'), may hold values from 0 to 7; in each aligned block of 1024 rows (0 to 1023, 1024 to 2047, ..., all dimensions but the last counted through in order) at most 256 rows name the same one
- counts: int32 [4, 8, 1024], P('macro', 'micro'), may hold values from 1 to 4
- stiffness: bfloat16 [8, 512, 512], P('micro'), may hold values from -0.5 to 2.5, as said below
- precond: bfloat16 [8, 512, 512], P('micro'), may hold values from -0.5 to 2.5, as said below
- forcing: bfloat16 [8, 6, 512], P('micro'), may hold values from -2.5 to 2.5
- coupling: bfloat16 [8, 512, 6], P('micro'), may hold values from -0.25 to 0.25
- lame_first: float32 [8], P('micro'), may hold values from 0.5 to 2
- lame_shear: float32 [8], P('micro'), may hold values from 0.5 to 2
Outputs:
- increment: float32 [3, 8, 16, 256], P(None, 'macro', 'micro')
- residual: float32 [3, 8, 16, 256], P(None, 'macro', 'micro')
Inputs may be any that keep to these rules, and one draw needn't show every extreme that they name: `routes`: among the points of one block (one device's points), no owner is named by more than 256 points, a bound that some block reaches. `stiffness`: Symmetric. `precond`: Symmetric.
All inputs are finite; a program needn't handle non-finite values.
Results may differ from a plain program's by a relative error of at most 0.002.
Values sent between devices are 32-bit elements; how exact they have to be, the bound alone decides.
A program may use at most 64 MiB of HBM per device.

v0:
```python
import jax
import jax.numpy as jnp
from jax import lax
from jax.experimental import pallas as pl
from jax.experimental.pallas import tpu as pltpu
from jax.sharding import PartitionSpec as P

ITMAX = 4
ITERS = 5


BETA = 0.1
OMEGA = 0.8
MASS = 0.1
VOIGT = ((0, 5, 4), (5, 1, 3), (4, 3, 2))
PAIRS = tuple((first, second) for first in range(6) for second in range(first, 6))
PAIR_AT = {pair: at for at, pair in enumerate(PAIRS)}
AROUND = tuple((dx, dy) for dx in (-1, 0, 1) for dy in (-1, 0, 1) if (dx, dy) != (0, 0))
MESH = pl.DeviceIdType.MESH


def with_halo(block, sides, width):
    for axis, dim in sides:
        count = lax.axis_size(axis)
        forward = [(i, i + 1) for i in range(count - 1)]
        backward = [(target, source) for source, target in forward]
        low = lax.ppermute(
            lax.slice_in_dim(block, block.shape[dim] - width, None, axis=dim), axis, forward
        )
        high = lax.ppermute(lax.slice_in_dim(block, 0, width, axis=dim), axis, backward)
        block = jnp.concatenate([low, block, high], axis=dim)
    return block


def passed_along(value, axis, steps):
    count = lax.axis_size(axis)
    initial, last = (max(0, -steps), min(count, count - steps))
    return lax.ppermute(value, axis, [(source, source + steps) for source in range(initial, last)])


def element_strain(nodes):
    count_x = nodes.shape[1] - 1
    count_y = nodes.shape[2] - 1
    count_z = nodes.shape[3]
    padded = jnp.pad(nodes, ((0, 0), (0, 0), (0, 0), (0, 1)))
    zeros = jnp.zeros((3, count_x, count_y, count_z), jnp.float32)
    grad_x, grad_y, grad_z = (zeros, zeros, zeros)
    for corner_x in (0, 1):
        for corner_y in (0, 1):
            for corner_z in (0, 1):
                piece = padded[
                    :,
                    corner_x : corner_x + count_x,
                    corner_y : corner_y + count_y,
                    corner_z : corner_z + count_z,
                ]
                grad_x = grad_x + 0.25 * (2 * corner_x - 1) * piece
                grad_y = grad_y + 0.25 * (2 * corner_y - 1) * piece
                grad_z = grad_z + 0.25 * (2 * corner_z - 1) * piece
    return jnp.stack(
        [
            grad_x[0],
            grad_y[1],
            grad_z[2],
            grad_z[1] + grad_y[2],
            grad_z[0] + grad_x[2],
            grad_y[0] + grad_x[1],
        ]
    )


def node_force(stress):
    count_x, count_y, count_z = (stress.shape[1], stress.shape[2], stress.shape[3])
    forces = jnp.zeros((3, count_x + 1, count_y + 1, count_z + 1), jnp.float32)
    for corner_x in (0, 1):
        for corner_y in (0, 1):
            for corner_z in (0, 1):
                signs = (2 * corner_x - 1, 2 * corner_y - 1, 2 * corner_z - 1)
                parts = []
                for component in range(3):
                    table = VOIGT[component]
                    parts.append(
                        0.25
                        * (
                            signs[0] * stress[table[0]]
                            + signs[1] * stress[table[1]]
                            + signs[2] * stress[table[2]]
                        )
                    )
                contrib = jnp.stack(parts)
                forces = forces + jnp.pad(
                    contrib,
                    (
                        (0, 0),
                        (corner_x, 1 - corner_x),
                        (corner_y, 1 - corner_y),
                        (corner_z, 1 - corner_z),
                    ),
                )
    return forces


def micro_kernel(bundle_ref, stiff_ref, pre_ref, force_ref, couple_ref, product_ref, coef_ref, out_ref):
    bundle = bundle_ref[...]
    sweeps = bundle[6:7]
    modal_load = jnp.dot(
        force_ref[...], bundle.astype(jnp.bfloat16), preferred_element_type=jnp.float32
    )
    modes = None
    for sweep in range(ITMAX):
        misfit = -modal_load
        if modes is not None:
            misfit = (
                jnp.dot(
                    stiff_ref[...], modes.astype(jnp.bfloat16), preferred_element_type=jnp.float32
                )
                + BETA * jnp.tanh(modes)
                - modal_load
            )
        change = OMEGA * jnp.dot(
            pre_ref[...], misfit.astype(jnp.bfloat16), preferred_element_type=jnp.float32
        )
        before = jnp.zeros_like(change) if modes is None else modes
        modes = jnp.where(sweeps > sweep, before - change, before)
    bent = jnp.tanh(modes)
    slope = 1.0 - bent * bent
    trace = bundle[0:1] + bundle[1:2] + bundle[2:3]
    rows = coef_ref.shape[0]
    tall = jnp.concatenate(
        [bundle, jnp.zeros((rows - bundle.shape[0], bundle.shape[1]), jnp.float32)], axis=0
    )
    coef = coef_ref[...]
    total = coef[:, 0:1] * trace + coef[:, 1:2] * tall + coef[:, 2:3]
    total = total + jnp.dot(
        couple_ref[...], modes.astype(jnp.bfloat16), preferred_element_type=jnp.float32
    )
    total = total + jnp.dot(
        product_ref[...], slope.astype(jnp.bfloat16), preferred_element_type=jnp.float32
    )
    out_ref[...] = total[: out_ref.shape[0]]


def micro_solve(bundle, stiffness, precond, forcing, coupling, lame_first, lame_shear, pairs):
    size, points = stiffness.shape[0], bundle.shape[1]
    tile = 512 if points % 512 == 0 else points
    count = 6 + len(pairs)
    rows = -(-count // 8) * 8
    force = jnp.pad(forcing.T, ((0, 0), (0, 2)))
    wide = coupling.astype(jnp.float32).T
    products = jnp.stack([wide[first] * wide[second] for first, second in pairs])
    products = jnp.pad(products.astype(jnp.bfloat16), ((6, rows - count), (0, 0)))
    couple = jnp.pad(coupling.T, ((0, rows - 6), (0, 0)))
    on_trace = jnp.array([1.0] * 3 + [0.0] * (rows - 3), jnp.float32)
    on_shear = jnp.array([2.0] * 3 + [1.0] * 3 + [0.0] * (rows - 6), jnp.float32)
    base_first = [0.0] * 6 + [float(i < 3 and j < 3) for i, j in pairs] + [0.0] * (rows - count)
    base_shear = (
        [0.0] * 6
        + [float(i == j) * (2.0 if i < 3 else 1.0) for i, j in pairs]
        + [0.0] * (rows - count)
    )
    base = lame_first * jnp.array(base_first, jnp.float32) + lame_shear * jnp.array(
        base_shear, jnp.float32
    )
    coef = jnp.stack([lame_first * on_trace, lame_shear * on_shear, base], axis=1)

    def whole(shape):
        return pl.BlockSpec(shape, lambda i: (0, 0))

    return pl.pallas_call(
        micro_kernel,
        grid=(points // tile,),
        out_shape=jax.ShapeDtypeStruct((count, points), jnp.float32),
        in_specs=[
            pl.BlockSpec((8, tile), lambda i: (0, i)),
            whole((size, size)),
            whole((size, size)),
            whole((size, 8)),
            whole((rows, size)),
            whole((rows, size)),
            whole((rows, 3)),
        ],
        out_specs=pl.BlockSpec((count, tile), lambda i: (0, i)),
        name="micro_solve",
    )(bundle, stiffness, precond, force, couple, products, coef)


def extend(field):
    return with_halo(field, (("macro", 1), ("micro", 2)), 1)


def cg_kernel(
    sizes,
    load_ref,
    elem_ref,
    inc_ref,
    res_ref,
    residual,
    direction,
    along,
    increment,
    image,
    send_halo,
    halo,
    part,
    got_micro,
    middle,
    got_macro,
    send_sem,
    recv_sem,
    micro_send,
    micro_recv,
    macro_send,
    macro_recv,
):
    count_x, count_y, n_macro, n_micro = sizes
    wide = count_y + 2
    rows, lanes = load_ref.shape[1], load_ref.shape[2]
    a, b = lax.axis_index("macro"), lax.axis_index("micro")

    def inside(dx, dy):
        test = None
        for place, step, count in ((a, dx, n_macro), (b, dy, n_micro)):
            if step != 0:
                good = (place > 0) if step < 0 else (place < count - 1)
                test = good if test is None else jnp.logical_and(test, good)
        return test

    barrier = pltpu.get_barrier_semaphore()
    for step in range(1, n_micro):
        pl.semaphore_signal(
            barrier, inc=1, device_id=(a, lax.rem(b + step, n_micro)), device_id_type=MESH
        )
    for step in range(1, n_macro):
        pl.semaphore_signal(
            barrier, inc=1, device_id=(lax.rem(a + step, n_macro), b), device_id_type=MESH
        )
    corners = [(dx, dy) for dx, dy in AROUND if dx != 0 and dy != 0]
    for dx, dy in corners:
        pl.semaphore_signal(
            barrier,
            inc=1,
            device_id=(lax.rem(a + dx + n_macro, n_macro), lax.rem(b + dy + n_micro, n_micro)),
            device_id_type=MESH,
        )
    pl.semaphore_wait(barrier, n_micro - 1 + n_macro - 1 + len(corners))
    for at, (dx, dy) in enumerate(AROUND):

        @pl.when(jnp.logical_not(inside(dx, dy)))
        def _():
            for it in range(ITERS + 1):
                halo[it, at] = jnp.zeros(halo.shape[2:], jnp.float32)

    def near(step, count):
        return {0: list(range(1, count + 1)), -1: [1], 1: [count]}[step]

    def far(step, count):
        return {0: list(range(1, count + 1)), -1: [0], 1: [count + 1]}[step]

    def places(at, pick):
        dx, dy = AROUND[at]
        return [i * wide + j for i in pick(dx, count_x) for j in pick(dy, count_y)]

    def hop(it, at):
        dx, dy = AROUND[at]
        other = len(AROUND) - 1 - at
        return pltpu.make_async_remote_copy(
            src_ref=send_halo.at[it, at],
            dst_ref=halo.at[it, other],
            send_sem=send_sem.at[it, at],
            recv_sem=recv_sem.at[it, other],
            device_id=(a + dx, b + dy),
            device_id_type=MESH,
        )

    def halo_start(it, ref):
        for at, (dx, dy) in enumerate(AROUND):

            @pl.when(inside(dx, dy))
            def _():
                mine = places(at, near)
                for c in range(3):
                    for k, row in enumerate(mine):
                        send_halo[it, at, pl.ds(c * len(mine) + k, 1)] = ref[c, pl.ds(row, 1)]
                hop(it, at).start()

    def halo_finish(it, ref):
        for at, (dx, dy) in enumerate(AROUND):

            @pl.when(inside(dx, dy))
            def _():
                hop(it, at).wait_send()
                pltpu.make_async_remote_copy(
                    src_ref=send_halo.at[it, at],
                    dst_ref=halo.at[it, at],
                    send_sem=send_sem.at[it, at],
                    recv_sem=recv_sem.at[it, at],
                    device_id=(a + dx, b + dy),
                    device_id_type=MESH,
                ).wait_recv()

        for at in range(len(AROUND)):
            theirs = places(at, far)
            for c in range(3):
                for k, row in enumerate(theirs):
                    ref[c, pl.ds(row, 1)] = halo[it, at, pl.ds(c * len(theirs) + k, 1)]

    row_at = lax.broadcasted_iota(jnp.int32, (rows, lanes), 0)
    lane_at = lax.broadcasted_iota(jnp.int32, (rows, lanes), 1)
    own = row_at < 0
    for i in range(1, count_x + 1):
        low = i * wide + 1
        own = jnp.logical_or(own, jnp.logical_and(row_at >= low, row_at < low + count_y))

    def up(value, axis):
        if axis == 2:
            moved = pltpu.roll(value, lanes - 1, 1)
            return jnp.where(lane_at == lanes - 1, 0.0, moved)
        return pltpu.roll(value, rows - (wide if axis == 0 else 1), 0)

    def down(value, axis):
        if axis == 2:
            return jnp.where(lane_at == 0, 0.0, pltpu.roll(value, 1, 1))
        return pltpu.roll(value, wide if axis == 0 else 1, 0)

    def strain_of(ref):
        grads = []
        for c in range(3):
            value = ref[c]
            moved = up(value, 2)
            total, gap = value + moved, moved - value
            total_up, gap_up = up(total, 1), up(gap, 1)
            flat, slope_y, slope_z = total + total_up, total_up - total, gap + gap_up
            grads.append(
                (
                    0.25 * (up(flat, 0) - flat),
                    0.25 * (up(slope_y, 0) + slope_y),
                    0.25 * (up(slope_z, 0) + slope_z),
                )
            )
        return [
            grads[0][0],
            grads[1][1],
            grads[2][2],
            grads[1][2] + grads[2][1],
            grads[0][2] + grads[2][0],
            grads[0][1] + grads[1][0],
        ]

    def force_of(stress, c):
        first, second, third = (stress[VOIGT[c][d]] for d in range(3))
        first = first + down(first, 2)
        second = second + down(second, 2)
        third = down(third, 2) - third
        first = first + down(first, 1)
        rest = down(second, 1) - second + third + down(third, 1)
        return 0.25 * (down(first, 0) - first + rest + down(rest, 0))

    stress = [elem_ref[i] for i in range(6)]
    for c in range(3):
        residual[c] = jnp.where(own, load_ref[c] - force_of(stress, c), 0.0)
        direction[c] = jnp.zeros((rows, lanes), jnp.float32)
        along[c] = jnp.zeros((rows, lanes), jnp.float32)
        increment[c] = jnp.zeros((rows, lanes), jnp.float32)
    halo_start(ITERS, residual)
    halo_finish(ITERS, residual)

    def gather_start(it, src, dst, count, me, send, recv, device):
        copies = []
        for step in range(1, count):
            copy = pltpu.make_async_remote_copy(
                src_ref=src.at[it],
                dst_ref=dst.at[it, me],
                send_sem=send.at[it, step - 1],
                recv_sem=recv.at[it, step - 1],
                device_id=device(lax.rem(me + step, count)),
                device_id_type=MESH,
            )
            copy.start()
            copies.append(copy)
        dst[it, me] = src[it]
        return copies

    def gather_finish(it, copies, dst, count):
        for copy in copies:
            copy.wait()
        total = dst[it, 0]
        for at in range(1, count):
            total = total + dst[it, at]
        return total

    def step_body(it, carry):
        norm_old, alpha_old = carry
        strain = strain_of(residual)
        stress = []
        for i in range(6):
            value = None
            for j in range(6):
                term = elem_ref[6 + PAIR_AT[(min(i, j), max(i, j))]] * strain[j]
                value = term if value is None else value + term
            stress.append(value)
        norm = jnp.zeros((rows, lanes), jnp.float32)
        cross = jnp.zeros((rows, lanes), jnp.float32)
        for c in range(3):
            here = residual[c]
            new = jnp.where(own, MASS * here + force_of(stress, c), 0.0)
            image[c] = new
            kept = jnp.where(own, here, 0.0)
            norm = norm + kept * kept
            cross = cross + kept * new

        def folded(value):
            value = jnp.sum(value, axis=0, keepdims=True)
            total = value[:, :128]
            for at in range(128, lanes, 128):
                total = total + value[:, at : at + 128]
            return total

        tile_row = lax.broadcasted_iota(jnp.int32, (8, 128), 0)
        part[it] = jnp.where(
            tile_row == 0, folded(norm), jnp.where(tile_row == 1, folded(cross), 0.0)
        )
        copies = gather_start(
            it, part, got_micro, n_micro, b, micro_send, micro_recv, lambda other: (a, other)
        )
        halo_start(it, image)
        middle[it] = gather_finish(it, copies, got_micro, n_micro)
        copies = gather_start(
            it, middle, got_macro, n_macro, a, macro_send, macro_recv, lambda other: (other, b)
        )
        halo_finish(it, image)
        totals = jnp.sum(gather_finish(it, copies, got_macro, n_macro), axis=1, keepdims=True)
        norm_now, product = totals[0:1], totals[1:2]
        first = jnp.full((1, 1), it, jnp.int32) == 0
        ratio = jnp.where(first, 0.0, norm_now / norm_old)
        alpha = norm_now / (product - ratio * norm_now / alpha_old)
        for c in range(3):
            here = residual[c]
            toward = here + ratio * direction[c]
            drop = image[c] + ratio * along[c]
            direction[c] = toward
            along[c] = drop
            increment[c] = increment[c] + alpha * toward
            residual[c] = here - alpha * drop
        return norm_now, alpha

    lax.fori_loop(
        0, ITERS, step_body, (jnp.ones((1, 1), jnp.float32), jnp.ones((1, 1), jnp.float32))
    )
    for c in range(3):
        for i in range(count_x):
            low = (i + 1) * wide + 1
            inc_ref[c, i] = increment[c, pl.ds(low, count_y)]
            res_ref[c, i] = residual[c, pl.ds(low, count_y)]


def conjugate_gradients(load, elements):
    _, count_x, count_y, count_z = load.shape
    n_macro, n_micro = lax.axis_size("macro"), lax.axis_size("micro")
    flat = (count_x + 2) * (count_y + 2)
    rows = -(-flat // 8) * 8

    def laid(value, high):
        value = jnp.pad(value, ((0, 0), (1 - high, 1), (1 - high, 1), (0, 0)))
        value = value.reshape(value.shape[0], flat, count_z)
        return jnp.pad(value, ((0, 0), (0, rows - flat), (0, 0)))

    side = -(-3 * max(count_x, count_y) // 8) * 8
    node = pltpu.VMEM((3, rows, count_z), jnp.float32)
    around = pltpu.VMEM((ITERS + 1, len(AROUND), side, count_z), jnp.float32)
    dma = pltpu.SemaphoreType.DMA

    def body(*refs):
        cg_kernel((count_x, count_y, n_macro, n_micro), *refs)

    vmem = pl.BlockSpec(memory_space=pltpu.VMEM)
    return pl.pallas_call(
        body,
        out_shape=[jax.ShapeDtypeStruct(load.shape, jnp.float32)] * 2,
        in_specs=[vmem, vmem],
        out_specs=[vmem, vmem],
        scratch_shapes=[node] * 5
        + [
            around,
            around,
            pltpu.VMEM((ITERS, 8, 128), jnp.float32),
            pltpu.VMEM((ITERS, n_micro, 8, 128), jnp.float32),
            pltpu.VMEM((ITERS, 8, 128), jnp.float32),
            pltpu.VMEM((ITERS, n_macro, 8, 128), jnp.float32),
            dma((ITERS + 1, len(AROUND))),
            dma((ITERS + 1, len(AROUND))),
            dma((ITERS, n_micro - 1)),
            dma((ITERS, n_micro - 1)),
            dma((ITERS, n_macro - 1)),
            dma((ITERS, n_macro - 1)),
        ],
        compiler_params=pltpu.CompilerParams(collective_id=0, has_side_effects=True),
        name="conjugate_gradients",
    )(laid(load, 0), laid(elements, 1))


def shards(
    displacement,
    load,
    routes,
    counts,
    stiffness,
    precond,
    forcing,
    coupling,
    lame_first,
    lame_shear,
):
    count_x, count_y, count_z = (
        displacement.shape[1],
        displacement.shape[2],
        displacement.shape[3],
    )
    points = count_x * count_y * count_z
    owners = lax.axis_size("micro")
    capacity = max(2, 2 * points // owners)
    strain_ext = element_strain(extend(displacement))
    strain_points = strain_ext[:, 1:, 1:].reshape(6, points)
    owner_of = routes.reshape(points)
    sweeps_of = counts.reshape(points)
    onehot = (owner_of[:, None] == jnp.arange(owners, dtype=jnp.int32)[None, :]).astype(jnp.int32)
    ranks = jnp.sum((jnp.cumsum(onehot, axis=0) - 1) * onehot, axis=1)
    target = owner_of * capacity + ranks
    bundle = jnp.concatenate([strain_points, sweeps_of.astype(jnp.float32)[None]], axis=0)
    bundle = jnp.pad(bundle, ((0, 1), (0, 0)))
    send = jnp.zeros((8, owners * capacity), jnp.float32).at[:, target].set(
        bundle, unique_indices=True, mode="promise_in_bounds"
    )
    got = lax.all_to_all(send, "micro", split_axis=1, concat_axis=1, tiled=True)
    rows = micro_solve(
        got,
        stiffness[0],
        precond[0],
        forcing[0],
        coupling[0],
        lame_first[0],
        lame_shear[0],
        PAIRS,
    )
    back = lax.all_to_all(rows, "micro", split_axis=1, concat_axis=1, tiled=True)
    values = jnp.take(back, target, axis=1, unique_indices=True, mode="clip")
    values = values.reshape(back.shape[0], count_x, count_y, count_z)
    left_x = passed_along(values[:, -1:], "macro", 1)
    values = jnp.concatenate([left_x, values], axis=1)
    left_y = passed_along(values[:, :, -1:], "micro", 1)
    values = jnp.concatenate([left_y, values], axis=2)
    return tuple(conjugate_gradients(load, values))


def solution(mesh):
    in_specs = (
        P(None, "macro", "micro", None),
        P(None, "macro", "micro", None),
        P("macro", "micro", None, None),
        P("macro", "micro", None),
        P("micro", None, None),
        P("micro", None, None),
        P("micro", None, None),
        P("micro", None, None),
        P("micro"),
        P("micro"),
    )
    out_specs = (P(None, "macro", "micro", None), P(None, "macro", "micro", None))
    return jax.shard_map(shards, mesh=mesh, in_specs=in_specs, out_specs=out_specs, check_vma=False)
```

profile of v0, /device:TPU:0, one launch (start us, length us, event | category | flops | bytes accessed | tf_op | source)
XLA Modules:
  0.0 130.6 jit_solution(6315789215589275761)
XLA Ops:
  0.6 0.0 copy-start.7
  0.6 0.7 fusion.16
  1.4 4.9 %collective-permute-start = (f32[3,1,2,256]{3,2,1,0:T(2,128)S(1)}, f32[3,1,2,256]{3,2,1,0:T(2,128)S(1)}, u32[]{:S(2)}, u32[]{:S(2)}) collective-permute-start(f32[3,1,2,256]{3,2,1,0:T(2,128)S(1)} %get-tuple-element.28), channel_id=1, source_target_pairs={{0,8},{8,16},{16,24},{1,9},{9,17},{17,25},{2,10},{10,18},{18,26},{... | collective-permute-start | bytes 18440 | tf_op jit(solution)/shard_map/ppermute | solution.py:27
  6.2 0.0 copy-start.2
  6.2 1.3 collective-permute-start.1
  7.5 0.0 copy-done.7
  7.6 0.0 copy-done.2
  7.6 2.3 %reduce-window.6 = s32[8,8,128]{2,1,0:T(8,128)S(1)} reduce-window(s32[8,8,128]{2,1,0:T(8,128)S(1)} %fusion.14, s32[]{:T(128)} %constant.11.clone.1), window={size=1x1x128 pad=0_0x0_0x127_0}, to_apply=%region_0.1 | reduce-window | flops 1040384 | bytes 65540 | tf_op jit(solution)/shard_map/reduce-window
  9.9 0.3 slice_reduce_fusion
  10.1 0.2 reduce-window.9
  10.3 0.1 add_bitcast_fusion
  10.4 0.0 copy-start.3
  10.4 0.7 copy-done.3
  11.1 0.0 copy-start.8
  11.2 0.0 copy-start.9
  11.2 0.0 copy-start.10
  11.2 0.0 copy-start.11
  12.5 0.0 copy-start.1
  12.6 0.0 copy-done.11
  12.6 0.0 collective-permute-done
  12.6 0.6 copy-done.1
  13.2 0.0 collective-permute-done.1
  13.3 1.5 %collective-permute-start.2 = (f32[3,4,1,256]{3,2,1,0:T(1,128)S(1)}, f32[3,4,1,256]{3,2,1,0:T(1,128)S(1)}, u32[]{:S(2)}, u32[]{:S(2)}) collective-permute-start(f32[3,4,1,256]{3,2,1,0:T(1,128)S(1)} %get-tuple-element.4), channel_id=1, source_target_pairs={{0,1},{1,2},{2,3},{3,4},{4,5},{5,6},{6,7},{8,9},{9,10},{10,11},{11... | collective-permute-start | bytes 36872 | tf_op jit(solution)/shard_map/ppermute | solution.py:27
  14.7 1.3 collective-permute-start.3
  16.0 0.0 copy-start.6
  16.1 0.7 copy.38.coef_ref
  16.7 0.0 copy-done.6
  16.7 0.2 copy.37
  16.9 0.0 collective-permute-done.2
  16.9 2.5 %collective-permute-done.3 = f32[3,4,1,256]{3,2,1,0:T(1,128)S(1)} collective-permute-done((f32[3,4,1,256]{3,2,1,0:T(1,128)S(1)}, f32[3,4,1,256]{3,2,1,0:T(1,128)S(1)}, u32[]{:S(2)}, u32[]{:S(2)}) %collective-permute-start.3) | collective-permute-done | bytes 12320 | tf_op jit(solution)/shard_map/ppermute | solution.py:30
  19.5 0.1 add_add_fusion.2
  19.6 0.1 add_add_fusion.1
  19.8 0.1 add_add_fusion
  20.1 0.2 copy.35
  20.3 3.3 %scatter_custom_fusion = f32[8,2048]{0,1:T(8,128)S(1)} fusion(s32[1024]{0:T(1024)S(1)} %bitcast.71, f32[1024,8]{1,0:T(8,128)S(1)} %copy.35, f32[]{:T(128)} %constant.12.clone.1), kind=kCustom, calls=%fused_computation.2 | custom fusion | bytes 65540 | tf_op jit(solution)/shard_map/scatter | solution.py:530
  23.6 0.9 copy.36
  24.6 5.9 %all-to-all-start = ((f32[8,8,256]{2,0,1:T(8,128)}), f32[8,8,256]{2,0,1:T(8,128)S(1)}, u32[]{:S(2)}, u32[]{:S(2)}) async-start(f32[8,8,256]{2,0,1:T(8,128)} %copy.36), calls=%async_computation | async-start | bytes 131072 | tf_op jit(solution)/shard_map/all_to_all | solution.py:533
  30.5 0.1 stack.14
  30.6 0.6 pad.33.product_ref
  31.2 0.7 pad.31.force_ref
  31.9 0.6 pad.32.couple_ref
  32.5 3.9 %all-to-all-done = f32[8,8,256]{2,0,1:T(8,128)S(1)} async-done(((f32[8,8,256]{2,0,1:T(8,128)}), f32[8,8,256]{2,0,1:T(8,128)S(1)}, u32[]{:S(2)}, u32[]{:S(2)}) %all-to-all-start) | async-done | bytes 65568 | tf_op jit(solution)/shard_map/all_to_all | solution.py:533
  36.4 0.6 copy-done
  37.0 14.1 %micro_solve.1 = f32[27,2048]{1,0:T(8,128)} custom-call(f32[8,2048]{1,0:T(8,128)} %bitcast.64, bf16[512,512]{1,0:T(8,128)(2,1)} %bitcast.61, bf16[512,512]{1,0:T(8,128)(2,1)} %bitcast.62, bf16[512,8]{1,0:T(8,128)(2,1)} %pad.31.force_ref, bf16[32,512]{1,0:T(8,128)(2,1)} %pad.32.couple_ref, bf16[32,512]{1,0:T(8,128)(2,1)} %pad.33.product_ref, ...), custom_call_target="tpu_custom_call" | custom-call | tf_op jit(solution)/shard_map/micro_solve/pallas_call | solution.py:169
  51.1 1.0 copy.44
  52.1 0.8 copy.39
  52.9 3.4 %all-to-all-start.1 = ((f32[27,8,256]{2,0,1:T(8,128)}), f32[27,8,256]{2,0,1:T(8,128)S(1)}, u32[]{:S(2)}, u32[]{:S(2)}) async-start(f32[27,8,256]{2,0,1:T(8,128)} %copy.39), calls=%async_computation.1 | async-start | bytes 524288 | tf_op jit(solution)/shard_map/all_to_all | solution.py:544
  56.3 9.6 %all-to-all-done.1 = f32[27,8,256]{2,0,1:T(8,128)S(1)} async-done(((f32[27,8,256]{2,0,1:T(8,128)}), f32[27,8,256]{2,0,1:T(8,128)S(1)}, u32[]{:S(2)}, u32[]{:S(2)}) %all-to-all-start.1) | async-done | bytes 221216 | tf_op jit(solution)/shard_map/all_to_all | solution.py:544
  66.0 0.4 copy.40
  66.3 2.8 %gather_fusion = f32[1024,27]{1,0:T(8,128)S(1)} fusion(f32[27,2048]{0,1:T(8,128)S(1)} %bitcast.56, s32[1024]{0:T(1024)S(1)} %broadcast_clamp_fusion), kind=kCustom, calls=%fused_computation | custom fusion | bytes 225280 | tf_op jit(solution)/shard_map/jit(_take)/gather | solution.py:545
  69.1 0.2 copy.41
  69.4 0.0 copy-start.5
  69.4 4.5 %collective-permute-start.4 = (f32[27,1,2,256]{3,2,1,0:T(2,128)S(1)}, f32[27,1,2,256]{3,2,1,0:T(2,128)S(1)}, u32[]{:S(2)}, u32[]{:S(2)}) collective-permute-start(f32[27,1,2,256]{3,2,1,0:T(2,128)S(1)} %slice.201), channel_id=1, source_target_pairs={{0,8},{8,16},{16,24},{1,9},{9,17},{17,25},{2,10},{10,18},{18,26},{... | collective-permute-start | bytes 165896 | tf_op jit(solution)/shard_map/ppermute | solution.py:38
  73.9 1.8 %collective-permute-done.4 = f32[27,1,2,256]{3,2,1,0:T(2,128)S(1)} collective-permute-done((f32[27,1,2,256]{3,2,1,0:T(2,128)S(1)}, f32[27,1,2,256]{3,2,1,0:T(2,128)S(1)}, u32[]{:S(2)}, u32[]{:S(2)}) %collective-permute-start.4) | collective-permute-done | bytes 55328 | tf_op jit(solution)/shard_map/ppermute | solution.py:38
  75.7 0.1 pad_maximum_fusion
  75.8 1.3 collective-permute-start.5
  77.2 0.6 reshape.88.refs_0_
  77.8 0.2 collective-permute-done.5
  78.0 0.2 select_maximum_fusion
  78.2 0.9 reshape.92.refs_1_
  79.2 49.5 %conjugate_gradients.1 = (f32[3,2,2,256]{3,2,1,0:T(2,128)}, f32[3,2,2,256]{3,2,1,0:T(2,128)}) custom-call(f32[3,16,256]{2,1,0:T(8,128)} %reshape.88.refs_0_, f32[27,16,256]{2,1,0:T(8,128)} %reshape.92.refs_1_), custom_call_target="tpu_custom_call" | custom-call | tf_op jit(solution)/shard_map/conjugate_gradients/pallas_call | solution.py:476
  128.7 1.3 %copy.57 = f32[3,2,2,256]{3,2,1,0:T(2,128)} copy(f32[3,2,2,256]{3,2,1,0:T(2,128)} %get-tuple-element.33) | data formatting | bytes 24576
  130.0 0.0 copy-done.4
  130.0 0.6 copy.58
  (34 shorter events, 0.4 us)
Async XLA Ops:
  0.6 6.9 %copy-start.7 = (s32[1,1,1024]{2,1,0:T(1,128)S(1)}, s32[1,1,1024]{2,1,0:T(1,128)}, u32[]{:S(2)}) copy-start(s32[1,1,1024]{2,1,0:T(1,128)} %param.17) | copy-start | bytes 12292
  1.4 11.2 %collective-permute-start = (f32[3,1,2,256]{3,2,1,0:T(2,128)S(1)}, f32[3,1,2,256]{3,2,1,0:T(2,128)S(1)}, u32[]{:S(2)}, u32[]{:S(2)}) collective-permute-start(f32[3,1,2,256]{3,2,1,0:T(2,128)S(1)} %get-tuple-element.28), channel_id=1, source_target_pairs={{0,8},{8,16},{16,24},{1,9},{9,17},{17,25},{2,10},{10,18},{18,26},{... | collective-permute-start | bytes 18440 | tf_op jit(solution)/shard_map/ppermute | solution.py:27
  6.2 1.3 %copy-start.2 = (s32[1,1,1024,1]{2,3,1,0:T(1,128)S(1)}, s32[1,1,1024,1]{2,3,1,0:T(1,128)}, u32[]{:S(2)}) copy-start(s32[1,1,1024,1]{2,3,1,0:T(1,128)} %param.16) | copy-start | bytes 12292
  6.2 7.0 %collective-permute-start.1 = (f32[3,1,2,256]{3,2,1,0:T(2,128)S(1)}, f32[3,1,2,256]{3,2,1,0:T(2,128)S(1)}, u32[]{:S(2)}, u32[]{:S(2)}) collective-permute-start(f32[3,1,2,256]{3,2,1,0:T(2,128)S(1)} %get-tuple-element.27), channel_id=1, source_target_pairs={{8,0},{16,8},{24,16},{9,1},{17,9},{25,17},{10,2},{18,10},{26,18},{... | collective-permute-start | bytes 18440 | tf_op jit(solution)/shard_map/ppermute | solution.py:30
  10.4 0.7 copy-start.3
  11.1 1.4 %copy-start.8 = (f32[32]{0:T(128)S(1)}, f32[32]{0:T(128)}, u32[]{:S(2)}) copy-start(f32[32]{0:T(128)} %constant.32.clone) | copy-start | bytes 388
  11.2 1.4 %copy-start.9 = (f32[32]{0:T(128)S(1)}, f32[32]{0:T(128)}, u32[]{:S(2)}) copy-start(f32[32]{0:T(128)} %constant.33.clone) | copy-start | bytes 388
  11.2 1.4 %copy-start.10 = (f32[32]{0:T(128)S(1)}, f32[32]{0:T(128)}, u32[]{:S(2)}) copy-start(f32[32]{0:T(128)} %constant.34.clone) | copy-start | bytes 388
  11.2 1.4 %copy-start.11 = (f32[32]{0:T(128)S(1)}, f32[32]{0:T(128)}, u32[]{:S(2)}) copy-start(f32[32]{0:T(128)} %constant.31.clone) | copy-start | bytes 388
  12.5 0.7 copy-start.1
  13.3 3.7 %collective-permute-start.2 = (f32[3,4,1,256]{3,2,1,0:T(1,128)S(1)}, f32[3,4,1,256]{3,2,1,0:T(1,128)S(1)}, u32[]{:S(2)}, u32[]{:S(2)}) collective-permute-start(f32[3,4,1,256]{3,2,1,0:T(1,128)S(1)} %get-tuple-element.4), channel_id=1, source_target_pairs={{0,1},{1,2},{2,3},{3,4},{4,5},{5,6},{6,7},{8,9},{9,10},{10,11},{11... | collective-permute-start | bytes 36872 | tf_op jit(solution)/shard_map/ppermute | solution.py:27
  14.7 4.7 %collective-permute-start.3 = (f32[3,4,1,256]{3,2,1,0:T(1,128)S(1)}, f32[3,4,1,256]{3,2,1,0:T(1,128)S(1)}, u32[]{:S(2)}, u32[]{:S(2)}) collective-permute-start(f32[3,4,1,256]{3,2,1,0:T(1,128)S(1)} %get-tuple-element.5), channel_id=1, source_target_pairs={{1,0},{2,1},{3,2},{4,3},{5,4},{6,5},{7,6},{9,8},{10,9},{11,10},{12... | collective-permute-start | bytes 36872 | tf_op jit(solution)/shard_map/ppermute | solution.py:30
  16.0 0.7 copy-start.6
  24.6 11.8 %all-to-all-start = ((f32[8,8,256]{2,0,1:T(8,128)}), f32[8,8,256]{2,0,1:T(8,128)S(1)}, u32[]{:S(2)}, u32[]{:S(2)}) async-start(f32[8,8,256]{2,0,1:T(8,128)} %copy.36), calls=%async_computation | async-start | bytes 131072 | tf_op jit(solution)/shard_map/all_to_all | solution.py:533
  36.4 0.6 copy-start
  52.9 13.1 %all-to-all-start.1 = ((f32[27,8,256]{2,0,1:T(8,128)}), f32[27,8,256]{2,0,1:T(8,128)S(1)}, u32[]{:S(2)}, u32[]{:S(2)}) async-start(f32[27,8,256]{2,0,1:T(8,128)} %copy.39), calls=%async_computation.1 | async-start | bytes 524288 | tf_op jit(solution)/shard_map/all_to_all | solution.py:544
  69.4 7.8 %copy-start.5 = (f32[3,2,2,256]{3,2,1,0:T(2,128)S(1)}, f32[3,2,2,256]{3,2,1,0:T(2,128)}, u32[]{:S(2)}) copy-start(f32[3,2,2,256]{3,2,1,0:T(2,128)} %param.15) | copy-start | bytes 36868
  69.4 6.3 %collective-permute-start.4 = (f32[27,1,2,256]{3,2,1,0:T(2,128)S(1)}, f32[27,1,2,256]{3,2,1,0:T(2,128)S(1)}, u32[]{:S(2)}, u32[]{:S(2)}) collective-permute-start(f32[27,1,2,256]{3,2,1,0:T(2,128)S(1)} %slice.201), channel_id=1, source_target_pairs={{0,8},{8,16},{16,24},{1,9},{9,17},{17,25},{2,10},{10,18},{18,26},{... | collective-permute-start | bytes 165896 | tf_op jit(solution)/shard_map/ppermute | solution.py:38
  75.8 2.2 %collective-permute-start.5 = (f32[27,3,1,256]{3,2,1,0:T(1,128)S(1)}, f32[27,3,1,256]{3,2,1,0:T(1,128)S(1)}, u32[]{:S(2)}, u32[]{:S(2)}) collective-permute-start(f32[27,3,1,256]{3,2,1,0:T(1,128)S(1)} %pad_maximum_fusion), channel_id=1, source_target_pairs={{0,1},{1,2},{2,3},{3,4},{4,5},{5,6},{6,7},{8,9},{9,10},{10,11},{11... | collective-permute-start | bytes 248840 | tf_op jit(solution)/shard_map/ppermute | solution.py:38
  128.7 1.3 %copy-start.4 = (f32[3,2,2,256]{3,2,1,0:T(2,128)S(1)}, f32[3,2,2,256]{3,2,1,0:T(2,128)}, u32[]{:S(2)}) copy-start(f32[3,2,2,256]{3,2,1,0:T(2,128)} %get-tuple-element.34) | copy-start | bytes 36868
where the time goes:
time: 131 us
  Pallas kernels  63.6 us (49%)
  starting transfers between devices  24.1 us (18%)
  local copies, waits for them, and re-layouts  19.1 us (15%)
  waiting for transfers between devices  18 us (14%)
  other arithmetic  3.46 us (3%)
  between operations  2.4 us (2%)
    pallas_call x1, Pallas kernels, conjugate_gradients(): pl.pallas_call(body, out_shape=[jax.ShapeDtypeStruct(load.shape, jnp.floa...  49.5 us
    pallas_call x1, Pallas kernels, micro_solve(): pl.pallas_call(micro_kernel, grid=(points // tile,), out_shape=jax.ShapeD...  14.1 us
    all_to_all x1, waiting for transfers between devices, shards(): lax.all_to_all(rows, 'micro', split_axis=1, concat_axis=1, tiled=True)  9.62 us
    ppermute x2, starting transfers between devices, with_halo(): lax.ppermute(lax.slice_in_dim(block, block.shape[dim] - width, None, axis...  6.32 us
    all_to_all x1, starting transfers between devices, shards(): got = lax.all_to_all(send, 'micro', split_axis=1, concat_axis=1, tiled=True)  5.91 us
    ppermute x2, starting transfers between devices, passed_along(): lax.ppermute(value, axis, [(source, source + steps) for source in range(i...  5.84 us
    unnamed x33, local copies, waits for them, and re-layouts  5.11 us
    all_to_all x1, waiting for transfers between devices, shards(): got = lax.all_to_all(send, 'micro', split_axis=1, concat_axis=1, tiled=True)  3.89 us
  transfers between devices with their start and end apart: 8, of which 5 were waited for; matrix products, arithmetic and copies ran while one was open for 5% of the time, Pallas kernels for 0%

commit v1 on v0

--- a/solution.py
+++ b/solution.py
@@ -194,11 +194,7 @@
     elem_ref,
     inc_ref,
     res_ref,
-    residual,
-    direction,
-    along,
-    increment,
-    image,
+    basis,
     send_halo,
     halo,
     part,
@@ -242,12 +238,11 @@
             device_id=(lax.rem(a + dx + n_macro, n_macro), lax.rem(b + dy + n_micro, n_micro)),
             device_id_type=MESH,
         )
-    pl.semaphore_wait(barrier, n_micro - 1 + n_macro - 1 + len(corners))
     for at, (dx, dy) in enumerate(AROUND):
 
         @pl.when(jnp.logical_not(inside(dx, dy)))
         def _():
-            for it in range(ITERS + 1):
+            for it in range(ITERS):
                 halo[it, at] = jnp.zeros(halo.shape[2:], jnp.float32)
 
     def near(step, count):
@@ -272,7 +267,7 @@
             device_id_type=MESH,
         )
 
-    def halo_start(it, ref):
+    def halo_start(it):
         for at, (dx, dy) in enumerate(AROUND):
 
             @pl.when(inside(dx, dy))
@@ -280,10 +275,10 @@
                 mine = places(at, near)
                 for c in range(3):
                     for k, row in enumerate(mine):
-                        send_halo[it, at, pl.ds(c * len(mine) + k, 1)] = ref[c, pl.ds(row, 1)]
+                        send_halo[it, at, pl.ds(c * len(mine) + k, 1)] = basis[it, c, pl.ds(row, 1)]
                 hop(it, at).start()
 
-    def halo_finish(it, ref):
+    def halo_finish(it):
         for at, (dx, dy) in enumerate(AROUND):
 
             @pl.when(inside(dx, dy))
@@ -302,7 +297,7 @@
             theirs = places(at, far)
             for c in range(3):
                 for k, row in enumerate(theirs):
-                    ref[c, pl.ds(row, 1)] = halo[it, at, pl.ds(c * len(theirs) + k, 1)]
+                    basis[it, c, pl.ds(row, 1)] = halo[it, at, pl.ds(c * len(theirs) + k, 1)]
 
     row_at = lax.broadcasted_iota(jnp.int32, (rows, lanes), 0)
     lane_at = lax.broadcasted_iota(jnp.int32, (rows, lanes), 1)
@@ -322,10 +317,10 @@
             return jnp.where(lane_at == 0, 0.0, pltpu.roll(value, 1, 1))
         return pltpu.roll(value, wide if axis == 0 else 1, 0)
 
-    def strain_of(ref):
+    def strain_of(it):
         grads = []
         for c in range(3):
-            value = ref[c]
+            value = basis[it, c]
             moved = up(value, 2)
             total, gap = value + moved, moved - value
             total_up, gap_up = up(total, 1), up(gap, 1)
@@ -355,14 +350,36 @@
         rest = down(second, 1) - second + third + down(third, 1)
         return 0.25 * (down(first, 0) - first + rest + down(rest, 0))
 
-    stress = [elem_ref[i] for i in range(6)]
-    for c in range(3):
-        residual[c] = jnp.where(own, load_ref[c] - force_of(stress, c), 0.0)
-        direction[c] = jnp.zeros((rows, lanes), jnp.float32)
-        along[c] = jnp.zeros((rows, lanes), jnp.float32)
-        increment[c] = jnp.zeros((rows, lanes), jnp.float32)
-    halo_start(ITERS, residual)
-    halo_finish(ITERS, residual)
+    def applied(it):
+        strain = strain_of(it)
+        stress = []
+        for i in range(6):
+            value = None
+            for j in range(6):
+                term = elem_ref[6 + PAIR_AT[(min(i, j), max(i, j))]] * strain[j]
+                value = term if value is None else value + term
+            stress.append(value)
+        return [
+            jnp.where(own, MASS * basis[it, c] + force_of(stress, c), 0.0) for c in range(3)
+        ]
+
+    def product(first, second):
+        total = None
+        for c in range(3):
+            term = first[c] * second[c]
+            total = term if total is None else total + term
+        total = jnp.sum(jnp.where(own, total, 0.0), axis=0, keepdims=True)
+        value = total[:, :128]
+        for at in range(128, lanes, 128):
+            value = value + total[:, at : at + 128]
+        return value
+
+    def stacked(pieces):
+        tile_row = lax.broadcasted_iota(jnp.int32, (part.shape[1], 128), 0)
+        value = jnp.zeros((part.shape[1], 128), jnp.float32)
+        for at, piece in enumerate(pieces):
+            value = jnp.where(tile_row == at, piece, value)
+        return value
 
     def gather_start(it, src, dst, count, me, send, recv, device):
         copies = []
@@ -388,69 +405,125 @@
             total = total + dst[it, at]
         return total
 
-    def step_body(it, carry):
-        norm_old, alpha_old = carry
-        strain = strain_of(residual)
-        stress = []
-        for i in range(6):
-            value = None
-            for j in range(6):
-                term = elem_ref[6 + PAIR_AT[(min(i, j), max(i, j))]] * strain[j]
-                value = term if value is None else value + term
-            stress.append(value)
-        norm = jnp.zeros((rows, lanes), jnp.float32)
-        cross = jnp.zeros((rows, lanes), jnp.float32)
-        for c in range(3):
-            here = residual[c]
-            new = jnp.where(own, MASS * here + force_of(stress, c), 0.0)
-            image[c] = new
-            kept = jnp.where(own, here, 0.0)
-            norm = norm + kept * kept
-            cross = cross + kept * new
-
-        def folded(value):
-            value = jnp.sum(value, axis=0, keepdims=True)
-            total = value[:, :128]
-            for at in range(128, lanes, 128):
-                total = total + value[:, at : at + 128]
-            return total
-
-        tile_row = lax.broadcasted_iota(jnp.int32, (8, 128), 0)
-        part[it] = jnp.where(
-            tile_row == 0, folded(norm), jnp.where(tile_row == 1, folded(cross), 0.0)
-        )
-        copies = gather_start(
+    def micro_start(it):
+        return gather_start(
             it, part, got_micro, n_micro, b, micro_send, micro_recv, lambda other: (a, other)
         )
-        halo_start(it, image)
-        middle[it] = gather_finish(it, copies, got_micro, n_micro)
-        copies = gather_start(
+
+    def macro_start(it):
+        return gather_start(
             it, middle, got_macro, n_macro, a, macro_send, macro_recv, lambda other: (other, b)
         )
-        halo_finish(it, image)
-        totals = jnp.sum(gather_finish(it, copies, got_macro, n_macro), axis=1, keepdims=True)
-        norm_now, product = totals[0:1], totals[1:2]
-        first = jnp.full((1, 1), it, jnp.int32) == 0
-        ratio = jnp.where(first, 0.0, norm_now / norm_old)
-        alpha = norm_now / (product - ratio * norm_now / alpha_old)
-        for c in range(3):
-            here = residual[c]
-            toward = here + ratio * direction[c]
-            drop = image[c] + ratio * along[c]
-            direction[c] = toward
-            along[c] = drop
-            increment[c] = increment[c] + alpha * toward
-            residual[c] = here - alpha * drop
-        return norm_now, alpha
-
-    lax.fori_loop(
-        0, ITERS, step_body, (jnp.ones((1, 1), jnp.float32), jnp.ones((1, 1), jnp.float32))
-    )
+
+    stress = [elem_ref[i] for i in range(6)]
     for c in range(3):
+        basis[0, c] = jnp.where(own, load_ref[c] - force_of(stress, c), 0.0)
+    pl.semaphore_wait(barrier, n_micro - 1 + n_macro - 1 + len(corners))
+    halo_start(0)
+    halo_finish(0)
+    first = applied(0)
+    for c in range(3):
+        basis[1, c] = first[c]
+    halo_start(1)
+    part[0] = stacked([product([basis[0, c] for c in range(3)], [basis[0, c] for c in range(3)]),
+                       product(first, first)])
+    copies = micro_start(0)
+    halo_finish(1)
+    second = applied(1)
+    for c in range(3):
+        basis[2, c] = second[c]
+    halo_start(2)
+    middle[0] = gather_finish(0, copies, got_micro, n_micro)
+    copies = macro_start(0)
+    halo_finish(2)
+    totals = jnp.sum(gather_finish(0, copies, got_macro, n_macro), axis=1, keepdims=True)
+    shift = jnp.sqrt(totals[1:2] / totals[0:1])
+    scale = 1.0 / shift
+    for c in range(3):
+        u0, w1, w2 = basis[0, c], basis[1, c] * scale, basis[2, c] * (scale * scale)
+        basis[1, c] = w1 - u0
+        basis[2, c] = (w2 - w1) - (w1 - u0)
+
+    def field(it):
+        return [basis[it, c] for c in range(3)]
+
+    def step(it):
+        grown = applied(it)
+        return [grown[c] * scale - jnp.where(own, basis[it, c], 0.0) for c in range(3)]
+
+    moments = []
+    for it in range(2, ITERS):
+        grown = step(it)
+        if it + 1 < ITERS:
+            for c in range(3):
+                basis[it + 1, c] = grown[c]
+            halo_start(it + 1)
+            if it == 2:
+                for k in range(3):
+                    moments.append(product(field(k), field(k)))
+                    moments.append(product(field(k), field(k + 1)))
+            else:
+                moments.append(product(field(it), field(it)))
+                moments.append(product(field(it), field(it + 1)))
+            halo_finish(it + 1)
+    moments.append(product(field(ITERS - 1), field(ITERS - 1)))
+    moments.append(product(field(ITERS - 1), grown))
+    part[1] = stacked(moments)
+    copies = micro_start(1)
+    middle[1] = gather_finish(1, copies, got_micro, n_micro)
+    copies = macro_start(1)
+    totals = jnp.sum(gather_finish(1, copies, got_macro, n_macro), axis=1, keepdims=True)
+    held = [totals[k : k + 1] for k in range(2 * ITERS)]
+
+    def inner(first, second, extra=0):
+        gathered = {}
+        for i, x in enumerate(first):
+            for j, y in enumerate(second):
+                gathered.setdefault(i + j, []).append(x * y)
+        value = None
+        for degree, terms in gathered.items():
+            total = terms[0]
+            for term in terms[1:]:
+                total = total + term
+            total = total * held[degree + extra]
+            value = total if value is None else value + total
+        return value
+
+    one = jnp.ones((1, 1), jnp.float32)
+    left, toward, done = [one], [one], []
+    norm = held[0]
+    for it in range(ITERS):
+        energy = inner(toward, toward) + inner(toward, toward, 1)
+        size = norm / energy
+        done = [x + size * scale * p for x, p in zip(done + [0.0], toward)]
+        raised = [
+            (toward[k] if k < len(toward) else 0.0) + (toward[k - 1] if k > 0 else 0.0)
+            for k in range(len(toward) + 1)
+        ]
+        left = [
+            (left[k] if k < len(left) else 0.0) - size * raised[k] for k in range(len(raised))
+        ]
+        if it + 1 < ITERS:
+            fresh = inner(left, left)
+            ratio = fresh / norm
+            toward = [
+                left[k] + (ratio * toward[k] if k < len(toward) else 0.0)
+                for k in range(len(left))
+            ]
+            norm = fresh
+    for c in range(3):
+        fields = [basis[k, c] for k in range(ITERS)] + [grown[c]]
+        moved, rest = None, None
+        for k in range(ITERS + 1):
+            if k < len(done):
+                term = done[k] * fields[k]
+                moved = term if moved is None else moved + term
+            term = left[k] * fields[k]
+            rest = term if rest is None else rest + term
         for i in range(count_x):
             low = (i + 1) * wide + 1
-            inc_ref[c, i] = increment[c, pl.ds(low, count_y)]
-            res_ref[c, i] = residual[c, pl.ds(low, count_y)]
+            inc_ref[c, i] = moved[low : low + count_y]
+            res_ref[c, i] = rest[low : low + count_y]
 
 
 def conjugate_gradients(load, elements):
@@ -465,8 +538,7 @@
         return jnp.pad(value, ((0, 0), (0, rows - flat), (0, 0)))
 
     side = -(-3 * max(count_x, count_y) // 8) * 8
-    node = pltpu.VMEM((3, rows, count_z), jnp.float32)
-    around = pltpu.VMEM((ITERS + 1, len(AROUND), side, count_z), jnp.float32)
+    around = pltpu.VMEM((ITERS, len(AROUND), side, count_z), jnp.float32)
     dma = pltpu.SemaphoreType.DMA
 
     def body(*refs):
@@ -478,20 +550,20 @@
         out_shape=[jax.ShapeDtypeStruct(load.shape, jnp.float32)] * 2,
         in_specs=[vmem, vmem],
         out_specs=[vmem, vmem],
-        scratch_shapes=[node] * 5
-        + [
+        scratch_shapes=[
+            pltpu.VMEM((ITERS, 3, rows, count_z), jnp.float32),
             around,
             around,
-            pltpu.VMEM((ITERS, 8, 128), jnp.float32),
-            pltpu.VMEM((ITERS, n_micro, 8, 128), jnp.float32),
-            pltpu.VMEM((ITERS, 8, 128), jnp.float32),
-            pltpu.VMEM((ITERS, n_macro, 8, 128), jnp.float32),
-            dma((ITERS + 1, len(AROUND))),
-            dma((ITERS + 1, len(AROUND))),
-            dma((ITERS, n_micro - 1)),
-            dma((ITERS, n_micro - 1)),
-            dma((ITERS, n_macro - 1)),
-            dma((ITERS, n_macro - 1)),
+            pltpu.VMEM((2, 16, 128), jnp.float32),
+            pltpu.VMEM((2, n_micro, 16, 128), jnp.float32),
+            pltpu.VMEM((2, 16, 128), jnp.float32),
+            pltpu.VMEM((2, n_macro, 16, 128), jnp.float32),
+            dma((ITERS, len(AROUND))),
+            dma((ITERS, len(AROUND))),
+            dma((2, n_micro - 1)),
+            dma((2, n_micro - 1)),
+            dma((2, n_macro - 1)),
+            dma((2, n_macro - 1)),
         ],
         compiler_params=pltpu.CompilerParams(collective_id=0, has_side_effects=True),
         name="conjugate_gradients",

time: 131 us -> 118 us (0.901)
  Pallas kernels: 63.6 us -> 49.7 us
    pallas_call x1, Pallas kernels: 49.5 us -> 35.7 us  [conjugate_gradients(): pl.pallas_call(body, out_shape=[jax.ShapeDtypeStruct(load.shape, jnp.floa...]
  transfers between devices with their start and end apart: 8 -> 8, of which waited for: 5 -> 5; matrix products, arithmetic and copies ran while one was open for 5% -> 6% of each run, Pallas kernels for 0% -> 0%
where the time goes in v1:
time: 118 us; the launch traced here: 117 us
  Pallas kernels  49.7 us (42%)
  starting transfers between devices  24.1 us (20%)
  local copies, waits for them, and re-layouts  19.1 us (16%)
  waiting for transfers between devices  18 us (15%)
  other arithmetic  3.46 us (3%)
  between operations  2.4 us (2%)
    pallas_call x1, Pallas kernels, conjugate_gradients(): pl.pallas_call(body, out_shape=[jax.ShapeDtypeStruct(load.shape, jnp.floa...  35.7 us
    pallas_call x1, Pallas kernels, micro_solve(): pl.pallas_call(micro_kernel, grid=(points // tile,), out_shape=jax.ShapeD...  14.1 us
    all_to_all x1, waiting for transfers between devices, shards(): lax.all_to_all(rows, 'micro', split_axis=1, concat_axis=1, tiled=True)  9.62 us
    ppermute x2, starting transfers between devices, with_halo(): lax.ppermute(lax.slice_in_dim(block, block.shape[dim] - width, None, axis...  6.32 us
    all_to_all x1, starting transfers between devices, shards(): got = lax.all_to_all(send, 'micro', split_axis=1, concat_axis=1, tiled=True)  5.91 us
    ppermute x2, starting transfers between devices, passed_along(): lax.ppermute(value, axis, [(source, source + steps) for source in range(i...  5.84 us
    unnamed x33, local copies, waits for them, and re-layouts  5.11 us
    all_to_all x1, waiting for transfers between devices, shards(): got = lax.all_to_all(send, 'micro', split_axis=1, concat_axis=1, tiled=True)  3.89 us
  transfers between devices with their start and end apart: 8, of which 5 were waited for; matrix products, arithmetic and copies ran while one was open for 6% of the time, Pallas kernels for 0%

profile of v1, /device:TPU:0, one launch (start us, length us, event | category | flops | bytes accessed | tf_op | source)
XLA Modules:
  0.0 116.7 jit_solution(14439154700056032355)
XLA Ops:
  0.6 0.0 copy-start.7
  0.6 0.7 fusion.16
  1.4 4.9 %collective-permute-start = (f32[3,1,2,256]{3,2,1,0:T(2,128)S(1)}, f32[3,1,2,256]{3,2,1,0:T(2,128)S(1)}, u32[]{:S(2)}, u32[]{:S(2)}) collective-permute-start(f32[3,1,2,256]{3,2,1,0:T(2,128)S(1)} %get-tuple-element.28), channel_id=1, source_target_pairs={{0,8},{8,16},{16,24},{1,9},{9,17},{17,25},{2,10},{10,18},{18,26},{... | collective-permute-start | bytes 18440 | tf_op jit(solution)/shard_map/ppermute | solution.py:27
  6.2 0.0 copy-start.2
  6.2 1.3 %collective-permute-start.1 = (f32[3,1,2,256]{3,2,1,0:T(2,128)S(1)}, f32[3,1,2,256]{3,2,1,0:T(2,128)S(1)}, u32[]{:S(2)}, u32[]{:S(2)}) collective-permute-start(f32[3,1,2,256]{3,2,1,0:T(2,128)S(1)} %get-tuple-element.27), channel_id=1, source_target_pairs={{8,0},{16,8},{24,16},{9,1},{17,9},{25,17},{10,2},{18,10},{26,18},{... | collective-permute-start | bytes 18440 | tf_op jit(solution)/shard_map/ppermute | solution.py:30
  7.5 0.0 copy-done.7
  7.6 0.0 copy-done.2
  7.6 2.3 %reduce-window.6 = s32[8,8,128]{2,1,0:T(8,128)S(1)} reduce-window(s32[8,8,128]{2,1,0:T(8,128)S(1)} %fusion.14, s32[]{:T(128)} %constant.11.clone.1), window={size=1x1x128 pad=0_0x0_0x127_0}, to_apply=%region_0.1 | reduce-window | flops 1040384 | bytes 65540 | tf_op jit(solution)/shard_map/reduce-window
  9.9 0.3 slice_reduce_fusion
  10.1 0.2 reduce-window.9
  10.3 0.1 add_bitcast_fusion
  10.4 0.0 copy-start.3
  10.4 0.7 copy-done.3
  11.1 0.0 copy-start.8
  11.2 0.0 copy-start.9
  11.2 0.0 copy-start.10
  11.2 0.0 copy-start.11
  12.5 0.0 copy-start.1
  12.5 0.0 copy-done.8
  12.5 0.0 copy-done.9
  12.6 0.0 collective-permute-done
  12.6 0.6 copy-done.1
  13.2 0.0 collective-permute-done.1
  13.3 1.5 %collective-permute-start.2 = (f32[3,4,1,256]{3,2,1,0:T(1,128)S(1)}, f32[3,4,1,256]{3,2,1,0:T(1,128)S(1)}, u32[]{:S(2)}, u32[]{:S(2)}) collective-permute-start(f32[3,4,1,256]{3,2,1,0:T(1,128)S(1)} %get-tuple-element.4), channel_id=1, source_target_pairs={{0,1},{1,2},{2,3},{3,4},{4,5},{5,6},{6,7},{8,9},{9,10},{10,11},{11... | collective-permute-start | bytes 36872 | tf_op jit(solution)/shard_map/ppermute | solution.py:27
  14.7 1.3 %collective-permute-start.3 = (f32[3,4,1,256]{3,2,1,0:T(1,128)S(1)}, f32[3,4,1,256]{3,2,1,0:T(1,128)S(1)}, u32[]{:S(2)}, u32[]{:S(2)}) collective-permute-start(f32[3,4,1,256]{3,2,1,0:T(1,128)S(1)} %get-tuple-element.5), channel_id=1, source_target_pairs={{1,0},{2,1},{3,2},{4,3},{5,4},{6,5},{7,6},{9,8},{10,9},{11,10},{12... | collective-permute-start | bytes 36872 | tf_op jit(solution)/shard_map/ppermute | solution.py:30
  16.0 0.0 copy-start.6
  16.1 0.7 copy.38.coef_ref
  16.7 0.2 copy.37
  16.9 0.0 collective-permute-done.2
  16.9 2.5 %collective-permute-done.3 = f32[3,4,1,256]{3,2,1,0:T(1,128)S(1)} collective-permute-done((f32[3,4,1,256]{3,2,1,0:T(1,128)S(1)}, f32[3,4,1,256]{3,2,1,0:T(1,128)S(1)}, u32[]{:S(2)}, u32[]{:S(2)}) %collective-permute-start.3) | collective-permute-done | bytes 12320 | tf_op jit(solution)/shard_map/ppermute | solution.py:30
  19.5 0.1 add_add_fusion.2
  19.6 0.1 add_add_fusion.1
  19.8 0.1 add_add_fusion
  20.1 0.2 copy.35
  20.3 3.3 %scatter_custom_fusion = f32[8,2048]{0,1:T(8,128)S(1)} fusion(s32[1024]{0:T(1024)S(1)} %bitcast.71, f32[1024,8]{1,0:T(8,128)S(1)} %copy.35, f32[]{:T(128)} %constant.12.clone.1), kind=kCustom, calls=%fused_computation.2 | custom fusion | bytes 65540 | tf_op jit(solution)/shard_map/scatter | solution.py:602
  23.6 0.9 copy.36
  24.6 5.9 %all-to-all-start = ((f32[8,8,256]{2,0,1:T(8,128)}), f32[8,8,256]{2,0,1:T(8,128)S(1)}, u32[]{:S(2)}, u32[]{:S(2)}) async-start(f32[8,8,256]{2,0,1:T(8,128)} %copy.36), calls=%async_computation | async-start | bytes 131072 | tf_op jit(solution)/shard_map/all_to_all | solution.py:605
  30.5 0.1 stack.14
  30.6 0.6 pad.33.product_ref
  31.2 0.7 pad.31.force_ref
  31.9 0.6 pad.32.couple_ref
  32.5 3.9 %all-to-all-done = f32[8,8,256]{2,0,1:T(8,128)S(1)} async-done(((f32[8,8,256]{2,0,1:T(8,128)}), f32[8,8,256]{2,0,1:T(8,128)S(1)}, u32[]{:S(2)}, u32[]{:S(2)}) %all-to-all-start) | async-done | bytes 65568 | tf_op jit(solution)/shard_map/all_to_all | solution.py:605
  36.4 0.6 copy-done
  37.0 14.1 %micro_solve.1 = f32[27,2048]{1,0:T(8,128)} custom-call(f32[8,2048]{1,0:T(8,128)} %bitcast.64, bf16[512,512]{1,0:T(8,128)(2,1)} %bitcast.61, bf16[512,512]{1,0:T(8,128)(2,1)} %bitcast.62, bf16[512,8]{1,0:T(8,128)(2,1)} %pad.31.force_ref, bf16[32,512]{1,0:T(8,128)(2,1)} %pad.32.couple_ref, bf16[32,512]{1,0:T(8,128)(2,1)} %pad.33.product_ref, ...), custom_call_target="tpu_custom_call" | custom-call | tf_op jit(solution)/shard_map/micro_solve/pallas_call | solution.py:169
  51.1 1.0 copy.44
  52.1 0.8 copy.39
  52.9 3.4 %all-to-all-start.1 = ((f32[27,8,256]{2,0,1:T(8,128)}), f32[27,8,256]{2,0,1:T(8,128)S(1)}, u32[]{:S(2)}, u32[]{:S(2)}) async-start(f32[27,8,256]{2,0,1:T(8,128)} %copy.39), calls=%async_computation.1 | async-start | bytes 524288 | tf_op jit(solution)/shard_map/all_to_all | solution.py:616
  56.3 9.6 %all-to-all-done.1 = f32[27,8,256]{2,0,1:T(8,128)S(1)} async-done(((f32[27,8,256]{2,0,1:T(8,128)}), f32[27,8,256]{2,0,1:T(8,128)S(1)}, u32[]{:S(2)}, u32[]{:S(2)}) %all-to-all-start.1) | async-done | bytes 221216 | tf_op jit(solution)/shard_map/all_to_all | solution.py:616
  66.0 0.4 copy.40
  66.3 2.8 %gather_fusion = f32[1024,27]{1,0:T(8,128)S(1)} fusion(f32[27,2048]{0,1:T(8,128)S(1)} %bitcast.56, s32[1024]{0:T(1024)S(1)} %broadcast_clamp_fusion), kind=kCustom, calls=%fused_computation | custom fusion | bytes 225280 | tf_op jit(solution)/shard_map/jit(_take)/gather | solution.py:617
  69.1 0.2 copy.41
  69.4 0.0 copy-start.5
  69.4 4.5 %collective-permute-start.4 = (f32[27,1,2,256]{3,2,1,0:T(2,128)S(1)}, f32[27,1,2,256]{3,2,1,0:T(2,128)S(1)}, u32[]{:S(2)}, u32[]{:S(2)}) collective-permute-start(f32[27,1,2,256]{3,2,1,0:T(2,128)S(1)} %slice.201), channel_id=1, source_target_pairs={{0,8},{8,16},{16,24},{1,9},{9,17},{17,25},{2,10},{10,18},{18,26},{... | collective-permute-start | bytes 165896 | tf_op jit(solution)/shard_map/ppermute | solution.py:38
  73.9 1.8 %collective-permute-done.4 = f32[27,1,2,256]{3,2,1,0:T(2,128)S(1)} collective-permute-done((f32[27,1,2,256]{3,2,1,0:T(2,128)S(1)}, f32[27,1,2,256]{3,2,1,0:T(2,128)S(1)}, u32[]{:S(2)}, u32[]{:S(2)}) %collective-permute-start.4) | collective-permute-done | bytes 55328 | tf_op jit(solution)/shard_map/ppermute | solution.py:38
  75.7 0.1 pad_maximum_fusion
  75.8 1.3 %collective-permute-start.5 = (f32[27,3,1,256]{3,2,1,0:T(1,128)S(1)}, f32[27,3,1,256]{3,2,1,0:T(1,128)S(1)}, u32[]{:S(2)}, u32[]{:S(2)}) collective-permute-start(f32[27,3,1,256]{3,2,1,0:T(1,128)S(1)} %pad_maximum_fusion), channel_id=1, source_target_pairs={{0,1},{1,2},{2,3},{3,4},{4,5},{5,6},{6,7},{8,9},{9,10},{10,11},{11... | collective-permute-start | bytes 248840 | tf_op jit(solution)/shard_map/ppermute | solution.py:38
  77.1 0.0 copy-done.5
  77.2 0.6 reshape.88.refs_0_
  77.8 0.2 collective-permute-done.5
  78.0 0.2 select_maximum_fusion
  78.2 0.9 reshape.92.refs_1_
  79.2 35.7 %conjugate_gradients.1 = (f32[3,2,2,256]{3,2,1,0:T(2,128)}, f32[3,2,2,256]{3,2,1,0:T(2,128)}) custom-call(f32[3,16,256]{2,1,0:T(8,128)} %reshape.88.refs_0_, f32[27,16,256]{2,1,0:T(8,128)} %reshape.92.refs_1_), custom_call_target="tpu_custom_call" | custom-call | tf_op jit(solution)/shard_map/conjugate_gradients/pallas_call | solution.py:548
  114.8 1.3 %copy.57 = f32[3,2,2,256]{3,2,1,0:T(2,128)} copy(f32[3,2,2,256]{3,2,1,0:T(2,128)} %get-tuple-element.33) | data formatting | bytes 24576
  116.1 0.6 copy.58
  (34 shorter events, 0.4 us)
Async XLA Ops:
  0.6 6.9 %copy-start.7 = (s32[1,1,1024]{2,1,0:T(1,128)S(1)}, s32[1,1,1024]{2,1,0:T(1,128)}, u32[]{:S(2)}) copy-start(s32[1,1,1024]{2,1,0:T(1,128)} %param.17) | copy-start | bytes 12292
  1.4 11.2 %collective-permute-start = (f32[3,1,2,256]{3,2,1,0:T(2,128)S(1)}, f32[3,1,2,256]{3,2,1,0:T(2,128)S(1)}, u32[]{:S(2)}, u32[]{:S(2)}) collective-permute-start(f32[3,1,2,256]{3,2,1,0:T(2,128)S(1)} %get-tuple-element.28), channel_id=1, source_target_pairs={{0,8},{8,16},{16,24},{1,9},{9,17},{17,25},{2,10},{10,18},{18,26},{... | collective-permute-start | bytes 18440 | tf_op jit(solution)/shard_map/ppermute | solution.py:27
  6.2 1.3 %copy-start.2 = (s32[1,1,1024,1]{2,3,1,0:T(1,128)S(1)}, s32[1,1,1024,1]{2,3,1,0:T(1,128)}, u32[]{:S(2)}) copy-start(s32[1,1,1024,1]{2,3,1,0:T(1,128)} %param.16) | copy-start | bytes 12292
  6.2 7.0 %collective-permute-start.1 = (f32[3,1,2,256]{3,2,1,0:T(2,128)S(1)}, f32[3,1,2,256]{3,2,1,0:T(2,128)S(1)}, u32[]{:S(2)}, u32[]{:S(2)}) collective-permute-start(f32[3,1,2,256]{3,2,1,0:T(2,128)S(1)} %get-tuple-element.27), channel_id=1, source_target_pairs={{8,0},{16,8},{24,16},{9,1},{17,9},{25,17},{10,2},{18,10},{26,18},{... | collective-permute-start | bytes 18440 | tf_op jit(solution)/shard_map/ppermute | solution.py:30
  10.4 0.7 copy-start.3
  11.1 1.4 %copy-start.8 = (f32[32]{0:T(128)S(1)}, f32[32]{0:T(128)}, u32[]{:S(2)}) copy-start(f32[32]{0:T(128)} %constant.32.clone) | copy-start | bytes 388
  11.2 1.4 %copy-start.9 = (f32[32]{0:T(128)S(1)}, f32[32]{0:T(128)}, u32[]{:S(2)}) copy-start(f32[32]{0:T(128)} %constant.33.clone) | copy-start | bytes 388
  11.2 1.4 %copy-start.10 = (f32[32]{0:T(128)S(1)}, f32[32]{0:T(128)}, u32[]{:S(2)}) copy-start(f32[32]{0:T(128)} %constant.34.clone) | copy-start | bytes 388
  11.2 1.4 %copy-start.11 = (f32[32]{0:T(128)S(1)}, f32[32]{0:T(128)}, u32[]{:S(2)}) copy-start(f32[32]{0:T(128)} %constant.31.clone) | copy-start | bytes 388
  12.5 0.7 copy-start.1
  13.3 3.7 %collective-permute-start.2 = (f32[3,4,1,256]{3,2,1,0:T(1,128)S(1)}, f32[3,4,1,256]{3,2,1,0:T(1,128)S(1)}, u32[]{:S(2)}, u32[]{:S(2)}) collective-permute-start(f32[3,4,1,256]{3,2,1,0:T(1,128)S(1)} %get-tuple-element.4), channel_id=1, source_target_pairs={{0,1},{1,2},{2,3},{3,4},{4,5},{5,6},{6,7},{8,9},{9,10},{10,11},{11... | collective-permute-start | bytes 36872 | tf_op jit(solution)/shard_map/ppermute | solution.py:27
  14.7 4.7 %collective-permute-start.3 = (f32[3,4,1,256]{3,2,1,0:T(1,128)S(1)}, f32[3,4,1,256]{3,2,1,0:T(1,128)S(1)}, u32[]{:S(2)}, u32[]{:S(2)}) collective-permute-start(f32[3,4,1,256]{3,2,1,0:T(1,128)S(1)} %get-tuple-element.5), channel_id=1, source_target_pairs={{1,0},{2,1},{3,2},{4,3},{5,4},{6,5},{7,6},{9,8},{10,9},{11,10},{12... | collective-permute-start | bytes 36872 | tf_op jit(solution)/shard_map/ppermute | solution.py:30
  16.0 0.7 copy-start.6
  24.6 11.8 %all-to-all-start = ((f32[8,8,256]{2,0,1:T(8,128)}), f32[8,8,256]{2,0,1:T(8,128)S(1)}, u32[]{:S(2)}, u32[]{:S(2)}) async-start(f32[8,8,256]{2,0,1:T(8,128)} %copy.36), calls=%async_computation | async-start | bytes 131072 | tf_op jit(solution)/shard_map/all_to_all | solution.py:605
  36.4 0.6 copy-start
  52.9 13.1 %all-to-all-start.1 = ((f32[27,8,256]{2,0,1:T(8,128)}), f32[27,8,256]{2,0,1:T(8,128)S(1)}, u32[]{:S(2)}, u32[]{:S(2)}) async-start(f32[27,8,256]{2,0,1:T(8,128)} %copy.39), calls=%async_computation.1 | async-start | bytes 524288 | tf_op jit(solution)/shard_map/all_to_all | solution.py:616
  69.4 7.8 %copy-start.5 = (f32[3,2,2,256]{3,2,1,0:T(2,128)S(1)}, f32[3,2,2,256]{3,2,1,0:T(2,128)}, u32[]{:S(2)}) copy-start(f32[3,2,2,256]{3,2,1,0:T(2,128)} %param.15) | copy-start | bytes 36868
  69.4 6.3 %collective-permute-start.4 = (f32[27,1,2,256]{3,2,1,0:T(2,128)S(1)}, f32[27,1,2,256]{3,2,1,0:T(2,128)S(1)}, u32[]{:S(2)}, u32[]{:S(2)}) collective-permute-start(f32[27,1,2,256]{3,2,1,0:T(2,128)S(1)} %slice.201), channel_id=1, source_target_pairs={{0,8},{8,16},{16,24},{1,9},{9,17},{17,25},{2,10},{10,18},{18,26},{... | collective-permute-start | bytes 165896 | tf_op jit(solution)/shard_map/ppermute | solution.py:38
  75.8 2.2 %collective-permute-start.5 = (f32[27,3,1,256]{3,2,1,0:T(1,128)S(1)}, f32[27,3,1,256]{3,2,1,0:T(1,128)S(1)}, u32[]{:S(2)}, u32[]{:S(2)}) collective-permute-start(f32[27,3,1,256]{3,2,1,0:T(1,128)S(1)} %pad_maximum_fusion), channel_id=1, source_target_pairs={{0,1},{1,2},{2,3},{3,4},{4,5},{5,6},{6,7},{8,9},{9,10},{10,11},{11... | collective-permute-start | bytes 248840 | tf_op jit(solution)/shard_map/ppermute | solution.py:38
  114.8 1.3 %copy-start.4 = (f32[3,2,2,256]{3,2,1,0:T(2,128)S(1)}, f32[3,2,2,256]{3,2,1,0:T(2,128)}, u32[]{:S(2)}) copy-start(f32[3,2,2,256]{3,2,1,0:T(2,128)} %get-tuple-element.34) | copy-start | bytes 36868

commit v2 on v1

v2 whole, which is shorter than its diff:
```python
import jax
import jax.numpy as jnp
from jax import lax
from jax.experimental import pallas as pl
from jax.experimental.pallas import tpu as pltpu
from jax.sharding import PartitionSpec as P

ITMAX = 4
ITERS = 5


BETA = 0.1
OMEGA = 0.8
MASS = 0.1
VOIGT = ((0, 5, 4), (5, 1, 3), (4, 3, 2))
PAIRS = tuple((first, second) for first in range(6) for second in range(first, 6))
PAIR_AT = {pair: at for at, pair in enumerate(PAIRS)}
AROUND = tuple((dx, dy) for dx in (-1, 0, 1) for dy in (-1, 0, 1) if (dx, dy) != (0, 0))
MESH = pl.DeviceIdType.MESH


def place_of(at, count):
    turned = jnp.where(at < 2, at, count + 1 - at)
    return lax.rem(jnp.where(turned % 2 == 1, (turned + 1) // 2, count - turned // 2), count)


def newton_kernel(
    sizes,
    disp_ref,
    load_ref,
    routes_ref,
    counts_ref,
    stiff_hbm,
    pre_hbm,
    force_ref,
    couple_ref,
    first_ref,
    shear_ref,
    inc_ref,
    res_ref,
    stiff,
    pre,
    force_t,
    couple,
    products,
    wide_products,
    spots,
    near_disp,
    bundle,
    route_out,
    route_in,
    back_out,
    back_in,
    values,
    beside,
    elem,
    basis,
    send_halo,
    halo,
    part,
    got_micro,
    middle,
    got_macro,
    last_part,
    last_all,
    weight_sem,
    disp_send,
    disp_recv,
    route_send,
    route_recv,
    back_send,
    back_recv,
    side_send,
    side_recv,
    send_sem,
    recv_sem,
    micro_send,
    micro_recv,
    macro_send,
    macro_recv,
    last_send,
    last_recv,
):
    count_x, count_y, lanes, n_macro, n_micro = sizes
    wide = count_y + 2
    rows = basis.shape[2]
    slots = spots.shape[1]
    points = spots.shape[2]
    groups = points // 128
    size = stiff.shape[0]
    tall = couple.shape[0]
    total = n_macro * n_micro
    a, b = lax.axis_index("macro"), lax.axis_index("micro")
    me = a * n_micro + b

    def device(other):
        return (other // n_micro, lax.rem(other, n_micro))

    def inside(dx, dy):
        test = None
        for place, step, count in ((a, dx, n_macro), (b, dy, n_micro)):
            if step != 0:
                good = (place > 0) if step < 0 else (place < count - 1)
                test = good if test is None else jnp.logical_and(test, good)
        return test

    barrier = pltpu.get_barrier_semaphore()

    def greet(step, carry):
        pl.semaphore_signal(
            barrier, inc=1, device_id=device(lax.rem(me + step, total)), device_id_type=MESH
        )
        return carry

    lax.fori_loop(1, total, greet, 0)
    weights = [
        pltpu.make_async_copy(stiff_hbm, stiff, weight_sem.at[0]),
        pltpu.make_async_copy(pre_hbm, pre, weight_sem.at[1]),
    ]
    for copy in weights:
        copy.start()

    force = force_ref[...].astype(jnp.float32)
    force = jnp.concatenate([force, jnp.zeros((2, size), jnp.float32)], axis=0)
    force_t[...] = force.T.astype(jnp.bfloat16)
    wide_products[...] = jnp.zeros((tall, size), jnp.float32)
    coupling = couple_ref[...].astype(jnp.float32)
    wide_products[pl.ds(0, 6)] = coupling
    couple[...] = wide_products[...].astype(jnp.bfloat16)
    wide_products[pl.ds(0, 6)] = jnp.zeros((6, size), jnp.float32)
    for at, (first, second) in enumerate(PAIRS):
        wide_products[pl.ds(6 + at, 1)] = coupling[first : first + 1] * coupling[second : second + 1]
    products[...] = wide_products[...].astype(jnp.bfloat16)

    route = routes_ref[...]
    row_of = lax.broadcasted_iota(jnp.int32, (128, 128), 0)
    column_of = lax.broadcasted_iota(jnp.int32, (128, 128), 1)
    until = jnp.where(row_of <= column_of, 1.0, 0.0).astype(jnp.bfloat16)
    named = [jnp.where(route == owner, 1.0, 0.0) for owner in range(n_micro)]
    named = jnp.concatenate(named, axis=0).astype(jnp.bfloat16)
    inner_rank = jnp.dot(named, until, preferred_element_type=jnp.float32)
    whole = jnp.dot(
        named, jnp.ones((128, 128), jnp.bfloat16), preferred_element_type=jnp.float32
    ).astype(jnp.bfloat16)
    span = n_micro * groups
    row_of = lax.broadcasted_iota(jnp.int32, (span, span), 0)
    column_of = lax.broadcasted_iota(jnp.int32, (span, span), 1)
    ahead = jnp.logical_and(column_of < row_of, column_of // groups == row_of // groups)
    before = jnp.dot(
        jnp.where(ahead, 1.0, 0.0).astype(jnp.bfloat16), whole, preferred_element_type=jnp.float32
    )
    ranks = inner_rank + before - 1.0
    rank = jnp.zeros((groups, 128), jnp.float32)
    for owner in range(n_micro):
        rank = jnp.where(route == owner, ranks[owner * groups : (owner + 1) * groups], rank)
    slot_at = lax.broadcasted_iota(jnp.int32, (slots, 128), 0).astype(jnp.float32)

    def spot(owner, carry):
        local = jnp.where(route == owner, rank, -1.0)
        for g in range(groups):
            hit = jnp.where(local[g : g + 1] == slot_at, 1.0, 0.0)
            spots[owner, :, g * 128 : (g + 1) * 128] = hit.astype(jnp.bfloat16)
        return carry

    lax.fori_loop(0, n_micro, spot, 0)

    for it in range(basis.shape[0]):
        for c in range(3):
            basis[it, c] = jnp.zeros((rows, lanes), jnp.float32)
    elem[...] = jnp.zeros(elem.shape, jnp.float32)
    values[...] = jnp.zeros(values.shape, jnp.float32)
    bundle[...] = jnp.zeros(bundle.shape, jnp.float32)
    for g in range(groups):
        bundle[6:7, g * 128 : (g + 1) * 128] = counts_ref[g : g + 1].astype(jnp.float32)

    for at, (dx, dy) in enumerate(AROUND):

        @pl.when(jnp.logical_not(inside(dx, dy)))
        def _():
            for it in range(ITERS):
                halo[it, at] = jnp.zeros(halo.shape[2:], jnp.float32)

    after = ((1, 0), (0, 1), (1, 1))
    for at, (dx, dy) in enumerate(after):

        @pl.when(jnp.logical_not(inside(dx, dy)))
        def _():
            near_disp[at] = jnp.zeros(near_disp.shape[1:], jnp.float32)

    owned = [(i, j) for i in range(count_x) for j in range(count_y)]
    column_at = {place: at for at, place in enumerate(owned)}
    handed = [((1, 0), (count_x - 1, j), (0, j + 1)) for j in range(count_y)]
    handed += [((0, 1), (i, count_y - 1), (i + 1, 0)) for i in range(count_x)]
    handed += [((1, 1), (count_x - 1, count_y - 1), (0, 0))]
    for at, ((dx, dy), _, _) in enumerate(handed):

        @pl.when(jnp.logical_not(inside(-dx, -dy)))
        def _():
            beside[at] = jnp.zeros(beside.shape[1:], jnp.float32)

    pl.semaphore_wait(barrier, total - 1)

    def show(at):
        dx, dy = after[at]
        return pltpu.make_async_remote_copy(
            src_ref=disp_ref,
            dst_ref=near_disp.at[at],
            send_sem=disp_send.at[at],
            recv_sem=disp_recv.at[at],
            device_id=(a - dx, b - dy),
            device_id_type=MESH,
        )

    for at, (dx, dy) in enumerate(after):

        @pl.when(inside(-dx, -dy))
        def _():
            show(at).start()

    for c in range(3):
        for i, j in owned:
            basis[0, c, pl.ds((i + 1) * wide + j + 1, 1)] = disp_ref[c, i, j : j + 1]
    for at, (dx, dy) in enumerate(after):

        @pl.when(inside(-dx, -dy))
        def _():
            show(at).wait_send()

        @pl.when(inside(dx, dy))
        def _():
            pltpu.make_async_remote_copy(
                src_ref=disp_ref,
                dst_ref=near_disp.at[at],
                send_sem=disp_send.at[at],
                recv_sem=disp_recv.at[at],
                device_id=(a + dx, b + dy),
                device_id_type=MESH,
            ).wait_recv()

    for c in range(3):
        for j in range(count_y):
            basis[0, c, pl.ds((count_x + 1) * wide + j + 1, 1)] = near_disp[0, c, 0, j : j + 1]
        for i in range(count_x):
            basis[0, c, pl.ds((i + 1) * wide + count_y + 1, 1)] = near_disp[1, c, i, 0:1]
        basis[0, c, pl.ds((count_x + 1) * wide + count_y + 1, 1)] = near_disp[2, c, 0, 0:1]

    row_at = lax.broadcasted_iota(jnp.int32, (rows, lanes), 0)
    lane_at = lax.broadcasted_iota(jnp.int32, (rows, lanes), 1)
    own = row_at < 0
    for i in range(1, count_x + 1):
        low = i * wide + 1
        own = jnp.logical_or(own, jnp.logical_and(row_at >= low, row_at < low + count_y))

    def up(value, axis):
        if axis == 2:
            moved = pltpu.roll(value, lanes - 1, 1)
            return jnp.where(lane_at == lanes - 1, 0.0, moved)
        return pltpu.roll(value, rows - (wide if axis == 0 else 1), 0)

    def down(value, axis):
        if axis == 2:
            return jnp.where(lane_at == 0, 0.0, pltpu.roll(value, 1, 1))
        return pltpu.roll(value, wide if axis == 0 else 1, 0)

    def strain_of(it):
        grads = []
        for c in range(3):
            value = basis[it, c]
            moved = up(value, 2)
            total, gap = value + moved, moved - value
            total_up, gap_up = up(total, 1), up(gap, 1)
            flat, slope_y, slope_z = total + total_up, total_up - total, gap + gap_up
            grads.append(
                (
                    0.25 * (up(flat, 0) - flat),
                    0.25 * (up(slope_y, 0) + slope_y),
                    0.25 * (up(slope_z, 0) + slope_z),
                )
            )
        return [
            grads[0][0],
            grads[1][1],
            grads[2][2],
            grads[1][2] + grads[2][1],
            grads[0][2] + grads[2][0],
            grads[0][1] + grads[1][0],
        ]

    strain = strain_of(0)
    for at, (i, j) in enumerate(owned):
        low = (i + 1) * wide + j + 1
        for k in range(6):
            bundle[k : k + 1, at * lanes : (at + 1) * lanes] = strain[k][low : low + 1]
    exact = bundle[...]
    high = exact.astype(jnp.bfloat16).astype(jnp.float32)
    both = jnp.concatenate([high, exact - high], axis=0).astype(jnp.bfloat16)

    def route_copy(other, mine):
        return pltpu.make_async_remote_copy(
            src_ref=route_out.at[other],
            dst_ref=route_in.at[mine],
            send_sem=route_send.at[other],
            recv_sem=route_recv.at[mine],
            device_id=(a, other),
            device_id_type=MESH,
        )

    def hand_out(at, carry):
        other = lax.rem(b + place_of(n_micro - 1 - at, n_micro), n_micro)
        moved = lax.dot_general(
            both, spots[other], (((1,), (1,)), ((), ())), preferred_element_type=jnp.float32
        )
        moved = moved[:8] + moved[8:]

        @pl.when(other != b)
        def _():
            route_out[other] = moved
            route_copy(other, b).start()

        @pl.when(other == b)
        def _():
            route_in[b] = moved

        return carry

    lax.fori_loop(0, n_micro, hand_out, 0)
    for copy in weights:
        copy.wait()

    lame_first, lame_shear = first_ref[0], shear_ref[0]
    tall_at = lax.broadcasted_iota(jnp.int32, (tall, slots), 0)
    on_trace = jnp.where(tall_at < 3, lame_first, 0.0)
    on_strain = jnp.where(tall_at < 3, 2.0 * lame_shear, jnp.where(tall_at < 6, lame_shear, 0.0))
    base = jnp.zeros((tall, slots), jnp.float32)
    for at, (i, j) in enumerate(PAIRS):
        if i == j:
            amount = lame_first + 2.0 * lame_shear if i < 3 else lame_shear
        elif j < 3:
            amount = lame_first
        else:
            continue
        base = jnp.where(tall_at == 6 + at, amount, base)

    def back_copy(other, mine):
        return pltpu.make_async_remote_copy(
            src_ref=back_out.at[other],
            dst_ref=back_in.at[mine],
            send_sem=back_send.at[other],
            recv_sem=back_recv.at[mine],
            device_id=(a, other),
            device_id_type=MESH,
        )

    def solve(at, carry):
        other = lax.rem(b + place_of(at, n_micro), n_micro)

        @pl.when(other != b)
        def _():
            route_copy(b, other).wait_recv()

        points_in = route_in[other]
        sweeps = points_in[6:7]
        modal_load = jnp.dot(
            force_t[...], points_in.astype(jnp.bfloat16), preferred_element_type=jnp.float32
        )
        modes = None
        for sweep in range(ITMAX):
            misfit = -modal_load
            if modes is not None:
                misfit = (
                    jnp.dot(
                        stiff[...], modes.astype(jnp.bfloat16), preferred_element_type=jnp.float32
                    )
                    + BETA * jnp.tanh(modes)
                    - modal_load
                )
            change = jnp.where(sweeps > sweep, OMEGA, 0.0) * jnp.dot(
                pre[...], misfit.astype(jnp.bfloat16), preferred_element_type=jnp.float32
            )
            modes = -change if modes is None else modes - change
        bent = jnp.tanh(modes)
        slope = 1.0 - bent * bent
        trace = points_in[0:1] + points_in[1:2] + points_in[2:3]
        padded = jnp.concatenate(
            [points_in, jnp.zeros((tall - 8, slots), jnp.float32)], axis=0
        )
        answer = on_trace * trace + on_strain * padded + base
        answer = answer + jnp.dot(
            couple[...], modes.astype(jnp.bfloat16), preferred_element_type=jnp.float32
        )
        answer = answer + jnp.dot(
            products[...], slope.astype(jnp.bfloat16), preferred_element_type=jnp.float32
        )

        @pl.when(other != b)
        def _():
            back_out[other] = answer
            back_copy(other, b).start()

        @pl.when(other == b)
        def _():
            back_in[b] = answer

        return carry

    lax.fori_loop(0, n_micro, solve, 0)

    def take_back(at, carry):
        other = lax.rem(b - place_of(at, n_micro) + n_micro, n_micro)

        @pl.when(other != b)
        def _():
            back_copy(b, other).wait_recv()

        exact = back_in[other]
        high = exact.astype(jnp.bfloat16).astype(jnp.float32)
        both = jnp.concatenate([high, exact - high], axis=0).astype(jnp.bfloat16)
        moved = jnp.dot(both, spots[other], preferred_element_type=jnp.float32)
        values[...] += moved[:tall] + moved[tall:]
        return carry

    lax.fori_loop(0, n_micro, take_back, 0)

    def side_copy(at):
        (dx, dy), place, _ = handed[at]
        low = column_at[place] * lanes
        return pltpu.make_async_remote_copy(
            src_ref=values.at[:, pl.ds(low, lanes)],
            dst_ref=beside.at[at],
            send_sem=side_send.at[at],
            recv_sem=side_recv.at[at],
            device_id=(a + dx, b + dy),
            device_id_type=MESH,
        )

    for at, ((dx, dy), _, _) in enumerate(handed):

        @pl.when(inside(dx, dy))
        def _():
            side_copy(at).start()

    def put_column(read, row):
        for v in range(6 + len(PAIRS)):
            elem[v, pl.ds(row, 1)] = read(v)

    for at, (i, j) in enumerate(owned):
        put_column(
            lambda v: values[v : v + 1, at * lanes : (at + 1) * lanes], (i + 1) * wide + j + 1
        )
    for at, ((dx, dy), _, (i, j)) in enumerate(handed):

        @pl.when(inside(dx, dy))
        def _():
            side_copy(at).wait_send()

        @pl.when(inside(-dx, -dy))
        def _():
            pltpu.make_async_remote_copy(
                src_ref=values.at[:, pl.ds(0, lanes)],
                dst_ref=beside.at[at],
                send_sem=side_send.at[at],
                recv_sem=side_recv.at[at],
                device_id=(a - dx, b - dy),
                device_id_type=MESH,
            ).wait_recv()

        put_column(lambda v: beside[at, v : v + 1], i * wide + j)

    def near(step, count):
        return {0: list(range(1, count + 1)), -1: [1], 1: [count]}[step]

    def far(step, count):
        return {0: list(range(1, count + 1)), -1: [0], 1: [count + 1]}[step]

    def places(at, pick):
        dx, dy = AROUND[at]
        return [i * wide + j for i in pick(dx, count_x) for j in pick(dy, count_y)]

    def hop(it, at):
        dx, dy = AROUND[at]
        other = len(AROUND) - 1 - at
        return pltpu.make_async_remote_copy(
            src_ref=send_halo.at[it, at],
            dst_ref=halo.at[it, other],
            send_sem=send_sem.at[it, at],
            recv_sem=recv_sem.at[it, other],
            device_id=(a + dx, b + dy),
            device_id_type=MESH,
        )

    def halo_start(it):
        for at, (dx, dy) in enumerate(AROUND):

            @pl.when(inside(dx, dy))
            def _():
                mine = places(at, near)
                for c in range(3):
                    for k, row in enumerate(mine):
                        send_halo[it, at, pl.ds(c * len(mine) + k, 1)] = basis[it, c, pl.ds(row, 1)]
                hop(it, at).start()

    def halo_finish(it):
        for at, (dx, dy) in enumerate(AROUND):

            @pl.when(inside(dx, dy))
            def _():
                hop(it, at).wait_send()
                pltpu.make_async_remote_copy(
                    src_ref=send_halo.at[it, at],
                    dst_ref=halo.at[it, at],
                    send_sem=send_sem.at[it, at],
                    recv_sem=recv_sem.at[it, at],
                    device_id=(a + dx, b + dy),
                    device_id_type=MESH,
                ).wait_recv()

        for at in range(len(AROUND)):
            theirs = places(at, far)
            for c in range(3):
                for k, row in enumerate(theirs):
                    basis[it, c, pl.ds(row, 1)] = halo[it, at, pl.ds(c * len(theirs) + k, 1)]

    def force_of(stress, c):
        first, second, third = (stress[VOIGT[c][d]] for d in range(3))
        first = first + down(first, 2)
        second = second + down(second, 2)
        third = down(third, 2) - third
        first = first + down(first, 1)
        rest = down(second, 1) - second + third + down(third, 1)
        return 0.25 * (down(first, 0) - first + rest + down(rest, 0))

    def applied(it):
        strain = strain_of(it)
        stress = []
        for i in range(6):
            value = None
            for j in range(6):
                term = elem[6 + PAIR_AT[(min(i, j), max(i, j))]] * strain[j]
                value = term if value is None else value + term
            stress.append(value)
        return [
            jnp.where(own, MASS * basis[it, c] + force_of(stress, c), 0.0) for c in range(3)
        ]

    def product(first, second):
        total = None
        for c in range(3):
            term = first[c] * second[c]
            total = term if total is None else total + term
        total = jnp.sum(jnp.where(own, total, 0.0), axis=0, keepdims=True)
        value = total[:, :128]
        for at in range(128, lanes, 128):
            value = value + total[:, at : at + 128]
        return value

    def stacked(pieces):
        tile_row = lax.broadcasted_iota(jnp.int32, (16, 128), 0)
        value = jnp.zeros((16, 128), jnp.float32)
        for at, piece in enumerate(pieces):
            value = jnp.where(tile_row == at, piece, value)
        return value

    def gather_start(src, dst, count, mine, send, recv, device):
        copies = []
        for step in range(1, count):
            copy = pltpu.make_async_remote_copy(
                src_ref=src,
                dst_ref=dst.at[mine],
                send_sem=send.at[step - 1],
                recv_sem=recv.at[step - 1],
                device_id=device(lax.rem(mine + step, count)),
                device_id_type=MESH,
            )
            copy.start()
            copies.append(copy)
        dst[mine] = src[...]
        return copies

    def gather_finish(copies, dst, count):
        for copy in copies:
            copy.wait()
        total = dst[0]
        for at in range(1, count):
            total = total + dst[at]
        return total

    stress = [elem[i] for i in range(6)]
    zero = jnp.zeros((rows, lanes), jnp.float32)
    for c in range(3):
        padded = jnp.concatenate(
            [jnp.zeros((wide + 1, lanes), jnp.float32)]
            + [
                piece
                for i in range(count_x)
                for piece in (load_ref[c, i], jnp.zeros((2, lanes), jnp.float32))
            ]
            + [jnp.zeros((rows - 1 - wide * (count_x + 1), lanes), jnp.float32)],
            axis=0,
        )
        basis[0, c] = jnp.where(own, padded - force_of(stress, c), zero)
    halo_start(0)
    halo_finish(0)
    grown = applied(0)
    for c in range(3):
        basis[1, c] = grown[c]
    halo_start(1)
    start = [basis[0, c] for c in range(3)]
    part[...] = stacked([product(start, start), product(grown, grown)])
    copies = gather_start(
        part, got_micro, n_micro, b, micro_send, micro_recv, lambda other: (a, other)
    )
    halo_finish(1)
    grown = applied(1)
    for c in range(3):
        basis[2, c] = grown[c]
    halo_start(2)
    middle[...] = gather_finish(copies, got_micro, n_micro)
    copies = gather_start(
        middle, got_macro, n_macro, a, macro_send, macro_recv, lambda other: (other, b)
    )
    halo_finish(2)
    totals = jnp.sum(gather_finish(copies, got_macro, n_macro), axis=1, keepdims=True)
    shift = jnp.sqrt(totals[1:2] / totals[0:1])
    scale = 1.0 / shift
    for c in range(3):
        u0, w1, w2 = basis[0, c], basis[1, c] * scale, basis[2, c] * (scale * scale)
        basis[1, c] = w1 - u0
        basis[2, c] = (w2 - w1) - (w1 - u0)

    def field(it):
        return [basis[it, c] for c in range(3)]

    def step(it):
        grown = applied(it)
        return [grown[c] * scale - jnp.where(own, basis[it, c], 0.0) for c in range(3)]

    moments = []
    for it in range(2, ITERS):
        grown = step(it)
        if it + 1 < ITERS:
            for c in range(3):
                basis[it + 1, c] = grown[c]
            halo_start(it + 1)
            if it == 2:
                for k in range(3):
                    moments.append(product(field(k), field(k)))
                    moments.append(product(field(k), field(k + 1)))
            else:
                moments.append(product(field(it), field(it)))
                moments.append(product(field(it), field(it + 1)))
            halo_finish(it + 1)
    moments.append(product(field(ITERS - 1), field(ITERS - 1)))
    moments.append(product(field(ITERS - 1), grown))
    sums = jnp.sum(stacked(moments), axis=1, keepdims=True)
    diagonal = lax.broadcasted_iota(jnp.int32, (16, 128), 0) == lax.broadcasted_iota(
        jnp.int32, (16, 128), 1
    )
    last_part[...] = jnp.sum(jnp.where(diagonal, sums, 0.0), axis=0, keepdims=True)

    def last_copy(step, other):
        return pltpu.make_async_remote_copy(
            src_ref=last_part,
            dst_ref=last_all.at[me],
            send_sem=last_send.at[step],
            recv_sem=last_recv.at[step],
            device_id=device(other),
            device_id_type=MESH,
        )

    def last_start(step, carry):
        last_copy(step, lax.rem(me + step, total)).start()
        return carry

    def last_wait(step, carry):
        last_copy(step, lax.rem(me + step, total)).wait()
        return carry

    lax.fori_loop(1, total, last_start, 0)
    last_all[me] = last_part[...]
    lax.fori_loop(1, total, last_wait, 0)
    totals = jnp.sum(last_all[...], axis=0)
    held = [totals[:, k : k + 1] for k in range(2 * ITERS)]

    def inner(first, second, extra=0):
        gathered = {}
        for i, x in enumerate(first):
            for j, y in enumerate(second):
                gathered.setdefault(i + j, []).append(x * y)
        value = None
        for degree, terms in gathered.items():
            total = terms[0]
            for term in terms[1:]:
                total = total + term
            total = total * held[degree + extra]
            value = total if value is None else value + total
        return value

    one = jnp.ones((1, 1), jnp.float32)
    left, toward, done = [one], [one], []
    norm = held[0]
    for it in range(ITERS):
        energy = inner(toward, toward) + inner(toward, toward, 1)
        length = norm / energy
        done = [x + length * scale * p for x, p in zip(done + [0.0], toward)]
        raised = [
            (toward[k] if k < len(toward) else 0.0) + (toward[k - 1] if k > 0 else 0.0)
            for k in range(len(toward) + 1)
        ]
        left = [
            (left[k] if k < len(left) else 0.0) - length * raised[k] for k in range(len(raised))
        ]
        if it + 1 < ITERS:
            fresh = inner(left, left)
            ratio = fresh / norm
            toward = [
                left[k] + (ratio * toward[k] if k < len(toward) else 0.0)
                for k in range(len(left))
            ]
            norm = fresh
    for c in range(3):
        fields = [basis[k, c] for k in range(ITERS)] + [grown[c]]
        moved, rest = None, None
        for k in range(ITERS + 1):
            if k < len(done):
                term = done[k] * fields[k]
                moved = term if moved is None else moved + term
            term = left[k] * fields[k]
            rest = term if rest is None else rest + term
        for i in range(count_x):
            low = (i + 1) * wide + 1
            inc_ref[c, i] = moved[low : low + count_y]
            res_ref[c, i] = rest[low : low + count_y]

    def sent(step, carry):
        other = lax.rem(b + step, n_micro)
        route_copy(other, b).wait_send()
        back_copy(other, b).wait_send()
        return carry

    lax.fori_loop(1, n_micro, sent, 0)


def shards(
    displacement,
    load,
    routes,
    counts,
    stiffness,
    precond,
    forcing,
    coupling,
    lame_first,
    lame_shear,
):
    _, count_x, count_y, lanes = displacement.shape
    points = count_x * count_y * lanes
    n_macro, n_micro = lax.axis_size("macro"), lax.axis_size("micro")
    capacity = max(2, 2 * points // n_micro)
    slots = -(-capacity // 128) * 128
    size = stiffness.shape[1]
    tall = -(-(6 + len(PAIRS)) // 8) * 8
    rows = -(-(count_x + 2) * (count_y + 2) // 8) * 8
    side = -(-3 * max(count_x, count_y) // 8) * 8
    total = n_macro * n_micro
    sides = count_x + count_y + 1
    vmem = pl.BlockSpec(memory_space=pltpu.VMEM)
    smem = pl.BlockSpec(memory_space=pltpu.SMEM)
    anywhere = pl.BlockSpec(memory_space=pl.ANY)
    dma = pltpu.SemaphoreType.DMA

    def held(*shape):
        return pltpu.VMEM(shape, jnp.float32)

    def half(*shape):
        return pltpu.VMEM(shape, jnp.bfloat16)

    def body(*refs):
        newton_kernel((count_x, count_y, lanes, n_macro, n_micro), *refs)

    return tuple(
        pl.pallas_call(
            body,
            out_shape=[jax.ShapeDtypeStruct(load.shape, jnp.float32)] * 2,
            in_specs=[vmem] * 4 + [anywhere] * 2 + [vmem] * 2 + [smem] * 2,
            out_specs=[vmem, vmem],
            scratch_shapes=[
                half(size, size),
                half(size, size),
                half(size, 8),
                half(tall, size),
                half(tall, size),
                held(tall, size),
                half(n_micro, slots, points),
                held(3, *displacement.shape),
                held(8, points),
                held(n_micro, 8, slots),
                held(n_micro, 8, slots),
                held(n_micro, tall, slots),
                held(n_micro, tall, slots),
                held(tall, points),
                held(sides, tall, lanes),
                held(6 + len(PAIRS), rows, lanes),
                held(ITERS, 3, rows, lanes),
                held(ITERS, len(AROUND), side, lanes),
                held(ITERS, len(AROUND), side, lanes),
                held(16, 128),
                held(n_micro, 16, 128),
                held(16, 128),
                held(n_macro, 16, 128),
                held(1, 128),
                held(total, 1, 128),
                dma((2,)),
                dma((3,)),
                dma((3,)),
                dma((n_micro,)),
                dma((n_micro,)),
                dma((n_micro,)),
                dma((n_micro,)),
                dma((sides,)),
                dma((sides,)),
                dma((ITERS, len(AROUND))),
                dma((ITERS, len(AROUND))),
                dma((n_micro - 1,)),
                dma((n_micro - 1,)),
                dma((n_macro - 1,)),
                dma((n_macro - 1,)),
                dma((total,)),
                dma((total,)),
            ],
            compiler_params=pltpu.CompilerParams(collective_id=0, has_side_effects=True),
            name="newton_step",
        )(
            displacement,
            load,
            routes.reshape(points // 128, 128),
            counts.reshape(points // 128, 128),
            stiffness[0],
            precond[0],
            forcing[0],
            coupling[0].T,
            lame_first,
            lame_shear,
        )
    )


def solution(mesh):
    in_specs = (
        P(None, "macro", "micro", None),
        P(None, "macro", "micro", None),
        P("macro", "micro", None, None),
        P("macro", "micro", None),
        P("micro", None, None),
        P("micro", None, None),
        P("micro", None, None),
        P("micro", None, None),
        P("micro"),
        P("micro"),
    )
    out_specs = (P(None, "macro", "micro", None), P(None, "macro", "micro", None))
    return jax.shard_map(shards, mesh=mesh, in_specs=in_specs, out_specs=out_specs, check_vma=False)
```

time: 118 us -> 70.5 us (0.60)
  starting transfers between devices: 24.1 us -> 0 us
  waiting for transfers between devices: 18 us -> 0 us
  local copies, waits for them, and re-layouts: 19.1 us -> 1.92 us
  Pallas kernels: 49.7 us -> 66.4 us
  other arithmetic: 3.46 us -> 0 us
    pallas_call x2 -> x1, Pallas kernels: 49.7 us -> 66.4 us  [shards(): pl.pallas_call(body, out_shape=[jax.ShapeDtypeStruct(load.shape, jnp.floa...]
    ppermute x6 -> x0, starting transfers between devices: 14.7 us -> none  [the longest x2 6.32 us: with_halo(): lax.ppermute(lax.slice_in_dim(block, block.shape[dim] - width, None, axis...]
    all_to_all x2 -> x0, waiting for transfers between devices: 13.5 us -> none  [the longest x1 9.62 us: shards(): lax.all_to_all(rows, 'micro', split_axis=1, concat_axis=1, tiled=True)]
    all_to_all x2 -> x0, starting transfers between devices: 9.32 us -> none  [the longest x1 5.91 us: shards(): got = lax.all_to_all(send, 'micro', split_axis=1, concat_axis=1, tiled=True)]
    ppermute x6 -> x0, waiting for transfers between devices: 4.53 us -> none  [the longest x2 2.51 us: with_halo(): lax.ppermute(lax.slice_in_dim(block, 0, width, axis=dim), axis, backward)]
    scatter x1 -> x0, local copies, waits for them, and re-layouts: 3.34 us -> none  [shards(): jnp.zeros((8, owners * capacity), jnp.float32).at[:, target]]
    unnamed x33 -> x4, local copies, waits for them, and re-layouts: 5.11 us -> 1.92 us
    gather x1 -> x0, local copies, waits for them, and re-layouts: 2.81 us -> none  [shards(): values = jnp.take(back, target, axis=1, unique_indices=True, mode='clip')]
  transfers between devices with their start and end apart: 8 -> 0, of which waited for: 5 -> 0; matrix products, arithmetic and copies ran while one was open for 6% -> 0% of each run, Pallas kernels for 0% -> 0%
where the time goes in v2:
time: 70.5 us; the launch traced here: 70.2 us
  Pallas kernels  66.4 us (94%)
  between operations  1.94 us (3%)
  local copies, waits for them, and re-layouts  1.92 us (3%)
    pallas_call x1, Pallas kernels, shards(): pl.pallas_call(body, out_shape=[jax.ShapeDtypeStruct(load.shape, jnp.floa...  66.4 us
    unnamed x4, local copies, waits for them, and re-layouts  1.92 us

profile of v2, /device:TPU:0, one launch (start us, length us, event | category | flops | bytes accessed | tf_op | source)
XLA Modules:
  0.0 70.2 jit_solution(10231913118434077739)
XLA Ops:
  1.9 66.4 %newton_step.1 = (f32[3,2,2,256]{3,2,1,0:T(2,128)}, f32[3,2,2,256]{3,2,1,0:T(2,128)}) custom-call(f32[3,2,2,256]{3,2,1,0:T(2,128)} %refs_0_.1, f32[3,2,2,256]{3,2,1,0:T(2,128)} %refs_1_.1, s32[8,128]{1,0:T(8,128)} %bitcast.12, s32[8,128]{1,0:T(8,128)} %bitcast.13, bf16[512,512]{1,0:T(8,128)(2,1)} %bitcast.8, bf16[512,512]{1,0:T(8,128)(2,1)} %bitcast.9, ...), custom_call_target="tpu_custom_call" | custom-call | tf_op jit(solution)/shard_map/newton_step/pallas_call | solution.py:781
  68.3 0.0 copy-start
  68.3 1.3 %copy.16 = f32[3,2,2,256]{3,2,1,0:T(2,128)} copy(f32[3,2,2,256]{3,2,1,0:T(2,128)} %get-tuple-element.4) | data formatting | bytes 24576
  69.6 0.0 copy-done
  69.6 0.6 copy.17
Async XLA Ops:
  68.3 1.3 %copy-start = (f32[3,2,2,256]{3,2,1,0:T(2,128)S(1)}, f32[3,2,2,256]{3,2,1,0:T(2,128)}, u32[]{:S(2)}) copy-start(f32[3,2,2,256]{3,2,1,0:T(2,128)} %get-tuple-element.5) | copy-start | bytes 36868

commit v3 on v2

--- a/solution.py
+++ b/solution.py
@@ -17,11 +17,6 @@
 PAIR_AT = {pair: at for at, pair in enumerate(PAIRS)}
 AROUND = tuple((dx, dy) for dx in (-1, 0, 1) for dy in (-1, 0, 1) if (dx, dy) != (0, 0))
 MESH = pl.DeviceIdType.MESH
-
-
-def place_of(at, count):
-    turned = jnp.where(at < 2, at, count + 1 - at)
-    return lax.rem(jnp.where(turned % 2 == 1, (turned + 1) // 2, count - turned // 2), count)
 
 
 def newton_kernel(
@@ -84,8 +79,9 @@
     count_x, count_y, lanes, n_macro, n_micro = sizes
     wide = count_y + 2
     rows = basis.shape[2]
-    slots = spots.shape[1]
-    points = spots.shape[2]
+    points = spots.shape[1]
+    slots = spots.shape[0] // n_micro
+    pairs = n_micro // 2
     groups = points // 128
     size = stiff.shape[0]
     tall = couple.shape[0]
@@ -159,7 +155,8 @@
         local = jnp.where(route == owner, rank, -1.0)
         for g in range(groups):
             hit = jnp.where(local[g : g + 1] == slot_at, 1.0, 0.0)
-            spots[owner, :, g * 128 : (g + 1) * 128] = hit.astype(jnp.bfloat16)
+            low = pl.multiple_of(owner * slots, slots)
+            spots[pl.ds(low, slots), g * 128 : (g + 1) * 128] = hit.astype(jnp.bfloat16)
         return carry
 
     lax.fori_loop(0, n_micro, spot, 0)
@@ -305,33 +302,44 @@
             device_id_type=MESH,
         )
 
+    chip, core = b // 2, lax.rem(b, 2)
+
+    def pair_rows(place):
+        return pl.ds(pl.multiple_of(place * (2 * slots), 2 * slots), 2 * slots)
+
     def hand_out(at, carry):
-        other = lax.rem(b + place_of(n_micro - 1 - at, n_micro), n_micro)
+        place = lax.rem(chip + pairs - 1 - at, pairs)
         moved = lax.dot_general(
-            both, spots[other], (((1,), (1,)), ((), ())), preferred_element_type=jnp.float32
+            both,
+            spots[pair_rows(place)],
+            (((1,), (1,)), ((), ())),
+            preferred_element_type=jnp.float32,
         )
         moved = moved[:8] + moved[8:]
-
-        @pl.when(other != b)
-        def _():
-            route_out[other] = moved
-            route_copy(other, b).start()
-
-        @pl.when(other == b)
-        def _():
-            route_in[b] = moved
+        for k in range(2):
+            other = 2 * place + k
+            piece = moved[:, k * slots : (k + 1) * slots]
+
+            @pl.when(other != b)
+            def _():
+                route_out[other] = piece
+                route_copy(other, b).start()
+
+            @pl.when(other == b)
+            def _():
+                route_in[b] = piece
 
         return carry
 
-    lax.fori_loop(0, n_micro, hand_out, 0)
+    lax.fori_loop(0, pairs, hand_out, 0)
     for copy in weights:
         copy.wait()
 
     lame_first, lame_shear = first_ref[0], shear_ref[0]
-    tall_at = lax.broadcasted_iota(jnp.int32, (tall, slots), 0)
+    tall_at = lax.broadcasted_iota(jnp.int32, (tall, 2 * slots), 0)
     on_trace = jnp.where(tall_at < 3, lame_first, 0.0)
     on_strain = jnp.where(tall_at < 3, 2.0 * lame_shear, jnp.where(tall_at < 6, lame_shear, 0.0))
-    base = jnp.zeros((tall, slots), jnp.float32)
+    base = jnp.zeros((tall, 2 * slots), jnp.float32)
     for at, (i, j) in enumerate(PAIRS):
         if i == j:
             amount = lame_first + 2.0 * lame_shear if i < 3 else lame_shear
@@ -352,37 +360,40 @@
         )
 
     def solve(at, carry):
-        other = lax.rem(b + place_of(at, n_micro), n_micro)
-
-        @pl.when(other != b)
-        def _():
-            route_copy(b, other).wait_recv()
-
-        points_in = route_in[other]
+        place = lax.rem(chip + at, pairs)
+        taken = []
+        for k in range(2):
+            other = 2 * place + k
+
+            @pl.when(other != b)
+            def _():
+                route_copy(b, other).wait_recv()
+
+            taken.append(route_in[other])
+        points_in = jnp.concatenate(taken, axis=1)
         sweeps = points_in[6:7]
         modal_load = jnp.dot(
             force_t[...], points_in.astype(jnp.bfloat16), preferred_element_type=jnp.float32
         )
         modes = None
         for sweep in range(ITMAX):
-            misfit = -modal_load
-            if modes is not None:
-                misfit = (
-                    jnp.dot(
-                        stiff[...], modes.astype(jnp.bfloat16), preferred_element_type=jnp.float32
-                    )
-                    + BETA * jnp.tanh(modes)
-                    - modal_load
-                )
-            change = jnp.where(sweeps > sweep, OMEGA, 0.0) * jnp.dot(
-                pre[...], misfit.astype(jnp.bfloat16), preferred_element_type=jnp.float32
-            )
-            modes = -change if modes is None else modes - change
+            if modes is None:
+                misfit = (-modal_load).astype(jnp.bfloat16)
+            else:
+                short = modes.astype(jnp.bfloat16)
+                misfit = jnp.dot(stiff[...], short, preferred_element_type=jnp.float32)
+                misfit = (misfit - modal_load).astype(jnp.bfloat16)
+                misfit = misfit + jnp.tanh(short) * jnp.bfloat16(BETA)
+            change = jnp.dot(pre[...], misfit, preferred_element_type=jnp.float32)
+            if modes is None:
+                modes = -OMEGA * change
+            else:
+                modes = modes - jnp.where(sweeps > sweep, OMEGA, 0.0) * change
         bent = jnp.tanh(modes)
         slope = 1.0 - bent * bent
         trace = points_in[0:1] + points_in[1:2] + points_in[2:3]
         padded = jnp.concatenate(
-            [points_in, jnp.zeros((tall - 8, slots), jnp.float32)], axis=0
+            [points_in, jnp.zeros((tall - 8, 2 * slots), jnp.float32)], axis=0
         )
         answer = on_trace * trace + on_strain * padded + base
         answer = answer + jnp.dot(
@@ -391,35 +402,42 @@
         answer = answer + jnp.dot(
             products[...], slope.astype(jnp.bfloat16), preferred_element_type=jnp.float32
         )
-
-        @pl.when(other != b)
-        def _():
-            back_out[other] = answer
-            back_copy(other, b).start()
-
-        @pl.when(other == b)
-        def _():
-            back_in[b] = answer
+        for k in range(2):
+            other = 2 * place + k
+            piece = answer[:, k * slots : (k + 1) * slots]
+
+            @pl.when(other != b)
+            def _():
+                back_out[other] = piece
+                back_copy(other, b).start()
+
+            @pl.when(other == b)
+            def _():
+                back_in[b] = piece
 
         return carry
 
-    lax.fori_loop(0, n_micro, solve, 0)
+    lax.fori_loop(0, pairs, solve, 0)
 
     def take_back(at, carry):
-        other = lax.rem(b - place_of(at, n_micro) + n_micro, n_micro)
-
-        @pl.when(other != b)
-        def _():
-            back_copy(b, other).wait_recv()
-
-        exact = back_in[other]
+        place = lax.rem(chip + pairs - at, pairs)
+        taken = []
+        for k in range(2):
+            other = 2 * place + k
+
+            @pl.when(other != b)
+            def _():
+                back_copy(b, other).wait_recv()
+
+            taken.append(back_in[other])
+        exact = jnp.concatenate(taken, axis=1)
         high = exact.astype(jnp.bfloat16).astype(jnp.float32)
         both = jnp.concatenate([high, exact - high], axis=0).astype(jnp.bfloat16)
-        moved = jnp.dot(both, spots[other], preferred_element_type=jnp.float32)
+        moved = jnp.dot(both, spots[pair_rows(place)], preferred_element_type=jnp.float32)
         values[...] += moved[:tall] + moved[tall:]
         return carry
 
-    lax.fori_loop(0, n_micro, take_back, 0)
+    lax.fori_loop(0, pairs, take_back, 0)
 
     def side_copy(at):
         (dx, dy), place, _ = handed[at]
@@ -790,7 +808,7 @@
                 half(tall, size),
                 half(tall, size),
                 held(tall, size),
-                half(n_micro, slots, points),
+                half(n_micro * slots, points),
                 held(3, *displacement.shape),
                 held(8, points),
                 held(n_micro, 8, slots),

time: 70.5 us -> 63.1 us (0.90)
  Pallas kernels: 66.4 us -> 59 us
    pallas_call x1, Pallas kernels: 66.4 us -> 59 us  [shards(): pl.pallas_call(body, out_shape=[jax.ShapeDtypeStruct(load.shape, jnp.floa...]
where the time goes in v3:
time: 63.1 us; the launch traced here: 62.8 us
  Pallas kernels  59 us (94%)
  between operations  1.94 us (3%)
  local copies, waits for them, and re-layouts  1.92 us (3%)
    pallas_call x1, Pallas kernels, shards(): pl.pallas_call(body, out_shape=[jax.ShapeDtypeStruct(load.shape, jnp.floa...  59 us
    unnamed x4, local copies, waits for them, and re-layouts  1.92 us

profile of v3, /device:TPU:0, one launch (start us, length us, event | category | flops | bytes accessed | tf_op | source)
XLA Modules:
  0.0 62.8 jit_solution(17278206757741759834)
XLA Ops:
  1.9 59.0 %newton_step.1 = (f32[3,2,2,256]{3,2,1,0:T(2,128)}, f32[3,2,2,256]{3,2,1,0:T(2,128)}) custom-call(f32[3,2,2,256]{3,2,1,0:T(2,128)} %refs_0_.1, f32[3,2,2,256]{3,2,1,0:T(2,128)} %refs_1_.1, s32[8,128]{1,0:T(8,128)} %bitcast.12, s32[8,128]{1,0:T(8,128)} %bitcast.13, bf16[512,512]{1,0:T(8,128)(2,1)} %bitcast.8, bf16[512,512]{1,0:T(8,128)(2,1)} %bitcast.9, ...), custom_call_target="tpu_custom_call" | custom-call | tf_op jit(solution)/shard_map/newton_step/pallas_call | solution.py:799
  60.9 0.0 copy-start
  60.9 1.3 %copy.16 = f32[3,2,2,256]{3,2,1,0:T(2,128)} copy(f32[3,2,2,256]{3,2,1,0:T(2,128)} %get-tuple-element.4) | data formatting | bytes 24576
  62.2 0.0 copy-done
  62.2 0.6 copy.17
Async XLA Ops:
  60.9 1.3 %copy-start = (f32[3,2,2,256]{3,2,1,0:T(2,128)S(1)}, f32[3,2,2,256]{3,2,1,0:T(2,128)}, u32[]{:S(2)}) copy-start(f32[3,2,2,256]{3,2,1,0:T(2,128)} %get-tuple-element.5) | copy-start | bytes 36868

commit v4 on v3

--- a/solution.py
+++ b/solution.py
@@ -35,7 +35,7 @@
     res_ref,
     stiff,
     pre,
-    force_t,
+    maps,
     couple,
     products,
     wide_products,
@@ -118,7 +118,7 @@
 
     force = force_ref[...].astype(jnp.float32)
     force = jnp.concatenate([force, jnp.zeros((2, size), jnp.float32)], axis=0)
-    force_t[...] = force.T.astype(jnp.bfloat16)
+    load_map = force.T
     wide_products[...] = jnp.zeros((tall, size), jnp.float32)
     coupling = couple_ref[...].astype(jnp.float32)
     wide_products[pl.ds(0, 6)] = coupling
@@ -214,6 +214,21 @@
         def _():
             show(at).start()
 
+    for copy in weights:
+        copy.wait()
+
+    def split(exact):
+        high = exact.astype(jnp.bfloat16)
+        return jnp.concatenate([high, (exact - high.astype(jnp.float32)).astype(jnp.bfloat16)], axis=1)
+
+    def through(matrix, exact):
+        moved = jnp.dot(matrix[...], split(exact), preferred_element_type=jnp.float32)
+        return moved[:, :8] + moved[:, 8:]
+
+    first_map = OMEGA * through(pre, load_map)
+    misfit_map = through(stiff, first_map) - load_map
+    for at, exact in enumerate((first_map, misfit_map, load_map)):
+        maps[pl.ds(at * size, size)] = split(exact)
     for c in range(3):
         for i, j in owned:
             basis[0, c, pl.ds((i + 1) * wide + j + 1, 1)] = disp_ref[c, i, j : j + 1]
@@ -308,7 +323,7 @@
         return pl.ds(pl.multiple_of(place * (2 * slots), 2 * slots), 2 * slots)
 
     def hand_out(at, carry):
-        place = lax.rem(chip + pairs - 1 - at, pairs)
+        place = lax.rem(chip + pairs - at, pairs)
         moved = lax.dot_general(
             both,
             spots[pair_rows(place)],
@@ -332,8 +347,7 @@
         return carry
 
     lax.fori_loop(0, pairs, hand_out, 0)
-    for copy in weights:
-        copy.wait()
+
 
     lame_first, lame_shear = first_ref[0], shear_ref[0]
     tall_at = lax.broadcasted_iota(jnp.int32, (tall, 2 * slots), 0)
@@ -372,23 +386,24 @@
             taken.append(route_in[other])
         points_in = jnp.concatenate(taken, axis=1)
         sweeps = points_in[6:7]
-        modal_load = jnp.dot(
-            force_t[...], points_in.astype(jnp.bfloat16), preferred_element_type=jnp.float32
-        )
-        modes = None
-        for sweep in range(ITMAX):
-            if modes is None:
-                misfit = (-modal_load).astype(jnp.bfloat16)
-            else:
-                short = modes.astype(jnp.bfloat16)
-                misfit = jnp.dot(stiff[...], short, preferred_element_type=jnp.float32)
-                misfit = (misfit - modal_load).astype(jnp.bfloat16)
-                misfit = misfit + jnp.tanh(short) * jnp.bfloat16(BETA)
+        strain_in = points_in.astype(jnp.bfloat16)
+        strain_in = jnp.concatenate([strain_in, strain_in], axis=0)
+
+        def mapped(at):
+            return jnp.dot(
+                maps[pl.ds(at * size, size)], strain_in, preferred_element_type=jnp.float32
+            )
+
+        modes, misfit, modal_load = mapped(0), mapped(1), mapped(2)
+        for sweep in range(1, ITMAX):
+            if sweep > 1:
+                misfit = jnp.dot(
+                    stiff[...], modes.astype(jnp.bfloat16), preferred_element_type=jnp.float32
+                )
+                misfit = misfit - modal_load
+            misfit = (misfit + BETA * jnp.tanh(modes)).astype(jnp.bfloat16)
             change = jnp.dot(pre[...], misfit, preferred_element_type=jnp.float32)
-            if modes is None:
-                modes = -OMEGA * change
-            else:
-                modes = modes - jnp.where(sweeps > sweep, OMEGA, 0.0) * change
+            modes = modes - jnp.where(sweeps > sweep, OMEGA, 0.0) * change
         bent = jnp.tanh(modes)
         slope = 1.0 - bent * bent
         trace = points_in[0:1] + points_in[1:2] + points_in[2:3]
@@ -804,7 +819,7 @@
             scratch_shapes=[
                 half(size, size),
                 half(size, size),
-                half(size, 8),
+                half(3 * size, 16),
                 half(tall, size),
                 half(tall, size),
                 held(tall, size),

time: 63.1 us -> 60.7 us (0.962)
  Pallas kernels: 59 us -> 56.5 us
    pallas_call x1, Pallas kernels: 59 us -> 56.5 us  [shards(): pl.pallas_call(body, out_shape=[jax.ShapeDtypeStruct(load.shape, jnp.floa...]
where the time goes in v4:
time: 60.7 us; the launch traced here: 60.4 us
  Pallas kernels  56.5 us (93%)
  between operations  1.94 us (3%)
  local copies, waits for them, and re-layouts  1.92 us (3%)
    pallas_call x1, Pallas kernels, shards(): pl.pallas_call(body, out_shape=[jax.ShapeDtypeStruct(load.shape, jnp.floa...  56.5 us
    unnamed x4, local copies, waits for them, and re-layouts  1.92 us

profile of v4, /device:TPU:0, one launch (start us, length us, event | category | flops | bytes accessed | tf_op | source)
XLA Modules:
  0.0 60.4 jit_solution(11535972166934546287)
XLA Ops:
  1.9 56.5 %newton_step.1 = (f32[3,2,2,256]{3,2,1,0:T(2,128)}, f32[3,2,2,256]{3,2,1,0:T(2,128)}) custom-call(f32[3,2,2,256]{3,2,1,0:T(2,128)} %refs_0_.1, f32[3,2,2,256]{3,2,1,0:T(2,128)} %refs_1_.1, s32[8,128]{1,0:T(8,128)} %bitcast.12, s32[8,128]{1,0:T(8,128)} %bitcast.13, bf16[512,512]{1,0:T(8,128)(2,1)} %bitcast.8, bf16[512,512]{1,0:T(8,128)(2,1)} %bitcast.9, ...), custom_call_target="tpu_custom_call" | custom-call | tf_op jit(solution)/shard_map/newton_step/pallas_call | solution.py:814
  58.5 0.0 copy-start
  58.5 1.3 %copy.16 = f32[3,2,2,256]{3,2,1,0:T(2,128)} copy(f32[3,2,2,256]{3,2,1,0:T(2,128)} %get-tuple-element.4) | data formatting | bytes 24576
  59.8 0.0 copy-done
  59.8 0.6 copy.17
Async XLA Ops:
  58.5 1.3 %copy-start = (f32[3,2,2,256]{3,2,1,0:T(2,128)S(1)}, f32[3,2,2,256]{3,2,1,0:T(2,128)}, u32[]{:S(2)}) copy-start(f32[3,2,2,256]{3,2,1,0:T(2,128)} %get-tuple-element.5) | copy-start | bytes 36868

commit v5 on v4

--- a/solution.py
+++ b/solution.py
@@ -21,20 +21,26 @@
 
 def newton_kernel(
     sizes,
+    disp_in,
+    load_in,
+    routes_in,
+    counts_in,
+    stiff_in,
+    pre_in,
+    force_in,
+    couple_in,
+    first_ref,
+    shear_ref,
+    inc_ref,
+    res_ref,
     disp_ref,
     load_ref,
     routes_ref,
     counts_ref,
-    stiff_hbm,
-    pre_hbm,
+    stiff,
+    pre,
     force_ref,
     couple_ref,
-    first_ref,
-    shear_ref,
-    inc_ref,
-    res_ref,
-    stiff,
-    pre,
     maps,
     couple,
     products,
@@ -58,7 +64,7 @@
     got_macro,
     last_part,
     last_all,
-    weight_sem,
+    input_sem,
     disp_send,
     disp_recv,
     route_send,
@@ -102,20 +108,39 @@
 
     barrier = pltpu.get_barrier_semaphore()
 
-    def greet(step, carry):
-        pl.semaphore_signal(
-            barrier, inc=1, device_id=device(lax.rem(me + step, total)), device_id_type=MESH
-        )
-        return carry
-
-    lax.fori_loop(1, total, greet, 0)
-    weights = [
-        pltpu.make_async_copy(stiff_hbm, stiff, weight_sem.at[0]),
-        pltpu.make_async_copy(pre_hbm, pre, weight_sem.at[1]),
-    ]
-    for copy in weights:
-        copy.start()
-
+    def every(count, act):
+        if count <= 32:
+            for step in range(1, count):
+                act(step)
+        else:
+            lax.fori_loop(1, count, lambda step, carry: (act(step), carry)[1], 0)
+
+    def greet(row, column):
+        pl.semaphore_signal(barrier, inc=1, device_id=(row, column), device_id_type=MESH)
+
+    for step in range(1, n_macro):
+        for aside in range(3):
+            greet(lax.rem(a + step, n_macro), lax.rem(b + n_micro - 1 + aside, n_micro))
+    every(n_micro, lambda step: greet(a, lax.rem(b + step, n_micro)))
+    greeted = 3 * (n_macro - 1) + n_micro - 1
+    inputs = {}
+    for at, (name, source, target) in enumerate(
+        (
+            ("routes", routes_in, routes_ref),
+            ("force", force_in, force_ref),
+            ("couple", couple_in, couple_ref),
+            ("counts", counts_in, counts_ref),
+            ("disp", disp_in, disp_ref),
+            ("load", load_in, load_ref),
+            ("pre", pre_in, pre),
+            ("stiff", stiff_in, stiff),
+        )
+    ):
+        inputs[name] = pltpu.make_async_copy(source, target, input_sem.at[at])
+        inputs[name].start()
+
+    for name in ("routes", "force", "couple", "counts", "disp"):
+        inputs[name].wait()
     force = force_ref[...].astype(jnp.float32)
     force = jnp.concatenate([force, jnp.zeros((2, size), jnp.float32)], axis=0)
     load_map = force.T
@@ -195,7 +220,7 @@
         def _():
             beside[at] = jnp.zeros(beside.shape[1:], jnp.float32)
 
-    pl.semaphore_wait(barrier, total - 1)
+    pl.semaphore_wait(barrier, greeted)
 
     def show(at):
         dx, dy = after[at]
@@ -214,8 +239,8 @@
         def _():
             show(at).start()
 
-    for copy in weights:
-        copy.wait()
+    for name in ("pre", "stiff", "load"):
+        inputs[name].wait()
 
     def split(exact):
         high = exact.astype(jnp.bfloat16)
@@ -700,17 +725,9 @@
             device_id_type=MESH,
         )
 
-    def last_start(step, carry):
-        last_copy(step, lax.rem(me + step, total)).start()
-        return carry
-
-    def last_wait(step, carry):
-        last_copy(step, lax.rem(me + step, total)).wait()
-        return carry
-
-    lax.fori_loop(1, total, last_start, 0)
+    every(total, lambda step: last_copy(step, lax.rem(me + step, total)).start())
     last_all[me] = last_part[...]
-    lax.fori_loop(1, total, last_wait, 0)
+    every(total, lambda step: last_copy(step, lax.rem(me + step, total)).wait())
     totals = jnp.sum(last_all[...], axis=0)
     held = [totals[:, k : k + 1] for k in range(2 * ITERS)]
 
@@ -814,11 +831,17 @@
         pl.pallas_call(
             body,
             out_shape=[jax.ShapeDtypeStruct(load.shape, jnp.float32)] * 2,
-            in_specs=[vmem] * 4 + [anywhere] * 2 + [vmem] * 2 + [smem] * 2,
+            in_specs=[anywhere] * 8 + [smem] * 2,
             out_specs=[vmem, vmem],
             scratch_shapes=[
+                held(*displacement.shape),
+                held(*load.shape),
+                pltpu.VMEM((points // 128, 128), jnp.int32),
+                pltpu.VMEM((points // 128, 128), jnp.int32),
                 half(size, size),
                 half(size, size),
+                half(6, size),
+                half(6, size),
                 half(3 * size, 16),
                 half(tall, size),
                 half(tall, size),
@@ -842,7 +865,7 @@
                 held(n_macro, 16, 128),
                 held(1, 128),
                 held(total, 1, 128),
-                dma((2,)),
+                dma((8,)),
                 dma((3,)),
                 dma((3,)),
                 dma((n_micro,)),

time: 60.7 us -> 59.4 us (0.979)
  Pallas kernels: 56.5 us -> 55.3 us
    pallas_call x1, Pallas kernels: 56.5 us -> 55.3 us  [shards(): pl.pallas_call(body, out_shape=[jax.ShapeDtypeStruct(load.shape, jnp.floa...]
where the time goes in v5:
time: 59.4 us; the launch traced here: 59.2 us
  Pallas kernels  55.3 us (93%)
  between operations  1.94 us (3%)
  local copies, waits for them, and re-layouts  1.92 us (3%)
    pallas_call x1, Pallas kernels, shards(): pl.pallas_call(body, out_shape=[jax.ShapeDtypeStruct(load.shape, jnp.floa...  55.3 us
    unnamed x4, local copies, waits for them, and re-layouts  1.92 us

profile of v5, /device:TPU:0, one launch (start us, length us, event | category | flops | bytes accessed | tf_op | source)
XLA Modules:
  0.0 59.2 jit_solution(796096122019898372)
XLA Ops:
  1.9 55.3 %newton_step.1 = (f32[3,2,2,256]{3,2,1,0:T(2,128)}, f32[3,2,2,256]{3,2,1,0:T(2,128)}) custom-call(f32[3,2,2,256]{3,2,1,0:T(2,128)} %refs_0_.1, f32[3,2,2,256]{3,2,1,0:T(2,128)} %refs_1_.1, s32[8,128]{1,0:T(8,128)} %bitcast.12, s32[8,128]{1,0:T(8,128)} %bitcast.13, bf16[512,512]{1,0:T(8,128)(2,1)} %bitcast.8, bf16[512,512]{1,0:T(8,128)(2,1)} %bitcast.9, ...), custom_call_target="tpu_custom_call" | custom-call | tf_op jit(solution)/shard_map/newton_step/pallas_call | solution.py:831
  57.2 0.0 copy-start
  57.2 1.3 %copy.16 = f32[3,2,2,256]{3,2,1,0:T(2,128)} copy(f32[3,2,2,256]{3,2,1,0:T(2,128)} %get-tuple-element.4) | data formatting | bytes 24576
  58.6 0.0 copy-done
  58.6 0.6 %copy.17 = f32[3,2,2,256]{3,2,1,0:T(2,128)} copy(f32[3,2,2,256]{3,2,1,0:T(2,128)S(1)} %copy-done) | data formatting | bytes 24576
Async XLA Ops:
  57.2 1.3 %copy-start = (f32[3,2,2,256]{3,2,1,0:T(2,128)S(1)}, f32[3,2,2,256]{3,2,1,0:T(2,128)}, u32[]{:S(2)}) copy-start(f32[3,2,2,256]{3,2,1,0:T(2,128)} %get-tuple-element.5) | copy-start | bytes 36868

commit v6 on v5

--- a/solution.py
+++ b/solution.py
@@ -1,3 +1,6 @@
+import functools
+import itertools
+
 import jax
 import jax.numpy as jnp
 from jax import lax
@@ -46,6 +49,10 @@
     products,
     wide_products,
     spots,
+    load_here,
+    values_here,
+    packed,
+    home,
     near_disp,
     bundle,
     route_out,
@@ -81,8 +88,12 @@
     macro_recv,
     last_send,
     last_recv,
+    seat_send,
+    seat_recv,
+    home_send,
+    home_recv,
 ):
-    count_x, count_y, lanes, n_macro, n_micro = sizes
+    count_x, count_y, lanes, n_macro, n_micro, line = sizes
     wide = count_y + 2
     rows = basis.shape[2]
     points = spots.shape[1]
@@ -95,12 +106,22 @@
     a, b = lax.axis_index("macro"), lax.axis_index("micro")
     me = a * n_micro + b
 
+    def pick(table, index):
+        value = table[0]
+        for at, entry in enumerate(table[1:], 1):
+            value = jnp.where(index == at, entry, value)
+        return value
+
+    level = pick([line.index(at) for at in range(n_macro)], a)
+    seat = pick(line, a)
+    moved_rows = list(line) != list(range(n_macro))
+
     def device(other):
         return (other // n_micro, lax.rem(other, n_micro))
 
-    def inside(dx, dy):
+    def inside(dx, dy, start=None):
         test = None
-        for place, step, count in ((a, dx, n_macro), (b, dy, n_micro)):
+        for place, step, count in ((a if start is None else start, dx, n_macro), (b, dy, n_micro)):
             if step != 0:
                 good = (place > 0) if step < 0 else (place < count - 1)
                 test = good if test is None else jnp.logical_and(test, good)
@@ -197,7 +218,7 @@
 
     for at, (dx, dy) in enumerate(AROUND):
 
-        @pl.when(jnp.logical_not(inside(dx, dy)))
+        @pl.when(jnp.logical_not(inside(dx, dy, level)))
         def _():
             for it in range(ITERS):
                 halo[it, at] = jnp.zeros(halo.shape[2:], jnp.float32)
@@ -216,7 +237,7 @@
     handed += [((1, 1), (count_x - 1, count_y - 1), (0, 0))]
     for at, ((dx, dy), _, _) in enumerate(handed):
 
-        @pl.when(jnp.logical_not(inside(-dx, -dy)))
+        @pl.when(jnp.logical_not(inside(-dx, -dy, level)))
         def _():
             beside[at] = jnp.zeros(beside.shape[1:], jnp.float32)
 
@@ -239,8 +260,46 @@
         def _():
             show(at).start()
 
+    def at_seat(source, target, at):
+        return pltpu.make_async_remote_copy(
+            src_ref=source,
+            dst_ref=target,
+            send_sem=seat_send.at[at],
+            recv_sem=seat_recv.at[at],
+            device_id=(seat, b),
+            device_id_type=MESH,
+        )
+
+    def at_home(at):
+        return pltpu.make_async_remote_copy(
+            src_ref=packed.at[at],
+            dst_ref=home.at[at],
+            send_sem=home_send.at[at],
+            recv_sem=home_recv.at[at],
+            device_id=(level, b),
+            device_id_type=MESH,
+        )
+
+    def when_moved(act, stay):
+        if not moved_rows:
+            stay()
+            return
+
+        @pl.when(seat != a)
+        def _():
+            act()
+
+        @pl.when(seat == a)
+        def _():
+            stay()
+
     for name in ("pre", "stiff", "load"):
         inputs[name].wait()
+
+    def load_stays():
+        load_here[...] = load_ref[...]
+
+    when_moved(at_seat(load_ref, load_here, 0).start if moved_rows else None, load_stays)
 
     def split(exact):
         high = exact.astype(jnp.bfloat16)
@@ -487,42 +546,66 @@
             dst_ref=beside.at[at],
             send_sem=side_send.at[at],
             recv_sem=side_recv.at[at],
-            device_id=(a + dx, b + dy),
+            device_id=(pick(line, a + dx), b + dy),
             device_id_type=MESH,
         )
 
-    for at, ((dx, dy), _, _) in enumerate(handed):
-
-        @pl.when(inside(dx, dy))
+    def values_stay():
+        values_here[...] = values[...]
+
+    def side_test(at, leaves, same):
+        (dx, dy), _, _ = handed[at]
+        test = inside(dx, dy) if leaves else inside(-dx, -dy, level)
+        if dy != 0 or not moved_rows:
+            return None if same else test
+        itself = (pick(line, a + dx) if leaves else level - dx) == a
+        return jnp.logical_and(test, itself if same else jnp.logical_not(itself))
+
+    when_moved(at_seat(values, values_here, 1).start if moved_rows else None, values_stay)
+    for at, (_, place, _) in enumerate(handed):
+
+        @pl.when(side_test(at, True, False))
         def _():
             side_copy(at).start()
+
+        test = side_test(at, True, True)
+        if test is not None:
+
+            @pl.when(test)
+            def _():
+                low = column_at[place] * lanes
+                beside[at] = values[:, low : low + lanes]
 
     def put_column(read, row):
         for v in range(6 + len(PAIRS)):
             elem[v, pl.ds(row, 1)] = read(v)
 
-    for at, (i, j) in enumerate(owned):
-        put_column(
-            lambda v: values[v : v + 1, at * lanes : (at + 1) * lanes], (i + 1) * wide + j + 1
-        )
+    def put_own():
+        for at, (i, j) in enumerate(owned):
+            put_column(
+                lambda v: values_here[v : v + 1, at * lanes : (at + 1) * lanes],
+                (i + 1) * wide + j + 1,
+            )
+
+    when_moved(lambda: None, put_own)
     for at, ((dx, dy), _, (i, j)) in enumerate(handed):
 
-        @pl.when(inside(dx, dy))
+        @pl.when(side_test(at, True, False))
         def _():
             side_copy(at).wait_send()
 
-        @pl.when(inside(-dx, -dy))
+        @pl.when(side_test(at, False, False))
         def _():
-            pltpu.make_async_remote_copy(
-                src_ref=values.at[:, pl.ds(0, lanes)],
-                dst_ref=beside.at[at],
-                send_sem=side_send.at[at],
-                recv_sem=side_recv.at[at],
-                device_id=(a - dx, b - dy),
-                device_id_type=MESH,
-            ).wait_recv()
+            side_copy(at).wait_recv()
 
         put_column(lambda v: beside[at, v : v + 1], i * wide + j)
+
+    def guest():
+        at_seat(load_ref, load_here, 0).wait()
+        at_seat(values, values_here, 1).wait()
+        put_own()
+
+    when_moved(guest, lambda: None)
 
     def near(step, count):
         return {0: list(range(1, count + 1)), -1: [1], 1: [count]}[step]
@@ -542,14 +625,14 @@
             dst_ref=halo.at[it, other],
             send_sem=send_sem.at[it, at],
             recv_sem=recv_sem.at[it, other],
-            device_id=(a + dx, b + dy),
+            device_id=(pick(line, level + dx), b + dy),
             device_id_type=MESH,
         )
 
     def halo_start(it):
         for at, (dx, dy) in enumerate(AROUND):
 
-            @pl.when(inside(dx, dy))
+            @pl.when(inside(dx, dy, level))
             def _():
                 mine = places(at, near)
                 for c in range(3):
@@ -560,7 +643,7 @@
     def halo_finish(it):
         for at, (dx, dy) in enumerate(AROUND):
 
-            @pl.when(inside(dx, dy))
+            @pl.when(inside(dx, dy, level))
             def _():
                 hop(it, at).wait_send()
                 pltpu.make_async_remote_copy(
@@ -568,7 +651,7 @@
                     dst_ref=halo.at[it, at],
                     send_sem=send_sem.at[it, at],
                     recv_sem=recv_sem.at[it, at],
-                    device_id=(a + dx, b + dy),
+                    device_id=(pick(line, level + dx), b + dy),
                     device_id_type=MESH,
                 ).wait_recv()
 
@@ -577,6 +660,25 @@
             for c in range(3):
                 for k, row in enumerate(theirs):
                     basis[it, c, pl.ds(row, 1)] = halo[it, at, pl.ds(c * len(theirs) + k, 1)]
+
+    def keep(it, read):
+        for target, there in ((packed, True), (home, False)) if moved_rows else ((home, None),):
+
+            def put():
+                for c in range(3):
+                    for at, (i, j) in enumerate(owned):
+                        place = (i + 1) * wide + j + 1
+                        target[it, pl.ds(c * len(owned) + at, 1)] = read(c, place)
+                if there:
+                    at_home(it).start()
+
+            if there is None:
+                put()
+            else:
+                pl.when((seat != a) if there else (seat == a))(put)
+
+    def kept(it):
+        keep(it, lambda c, place: basis[it, c, pl.ds(place, 1)])
 
     def force_of(stress, c):
         first, second, third = (stress[VOIGT[c][d]] for d in range(3))
@@ -650,18 +752,20 @@
             + [
                 piece
                 for i in range(count_x)
-                for piece in (load_ref[c, i], jnp.zeros((2, lanes), jnp.float32))
+                for piece in (load_here[c, i], jnp.zeros((2, lanes), jnp.float32))
             ]
             + [jnp.zeros((rows - 1 - wide * (count_x + 1), lanes), jnp.float32)],
             axis=0,
         )
         basis[0, c] = jnp.where(own, padded - force_of(stress, c), zero)
     halo_start(0)
+    kept(0)
     halo_finish(0)
     grown = applied(0)
     for c in range(3):
         basis[1, c] = grown[c]
     halo_start(1)
+    kept(1)
     start = [basis[0, c] for c in range(3)]
     part[...] = stacked([product(start, start), product(grown, grown)])
     copies = gather_start(
@@ -672,6 +776,7 @@
     for c in range(3):
         basis[2, c] = grown[c]
     halo_start(2)
+    kept(2)
     middle[...] = gather_finish(copies, got_micro, n_micro)
     copies = gather_start(
         middle, got_macro, n_macro, a, macro_send, macro_recv, lambda other: (other, b)
@@ -699,6 +804,7 @@
             for c in range(3):
                 basis[it + 1, c] = grown[c]
             halo_start(it + 1)
+            kept(it + 1)
             if it == 2:
                 for k in range(3):
                     moments.append(product(field(k), field(k)))
@@ -707,6 +813,7 @@
                 moments.append(product(field(it), field(it)))
                 moments.append(product(field(it), field(it + 1)))
             halo_finish(it + 1)
+    keep(ITERS, lambda c, place: grown[c][place : place + 1])
     moments.append(product(field(ITERS - 1), field(ITERS - 1)))
     moments.append(product(field(ITERS - 1), grown))
     sums = jnp.sum(stacked(moments), axis=1, keepdims=True)
@@ -767,17 +874,25 @@
                 for k in range(len(left))
             ]
             norm = fresh
+    def landed():
+        for at in range(ITERS + 1):
+            at_home(at).wait()
+
+    when_moved(landed, lambda: None)
+    fields = [home[k] for k in range(ITERS + 1)]
+    u0, w1, w2 = fields[0], fields[1] * scale, fields[2] * (scale * scale)
+    fields[1] = w1 - u0
+    fields[2] = (w2 - w1) - (w1 - u0)
+    moved, rest = None, None
+    for k in range(ITERS + 1):
+        if k < len(done):
+            term = done[k] * fields[k]
+            moved = term if moved is None else moved + term
+        term = left[k] * fields[k]
+        rest = term if rest is None else rest + term
     for c in range(3):
-        fields = [basis[k, c] for k in range(ITERS)] + [grown[c]]
-        moved, rest = None, None
-        for k in range(ITERS + 1):
-            if k < len(done):
-                term = done[k] * fields[k]
-                moved = term if moved is None else moved + term
-            term = left[k] * fields[k]
-            rest = term if rest is None else rest + term
         for i in range(count_x):
-            low = (i + 1) * wide + 1
+            low = c * len(owned) + i * count_y
             inc_ref[c, i] = moved[low : low + count_y]
             res_ref[c, i] = rest[low : low + count_y]
 
@@ -790,7 +905,23 @@
     lax.fori_loop(1, n_micro, sent, 0)
 
 
+def line_of(mesh):
+    places = [tuple(getattr(device, "coords", ())) for device in mesh.devices[:, 0]]
+
+    def cost(order):
+        hops = sum(
+            sum(abs(x - y) for x, y in zip(places[p], places[q]))
+            for p, q in zip(order, order[1:])
+        )
+        return hops, sum(p != at for at, p in enumerate(order)), order
+
+    if len(places) > 6:
+        return list(range(len(places)))
+    return list(min(itertools.permutations(range(len(places))), key=cost))
+
+
 def shards(
+    line,
     displacement,
     load,
     routes,
@@ -812,6 +943,7 @@
     rows = -(-(count_x + 2) * (count_y + 2) // 8) * 8
     side = -(-3 * max(count_x, count_y) // 8) * 8
     total = n_macro * n_micro
+    fields = -(-3 * count_x * count_y // 8) * 8
     sides = count_x + count_y + 1
     vmem = pl.BlockSpec(memory_space=pltpu.VMEM)
     smem = pl.BlockSpec(memory_space=pltpu.SMEM)
@@ -825,7 +957,7 @@
         return pltpu.VMEM(shape, jnp.bfloat16)
 
     def body(*refs):
-        newton_kernel((count_x, count_y, lanes, n_macro, n_micro), *refs)
+        newton_kernel((count_x, count_y, lanes, n_macro, n_micro, line), *refs)
 
     return tuple(
         pl.pallas_call(
@@ -847,6 +979,10 @@
                 half(tall, size),
                 held(tall, size),
                 half(n_micro * slots, points),
+                held(*load.shape),
+                held(tall, points),
+                held(ITERS + 1, fields, lanes),
+                held(ITERS + 1, fields, lanes),
                 held(3, *displacement.shape),
                 held(8, points),
                 held(n_micro, 8, slots),
@@ -882,6 +1018,10 @@
                 dma((n_macro - 1,)),
                 dma((total,)),
                 dma((total,)),
+                dma((2,)),
+                dma((2,)),
+                dma((ITERS + 1,)),
+                dma((ITERS + 1,)),
             ],
             compiler_params=pltpu.CompilerParams(collective_id=0, has_side_effects=True),
             name="newton_step",
@@ -914,4 +1054,4 @@
         P("micro"),
     )
     out_specs = (P(None, "macro", "micro", None), P(None, "macro", "micro", None))
-    return jax.shard_map(shards, mesh=mesh, in_specs=in_specs, out_specs=out_specs, check_vma=False)
+    return jax.shard_map(functools.partial(shards, line_of(mesh)), mesh=mesh, in_specs=in_specs, out_specs=out_specs, check_vma=False)

time: 59.4 us -> 59.5 us (level)
  no operation moved by 1% of the time
where the time goes in v6:
time: 59.5 us; the launch traced here: 59.3 us
  Pallas kernels  55.4 us (93%)
  between operations  1.94 us (3%)
  local copies, waits for them, and re-layouts  1.92 us (3%)
    pallas_call x1, Pallas kernels, shards(): pl.pallas_call(body, out_shape=[jax.ShapeDtypeStruct(load.shape, jnp.floa...  55.4 us
    unnamed x4, local copies, waits for them, and re-layouts  1.92 us

profile of v6, /device:TPU:0, one launch (start us, length us, event | category | flops | bytes accessed | tf_op | source)
XLA Modules:
  0.0 59.3 jit_solution(9064721417709021694)
XLA Ops:
  1.9 55.4 %newton_step.1 = (f32[3,2,2,256]{3,2,1,0:T(2,128)}, f32[3,2,2,256]{3,2,1,0:T(2,128)}) custom-call(f32[3,2,2,256]{3,2,1,0:T(2,128)} %refs_0_.1, f32[3,2,2,256]{3,2,1,0:T(2,128)} %refs_1_.1, s32[8,128]{1,0:T(8,128)} %bitcast.12, s32[8,128]{1,0:T(8,128)} %bitcast.13, bf16[512,512]{1,0:T(8,128)(2,1)} %bitcast.8, bf16[512,512]{1,0:T(8,128)(2,1)} %bitcast.9, ...), custom_call_target="tpu_custom_call" | custom-call | tf_op jit(solution)/shard_map/newton_step/pallas_call | solution.py:963
  57.4 0.0 copy-start
  57.4 1.3 %copy.16 = f32[3,2,2,256]{3,2,1,0:T(2,128)} copy(f32[3,2,2,256]{3,2,1,0:T(2,128)} %get-tuple-element.4) | data formatting | bytes 24576
  58.7 0.0 copy-done
  58.7 0.6 %copy.17 = f32[3,2,2,256]{3,2,1,0:T(2,128)} copy(f32[3,2,2,256]{3,2,1,0:T(2,128)S(1)} %copy-done) | data formatting | bytes 24576
Async XLA Ops:
  57.4 1.3 %copy-start = (f32[3,2,2,256]{3,2,1,0:T(2,128)S(1)}, f32[3,2,2,256]{3,2,1,0:T(2,128)}, u32[]{:S(2)}) copy-start(f32[3,2,2,256]{3,2,1,0:T(2,128)} %get-tuple-element.5) | copy-start | bytes 36868

commit v7 on v5

--- a/solution.py
+++ b/solution.py
@@ -139,7 +139,28 @@
         inputs[name] = pltpu.make_async_copy(source, target, input_sem.at[at])
         inputs[name].start()
 
-    for name in ("routes", "force", "couple", "counts", "disp"):
+    inputs["disp"].wait()
+    after = ((1, 0), (0, 1), (1, 1))
+    pl.semaphore_wait(barrier, greeted)
+
+    def show(at):
+        dx, dy = after[at]
+        return pltpu.make_async_remote_copy(
+            src_ref=disp_ref,
+            dst_ref=near_disp.at[at],
+            send_sem=disp_send.at[at],
+            recv_sem=disp_recv.at[at],
+            device_id=(a - dx, b - dy),
+            device_id_type=MESH,
+        )
+
+    for at, (dx, dy) in enumerate(after):
+
+        @pl.when(inside(-dx, -dy))
+        def _():
+            show(at).start()
+
+    for name in ("routes", "force", "couple", "counts"):
         inputs[name].wait()
     force = force_ref[...].astype(jnp.float32)
     force = jnp.concatenate([force, jnp.zeros((2, size), jnp.float32)], axis=0)
@@ -202,7 +223,6 @@
             for it in range(ITERS):
                 halo[it, at] = jnp.zeros(halo.shape[2:], jnp.float32)
 
-    after = ((1, 0), (0, 1), (1, 1))
     for at, (dx, dy) in enumerate(after):
 
         @pl.when(jnp.logical_not(inside(dx, dy)))
@@ -219,25 +239,6 @@
         @pl.when(jnp.logical_not(inside(-dx, -dy)))
         def _():
             beside[at] = jnp.zeros(beside.shape[1:], jnp.float32)
-
-    pl.semaphore_wait(barrier, greeted)
-
-    def show(at):
-        dx, dy = after[at]
-        return pltpu.make_async_remote_copy(
-            src_ref=disp_ref,
-            dst_ref=near_disp.at[at],
-            send_sem=disp_send.at[at],
-            recv_sem=disp_recv.at[at],
-            device_id=(a - dx, b - dy),
-            device_id_type=MESH,
-        )
-
-    for at, (dx, dy) in enumerate(after):
-
-        @pl.when(inside(-dx, -dy))
-        def _():
-            show(at).start()
 
     for name in ("pre", "stiff", "load"):
         inputs[name].wait()

time: 59.4 us -> 59.2 us (level)
  no operation moved by 1% of the time
where the time goes in v7:
time: 59.2 us; the launch traced here: 59 us
  Pallas kernels  55.2 us (93%)
  between operations  1.94 us (3%)
  local copies, waits for them, and re-layouts  1.92 us (3%)
    pallas_call x1, Pallas kernels, shards(): pl.pallas_call(body, out_shape=[jax.ShapeDtypeStruct(load.shape, jnp.floa...  55.2 us
    unnamed x4, local copies, waits for them, and re-layouts  1.92 us

profile of v7, /device:TPU:0, one launch (start us, length us, event | category | flops | bytes accessed | tf_op | source)
XLA Modules:
  0.0 59.0 jit_solution(2012380765803606525)
XLA Ops:
  1.9 55.2 %newton_step.1 = (f32[3,2,2,256]{3,2,1,0:T(2,128)}, f32[3,2,2,256]{3,2,1,0:T(2,128)}) custom-call(f32[3,2,2,256]{3,2,1,0:T(2,128)} %refs_0_.1, f32[3,2,2,256]{3,2,1,0:T(2,128)} %refs_1_.1, s32[8,128]{1,0:T(8,128)} %bitcast.12, s32[8,128]{1,0:T(8,128)} %bitcast.13, bf16[512,512]{1,0:T(8,128)(2,1)} %bitcast.8, bf16[512,512]{1,0:T(8,128)(2,1)} %bitcast.9, ...), custom_call_target="tpu_custom_call" | custom-call | tf_op jit(solution)/shard_map/newton_step/pallas_call | solution.py:832
  57.1 0.0 copy-start
  57.1 1.3 %copy.16 = f32[3,2,2,256]{3,2,1,0:T(2,128)} copy(f32[3,2,2,256]{3,2,1,0:T(2,128)} %get-tuple-element.4) | data formatting | bytes 24576
  58.4 0.0 copy-done
  58.4 0.6 %copy.17 = f32[3,2,2,256]{3,2,1,0:T(2,128)} copy(f32[3,2,2,256]{3,2,1,0:T(2,128)S(1)} %copy-done) | data formatting | bytes 24576
Async XLA Ops:
  57.1 1.3 %copy-start = (f32[3,2,2,256]{3,2,1,0:T(2,128)S(1)}, f32[3,2,2,256]{3,2,1,0:T(2,128)}, u32[]{:S(2)}) copy-start(f32[3,2,2,256]{3,2,1,0:T(2,128)} %get-tuple-element.5) | copy-start | bytes 36868

commit v8 on v7

--- a/solution.py
+++ b/solution.py
@@ -17,6 +17,17 @@
 PAIR_AT = {pair: at for at, pair in enumerate(PAIRS)}
 AROUND = tuple((dx, dy) for dx in (-1, 0, 1) for dy in (-1, 0, 1) if (dx, dy) != (0, 0))
 MESH = pl.DeviceIdType.MESH
+
+
+def strips_of(count_x, count_y):
+    strips = []
+    for dx, dy in AROUND:
+        across = range(count_x if dx >= 0 else 1)
+        if dy >= 0:
+            strips.append(((dx, dy), 0, len(across) * count_y))
+        else:
+            strips += [((dx, dy), i * count_y, 1) for i in across]
+    return strips
 
 
 def newton_kernel(
@@ -46,6 +57,10 @@
     products,
     wide_products,
     spots,
+    near_load,
+    near_stress,
+    outer,
+    loads,
     near_disp,
     bundle,
     route_out,
@@ -81,6 +96,10 @@
     macro_recv,
     last_send,
     last_recv,
+    load_send,
+    load_recv,
+    strip_send,
+    strip_recv,
 ):
     count_x, count_y, lanes, n_macro, n_micro = sizes
     wide = count_y + 2
@@ -160,6 +179,44 @@
         def _():
             show(at).start()
 
+    inputs["load"].wait()
+
+    def load_copy(at):
+        dx, dy = AROUND[at]
+        other = len(AROUND) - 1 - at
+        return pltpu.make_async_remote_copy(
+            src_ref=load_ref,
+            dst_ref=near_load.at[other],
+            send_sem=load_send.at[at],
+            recv_sem=load_recv.at[other],
+            device_id=(a + dx, b + dy),
+            device_id_type=MESH,
+        )
+
+    def load_arrival(at):
+        dx, dy = AROUND[at]
+        return pltpu.make_async_remote_copy(
+            src_ref=load_ref,
+            dst_ref=near_load.at[at],
+            send_sem=load_send.at[at],
+            recv_sem=load_recv.at[at],
+            device_id=(a + dx, b + dy),
+            device_id_type=MESH,
+        )
+
+    for at, (dx, dy) in enumerate(AROUND):
+
+        @pl.when(inside(dx, dy))
+        def _():
+            load_copy(at).start()
+
+        @pl.when(jnp.logical_not(inside(dx, dy)))
+        def _():
+            near_load[at] = jnp.zeros(near_load.shape[1:], jnp.float32)
+            near_stress[at] = jnp.zeros(near_stress.shape[1:], jnp.float32)
+
+    outer[...] = jnp.zeros(outer.shape, jnp.float32)
+    loads[...] = jnp.zeros(loads.shape, jnp.float32)
     for name in ("routes", "force", "couple", "counts"):
         inputs[name].wait()
     force = force_ref[...].astype(jnp.float32)
@@ -220,7 +277,7 @@
 
         @pl.when(jnp.logical_not(inside(dx, dy)))
         def _():
-            for it in range(ITERS):
+            for it in range(1, ITERS):
                 halo[it, at] = jnp.zeros(halo.shape[2:], jnp.float32)
 
     for at, (dx, dy) in enumerate(after):
@@ -240,7 +297,7 @@
         def _():
             beside[at] = jnp.zeros(beside.shape[1:], jnp.float32)
 
-    for name in ("pre", "stiff", "load"):
+    for name in ("pre", "stiff"):
         inputs[name].wait()
 
     def split(exact):
@@ -484,7 +541,7 @@
         (dx, dy), place, _ = handed[at]
         low = column_at[place] * lanes
         return pltpu.make_async_remote_copy(
-            src_ref=values.at[:, pl.ds(low, lanes)],
+            src_ref=values.at[pl.ds(8, tall - 8), pl.ds(low, lanes)],
             dst_ref=beside.at[at],
             send_sem=side_send.at[at],
             recv_sem=side_recv.at[at],
@@ -492,20 +549,91 @@
             device_id_type=MESH,
         )
 
+    strips = strips_of(count_x, count_y)
+
+    def strip_copy(at):
+        (dx, dy), first, count = strips[at]
+        columns = pl.ds(first * lanes, count * lanes)
+        return pltpu.make_async_remote_copy(
+            src_ref=values.at[pl.ds(0, 8), columns],
+            dst_ref=near_stress.at[len(AROUND) - 1 - AROUND.index((dx, dy)), pl.ds(0, 8), columns],
+            send_sem=strip_send.at[at],
+            recv_sem=strip_recv.at[at],
+            device_id=(a + dx, b + dy),
+            device_id_type=MESH,
+        )
+
+    for at, ((dx, dy), _, _) in enumerate(strips):
+
+        @pl.when(inside(dx, dy))
+        def _():
+            strip_copy(at).start()
+
     for at, ((dx, dy), _, _) in enumerate(handed):
 
         @pl.when(inside(dx, dy))
         def _():
             side_copy(at).start()
 
-    def put_column(read, row):
-        for v in range(6 + len(PAIRS)):
+    for at, (dx, dy) in enumerate(AROUND):
+
+        @pl.when(inside(dx, dy))
+        def _():
+            load_copy(at).wait_send()
+            load_arrival(at).wait_recv()
+
+    def span(step, count, below):
+        if step == 0:
+            return [(k, k) for k in range(count)]
+        if step > 0:
+            return [(count, 0)]
+        return [(k - below, count + k - below) for k in range(below)]
+
+    for c in range(3):
+        for i in range(count_x):
+            loads[c, pl.ds((i + 1) * wide + 1, count_y)] = load_ref[c, i]
+        for at, (dx, dy) in enumerate(AROUND):
+            for i, from_i in span(dx, count_x, 1):
+                for j, from_j in span(dy, count_y, 1):
+                    loads[c, pl.ds((i + 1) * wide + j + 1, 1)] = near_load[
+                        at, c, from_i, from_j : from_j + 1
+                    ]
+
+    broad = count_y + 3
+
+    def put_stress(read, i, j):
+        for v in range(6):
+            outer[v, pl.ds((i + 2) * broad + j + 2, 1)] = read(v)
+
+    def put_tangent(read, row, first=6):
+        for v in range(first, 6 + len(PAIRS)):
             elem[v, pl.ds(row, 1)] = read(v)
 
     for at, (i, j) in enumerate(owned):
-        put_column(
+        put_stress(lambda v: values[v : v + 1, at * lanes : (at + 1) * lanes], i, j)
+        put_tangent(
             lambda v: values[v : v + 1, at * lanes : (at + 1) * lanes], (i + 1) * wide + j + 1
         )
+    for at, ((dx, dy), _, _) in enumerate(strips):
+
+        @pl.when(inside(dx, dy))
+        def _():
+            strip_copy(at).wait_send()
+
+        @pl.when(inside(-dx, -dy))
+        def _():
+            strip_copy(at).wait_recv()
+
+    for at, (dx, dy) in enumerate(AROUND):
+        for i, from_i in span(dx, count_x, 2):
+            for j, from_j in span(dy, count_y, 2):
+                low = column_at[from_i, from_j] * lanes
+                put_stress(lambda v: near_stress[at, v : v + 1, low : low + lanes], i, j)
+    for at, ((dx, dy), place, (i, j)) in enumerate(handed):
+        low = column_at[place] * lanes
+        source = AROUND.index((-dx, -dy))
+        for v in (6, 7):
+            elem[v, pl.ds(i * wide + j, 1)] = near_stress[source, v : v + 1, low : low + lanes]
     for at, ((dx, dy), _, (i, j)) in enumerate(handed):
 
         @pl.when(inside(dx, dy))
@@ -514,16 +642,9 @@
 
         @pl.when(inside(-dx, -dy))
         def _():
-            pltpu.make_async_remote_copy(
-                src_ref=values.at[:, pl.ds(0, lanes)],
-                dst_ref=beside.at[at],
-                send_sem=side_send.at[at],
-                recv_sem=side_recv.at[at],
-                device_id=(a - dx, b - dy),
-                device_id_type=MESH,
-            ).wait_recv()
-
-        put_column(lambda v: beside[at, v : v + 1], i * wide + j)
+            side_copy(at).wait_recv()
+
+        put_tangent(lambda v: beside[at, v - 8 : v - 7], i * wide + j, 8)
 
     def near(step, count):
         return {0: list(range(1, count + 1)), -1: [1], 1: [count]}[step]
@@ -579,7 +700,7 @@
                 for k, row in enumerate(theirs):
                     basis[it, c, pl.ds(row, 1)] = halo[it, at, pl.ds(c * len(theirs) + k, 1)]
 
-    def force_of(stress, c):
+    def force_of(stress, c, down=down):
         first, second, third = (stress[VOIGT[c][d]] for d in range(3))
         first = first + down(first, 2)
         second = second + down(second, 2)
@@ -643,22 +764,31 @@
             total = total + dst[at]
         return total
 
-    stress = [elem[i] for i in range(6)]
-    zero = jnp.zeros((rows, lanes), jnp.float32)
+    broad_lane = lax.broadcasted_iota(jnp.int32, outer.shape[1:], 1)
+
+    def back(value, axis):
+        if axis == 2:
+            return jnp.where(broad_lane == 0, 0.0, pltpu.roll(value, 1, 1))
+        return pltpu.roll(value, broad if axis == 0 else 1, 0)
+
+    row_x, row_y = row_at // wide, row_at % wide
+    real = jnp.logical_and(
+        jnp.logical_and(
+            row_x >= jnp.where(a > 0, 0, 1),
+            row_x <= jnp.where(a < n_macro - 1, count_x + 1, count_x),
+        ),
+        jnp.logical_and(
+            row_y >= jnp.where(b > 0, 0, 1),
+            row_y <= jnp.where(b < n_micro - 1, count_y + 1, count_y),
+        ),
+    )
+    stress = [outer[v] for v in range(6)]
     for c in range(3):
-        padded = jnp.concatenate(
-            [jnp.zeros((wide + 1, lanes), jnp.float32)]
-            + [
-                piece
-                for i in range(count_x)
-                for piece in (load_ref[c, i], jnp.zeros((2, lanes), jnp.float32))
-            ]
-            + [jnp.zeros((rows - 1 - wide * (count_x + 1), lanes), jnp.float32)],
-            axis=0,
-        )
-        basis[0, c] = jnp.where(own, padded - force_of(stress, c), zero)
-    halo_start(0)
-    halo_finish(0)
+        pushed = force_of(stress, c, back)
+        for i in range(count_x + 2):
+            low = (i + 1) * broad + 1
+            basis[0, c, pl.ds(i * wide, wide)] = pushed[low : low + wide]
+        basis[0, c] = jnp.where(real, loads[c] - basis[0, c], 0.0)
     grown = applied(0)
     for c in range(3):
         basis[1, c] = grown[c]
@@ -814,6 +944,8 @@
     side = -(-3 * max(count_x, count_y) // 8) * 8
     total = n_macro * n_micro
     sides = count_x + count_y + 1
+    outer_rows = -(-(count_x + 3) * (count_y + 3) // 8) * 8
+    strips = len(strips_of(count_x, count_y))
     vmem = pl.BlockSpec(memory_space=pltpu.VMEM)
     smem = pl.BlockSpec(memory_space=pltpu.SMEM)
     anywhere = pl.BlockSpec(memory_space=pl.ANY)
@@ -848,6 +980,10 @@
                 half(tall, size),
                 held(tall, size),
                 half(n_micro * slots, points),
+                held(len(AROUND), *load.shape),
+                held(len(AROUND), 8, points),
+                held(6, outer_rows, lanes),
+                held(3, rows, lanes),
                 held(3, *displacement.shape),
                 held(8, points),
                 held(n_micro, 8, slots),
@@ -855,7 +991,7 @@
                 held(n_micro, tall, slots),
                 held(n_micro, tall, slots),
                 held(tall, points),
-                held(sides, tall, lanes),
+                held(sides, tall - 8, lanes),
                 held(6 + len(PAIRS), rows, lanes),
                 held(ITERS, 3, rows, lanes),
                 held(ITERS, len(AROUND), side, lanes),
@@ -883,6 +1019,10 @@
                 dma((n_macro - 1,)),
                 dma((total,)),
                 dma((total,)),
+                dma((len(AROUND),)),
+                dma((len(AROUND),)),
+                dma((strips,)),
+                dma((strips,)),
             ],
             compiler_params=pltpu.CompilerParams(collective_id=0, has_side_effects=True),
             name="newton_step",

time: 59.2 us -> 58 us (0.980)
  Pallas kernels: 55.2 us -> 53.9 us
    pallas_call x1, Pallas kernels: 55.2 us -> 53.9 us  [shards(): pl.pallas_call(body, out_shape=[jax.ShapeDtypeStruct(load.shape, jnp.floa...]
where the time goes in v8:
time: 58 us; the launch traced here: 57.8 us
  Pallas kernels  53.9 us (93%)
  between operations  1.94 us (3%)
  local copies, waits for them, and re-layouts  1.92 us (3%)
    pallas_call x1, Pallas kernels, shards(): pl.pallas_call(body, out_shape=[jax.ShapeDtypeStruct(load.shape, jnp.floa...  53.9 us
    unnamed x4, local copies, waits for them, and re-layouts  1.92 us

profile of v8, /device:TPU:0, one launch (start us, length us, event | category | flops | bytes accessed | tf_op | source)
XLA Modules:
  0.0 57.8 jit_solution(2204674653136858132)
XLA Ops:
  1.9 53.9 %newton_step.1 = (f32[3,2,2,256]{3,2,1,0:T(2,128)}, f32[3,2,2,256]{3,2,1,0:T(2,128)}) custom-call(f32[3,2,2,256]{3,2,1,0:T(2,128)} %refs_0_.1, f32[3,2,2,256]{3,2,1,0:T(2,128)} %refs_1_.1, s32[8,128]{1,0:T(8,128)} %bitcast.12, s32[8,128]{1,0:T(8,128)} %bitcast.13, bf16[512,512]{1,0:T(8,128)(2,1)} %bitcast.8, bf16[512,512]{1,0:T(8,128)(2,1)} %bitcast.9, ...), custom_call_target="tpu_custom_call" | custom-call | tf_op jit(solution)/shard_map/newton_step/pallas_call | solution.py:964
  55.8 0.0 copy-start
  55.8 1.3 %copy.16 = f32[3,2,2,256]{3,2,1,0:T(2,128)} copy(f32[3,2,2,256]{3,2,1,0:T(2,128)} %get-tuple-element.4) | data formatting | bytes 24576
  57.2 0.0 copy-done
  57.2 0.6 %copy.17 = f32[3,2,2,256]{3,2,1,0:T(2,128)} copy(f32[3,2,2,256]{3,2,1,0:T(2,128)S(1)} %copy-done) | data formatting | bytes 24576
Async XLA Ops:
  55.8 1.3 %copy-start = (f32[3,2,2,256]{3,2,1,0:T(2,128)S(1)}, f32[3,2,2,256]{3,2,1,0:T(2,128)}, u32[]{:S(2)}) copy-start(f32[3,2,2,256]{3,2,1,0:T(2,128)} %get-tuple-element.5) | copy-start | bytes 36868

commit v9 on v8

--- a/solution.py
+++ b/solution.py
@@ -90,16 +90,8 @@
     side_recv,
     send_sem,
     recv_sem,
-    micro_send,
-    micro_recv,
-    macro_send,
-    macro_recv,
-    last_send,
-    last_recv,
-    load_send,
-    load_recv,
-    strip_send,
-    strip_recv,
+    sum_send,
+    sum_recv,
 ):
     count_x, count_y, lanes, n_macro, n_micro = sizes
     wide = count_y + 2
@@ -187,8 +179,8 @@
         return pltpu.make_async_remote_copy(
             src_ref=load_ref,
             dst_ref=near_load.at[other],
-            send_sem=load_send.at[at],
-            recv_sem=load_recv.at[other],
+            send_sem=send_sem.at[0, at],
+            recv_sem=recv_sem.at[0, other],
             device_id=(a + dx, b + dy),
             device_id_type=MESH,
         )
@@ -198,8 +190,8 @@
         return pltpu.make_async_remote_copy(
             src_ref=load_ref,
             dst_ref=near_load.at[at],
-            send_sem=load_send.at[at],
-            recv_sem=load_recv.at[at],
+            send_sem=send_sem.at[0, at],
+            recv_sem=recv_sem.at[0, at],
             device_id=(a + dx, b + dy),
             device_id_type=MESH,
         )
@@ -394,7 +386,7 @@
         return pltpu.make_async_remote_copy(
             src_ref=route_out.at[other],
             dst_ref=route_in.at[mine],
-            send_sem=route_send.at[other],
+            send_sem=route_send.at[0],
             recv_sem=route_recv.at[mine],
             device_id=(a, other),
             device_id_type=MESH,
@@ -432,7 +424,7 @@
     lax.fori_loop(0, pairs, hand_out, 0)
 
 
-    lame_first, lame_shear = first_ref[0], shear_ref[0]
+    lame_first, lame_shear = first_ref[...], shear_ref[...]
     tall_at = lax.broadcasted_iota(jnp.int32, (tall, 2 * slots), 0)
     on_trace = jnp.where(tall_at < 3, lame_first, 0.0)
     on_strain = jnp.where(tall_at < 3, 2.0 * lame_shear, jnp.where(tall_at < 6, lame_shear, 0.0))
@@ -450,7 +442,7 @@
         return pltpu.make_async_remote_copy(
             src_ref=back_out.at[other],
             dst_ref=back_in.at[mine],
-            send_sem=back_send.at[other],
+            send_sem=back_send.at[0],
             recv_sem=back_recv.at[mine],
             device_id=(a, other),
             device_id_type=MESH,
@@ -543,8 +535,8 @@
         return pltpu.make_async_remote_copy(
             src_ref=values.at[pl.ds(8, tall - 8), pl.ds(low, lanes)],
             dst_ref=beside.at[at],
-            send_sem=side_send.at[at],
-            recv_sem=side_recv.at[at],
+            send_sem=side_send.at[after.index((dx, dy))],
+            recv_sem=side_recv.at[after.index((dx, dy))],
             device_id=(a + dx, b + dy),
             device_id_type=MESH,
         )
@@ -554,26 +546,30 @@
     def strip_copy(at):
         (dx, dy), first, count = strips[at]
         columns = pl.ds(first * lanes, count * lanes)
+        way = AROUND.index((dx, dy))
+        other = len(AROUND) - 1 - way
         return pltpu.make_async_remote_copy(
             src_ref=values.at[pl.ds(0, 8), columns],
-            dst_ref=near_stress.at[len(AROUND) - 1 - AROUND.index((dx, dy)), pl.ds(0, 8), columns],
-            send_sem=strip_send.at[at],
-            recv_sem=strip_recv.at[at],
+            dst_ref=near_stress.at[other, pl.ds(0, 8), columns],
+            send_sem=send_sem.at[1, way],
+            recv_sem=recv_sem.at[1, other],
             device_id=(a + dx, b + dy),
             device_id_type=MESH,
         )
 
-    for at, ((dx, dy), _, _) in enumerate(strips):
-
-        @pl.when(inside(dx, dy))
-        def _():
-            strip_copy(at).start()
-
-    for at, ((dx, dy), _, _) in enumerate(handed):
-
-        @pl.when(inside(dx, dy))
-        def _():
-            side_copy(at).start()
+    def strips_moved(way, sent):
+        dx, dy = AROUND[way]
+        offset = (dx, dy) if sent else (-dx, -dy)
+        count = sum(count for place, _, count in strips if place == offset)
+        columns = near_stress.at[way, pl.ds(0, 8), pl.ds(0, count * lanes)]
+        return pltpu.make_async_remote_copy(
+            src_ref=columns,
+            dst_ref=columns,
+            send_sem=send_sem.at[1, way],
+            recv_sem=recv_sem.at[1, way],
+            device_id=(a + dx, b + dy),
+            device_id_type=MESH,
+        )
 
     for at, (dx, dy) in enumerate(AROUND):
 
@@ -581,6 +577,18 @@
         def _():
             load_copy(at).wait_send()
             load_arrival(at).wait_recv()
+
+    for at, ((dx, dy), _, _) in enumerate(strips):
+
+        @pl.when(inside(dx, dy))
+        def _():
+            strip_copy(at).start()
+
+    for at, ((dx, dy), _, _) in enumerate(handed):
+
+        @pl.when(inside(dx, dy))
+        def _():
+            side_copy(at).start()
 
     def span(step, count, below):
         if step == 0:
@@ -614,15 +622,12 @@
         put_tangent(
             lambda v: values[v : v + 1, at * lanes : (at + 1) * lanes], (i + 1) * wide + j + 1
         )
-    for at, ((dx, dy), _, _) in enumerate(strips):
+    for at, (dx, dy) in enumerate(AROUND):
 
         @pl.when(inside(dx, dy))
         def _():
-            strip_copy(at).wait_send()
-
-        @pl.when(inside(-dx, -dy))
-        def _():
-            strip_copy(at).wait_recv()
+            strips_moved(at, True).wait_send()
+            strips_moved(at, False).wait_recv()
 
     for at, (dx, dy) in enumerate(AROUND):
         for i, from_i in span(dx, count_x, 2):
@@ -634,18 +639,6 @@
         source = AROUND.index((-dx, -dy))
         for v in (6, 7):
             elem[v, pl.ds(i * wide + j, 1)] = near_stress[source, v : v + 1, low : low + lanes]
-    for at, ((dx, dy), _, (i, j)) in enumerate(handed):
-
-        @pl.when(inside(dx, dy))
-        def _():
-            side_copy(at).wait_send()
-
-        @pl.when(inside(-dx, -dy))
-        def _():
-            side_copy(at).wait_recv()
-
-        put_tangent(lambda v: beside[at, v - 8 : v - 7], i * wide + j, 8)
-
     def near(step, count):
         return {0: list(range(1, count + 1)), -1: [1], 1: [count]}[step]
 
@@ -662,8 +655,8 @@
         return pltpu.make_async_remote_copy(
             src_ref=send_halo.at[it, at],
             dst_ref=halo.at[it, other],
-            send_sem=send_sem.at[it, at],
-            recv_sem=recv_sem.at[it, other],
+            send_sem=send_sem.at[(it - 1) % 2, at],
+            recv_sem=recv_sem.at[(it - 1) % 2, other],
             device_id=(a + dx, b + dy),
             device_id_type=MESH,
         )
@@ -688,8 +681,8 @@
                 pltpu.make_async_remote_copy(
                     src_ref=send_halo.at[it, at],
                     dst_ref=halo.at[it, at],
-                    send_sem=send_sem.at[it, at],
-                    recv_sem=recv_sem.at[it, at],
+                    send_sem=send_sem.at[(it - 1) % 2, at],
+                    recv_sem=recv_sem.at[(it - 1) % 2, at],
                     device_id=(a + dx, b + dy),
                     device_id_type=MESH,
                 ).wait_recv()
@@ -734,35 +727,43 @@
         return value
 
     def stacked(pieces):
-        tile_row = lax.broadcasted_iota(jnp.int32, (16, 128), 0)
-        value = jnp.zeros((16, 128), jnp.float32)
+        high = -(-len(pieces) // 8) * 8
+        tile_row = lax.broadcasted_iota(jnp.int32, (high, 128), 0)
+        value = jnp.zeros((high, 128), jnp.float32)
         for at, piece in enumerate(pieces):
             value = jnp.where(tile_row == at, piece, value)
         return value
 
-    def gather_start(src, dst, count, mine, send, recv, device):
-        copies = []
-        for step in range(1, count):
-            copy = pltpu.make_async_remote_copy(
+    def gather_start(at, src, dst, count, mine, device):
+        def send(step):
+            pltpu.make_async_remote_copy(
                 src_ref=src,
                 dst_ref=dst.at[mine],
-                send_sem=send.at[step - 1],
-                recv_sem=recv.at[step - 1],
+                send_sem=sum_send.at[at],
+                recv_sem=sum_recv.at[at],
                 device_id=device(lax.rem(mine + step, count)),
                 device_id_type=MESH,
-            )
-            copy.start()
-            copies.append(copy)
+            ).start()
+
+        every(count, send)
         dst[mine] = src[...]
-        return copies
-
-    def gather_finish(copies, dst, count):
-        for copy in copies:
-            copy.wait()
-        total = dst[0]
-        for at in range(1, count):
-            total = total + dst[at]
-        return total
+
+    def gather_finish(at, dst, count, device, mine):
+        others = dst.at[pl.ds(0, count - 1)]
+        pltpu.make_async_remote_copy(
+            src_ref=others,
+            dst_ref=others,
+            send_sem=sum_send.at[at],
+            recv_sem=sum_recv.at[at],
+            device_id=device(lax.rem(mine + 1, count)),
+            device_id_type=MESH,
+        ).wait()
+
+    def along_micro(other):
+        return (a, other)
+
+    def along_macro(other):
+        return (other, b)
 
     broad_lane = lax.broadcasted_iota(jnp.int32, outer.shape[1:], 1)
 
@@ -789,26 +790,47 @@
             low = (i + 1) * broad + 1
             basis[0, c, pl.ds(i * wide, wide)] = pushed[low : low + wide]
         basis[0, c] = jnp.where(real, loads[c] - basis[0, c], 0.0)
+    for way, (dx, dy) in enumerate(after):
+        mine = [at for at, (offset, _, _) in enumerate(handed) if offset == (dx, dy)]
+        landed = beside.at[pl.ds(mine[0], len(mine))]
+        moved = pltpu.make_async_remote_copy(
+            src_ref=landed,
+            dst_ref=landed,
+            send_sem=side_send.at[way],
+            recv_sem=side_recv.at[way],
+            device_id=(a + dx, b + dy),
+            device_id_type=MESH,
+        )
+
+        @pl.when(inside(dx, dy))
+        def _():
+            moved.wait_send()
+
+        @pl.when(inside(-dx, -dy))
+        def _():
+            moved.wait_recv()
+
+    for at, (_, _, (i, j)) in enumerate(handed):
+        put_tangent(lambda v: beside[at, v - 8 : v - 7], i * wide + j, 8)
+
     grown = applied(0)
     for c in range(3):
         basis[1, c] = grown[c]
     halo_start(1)
     start = [basis[0, c] for c in range(3)]
     part[...] = stacked([product(start, start), product(grown, grown)])
-    copies = gather_start(
-        part, got_micro, n_micro, b, micro_send, micro_recv, lambda other: (a, other)
-    )
+    gather_start(0, part, got_micro, n_micro, b, along_micro)
     halo_finish(1)
     grown = applied(1)
     for c in range(3):
         basis[2, c] = grown[c]
     halo_start(2)
-    middle[...] = gather_finish(copies, got_micro, n_micro)
-    copies = gather_start(
-        middle, got_macro, n_macro, a, macro_send, macro_recv, lambda other: (other, b)
-    )
+    gather_finish(0, got_micro, n_micro, along_micro, b)
+    middle[...] = jnp.sum(got_micro[...], axis=0)
+    gather_start(1, middle, got_macro, n_macro, a, along_macro)
     halo_finish(2)
-    totals = jnp.sum(gather_finish(copies, got_macro, n_macro), axis=1, keepdims=True)
+    gather_finish(1, got_macro, n_macro, along_macro, a)
+    totals = jnp.sum(jnp.sum(got_macro[...], axis=0), axis=1, keepdims=True)
     shift = jnp.sqrt(totals[1:2] / totals[0:1])
     scale = 1.0 / shift
     for c in range(3):
@@ -846,19 +868,8 @@
     )
     last_part[...] = jnp.sum(jnp.where(diagonal, sums, 0.0), axis=0, keepdims=True)
 
-    def last_copy(step, other):
-        return pltpu.make_async_remote_copy(
-            src_ref=last_part,
-            dst_ref=last_all.at[me],
-            send_sem=last_send.at[step],
-            recv_sem=last_recv.at[step],
-            device_id=device(other),
-            device_id_type=MESH,
-        )
-
-    every(total, lambda step: last_copy(step, lax.rem(me + step, total)).start())
-    last_all[me] = last_part[...]
-    every(total, lambda step: last_copy(step, lax.rem(me + step, total)).wait())
+    gather_start(2, last_part, last_all, total, me, device)
+    gather_finish(2, last_all, total, device, me)
     totals = jnp.sum(last_all[...], axis=0)
     held = [totals[:, k : k + 1] for k in range(2 * ITERS)]
 
@@ -912,13 +923,21 @@
             inc_ref[c, i] = moved[low : low + count_y]
             res_ref[c, i] = rest[low : low + count_y]
 
-    def sent(step, carry):
-        other = lax.rem(b + step, n_micro)
-        route_copy(other, b).wait_send()
-        back_copy(other, b).wait_send()
-        return carry
-
-    lax.fori_loop(1, n_micro, sent, 0)
+    for buffer, semaphore in ((route_out, route_send), (back_out, back_send)):
+        others = buffer.at[pl.ds(0, n_micro - 1)]
+        pltpu.make_async_remote_copy(
+            src_ref=others,
+            dst_ref=others,
+            send_sem=semaphore.at[0],
+            recv_sem=semaphore.at[0],
+            device_id=(a, lax.rem(b + 1, n_micro)),
+            device_id_type=MESH,
+        ).wait_send()
+
+
+def hand_over(inc_in, res_in, inc_ref, res_ref):
+    inc_ref[...] = inc_in[...]
+    res_ref[...] = res_in[...]
 
 
 def shards(
@@ -945,9 +964,7 @@
     total = n_macro * n_micro
     sides = count_x + count_y + 1
     outer_rows = -(-(count_x + 3) * (count_y + 3) // 8) * 8
-    strips = len(strips_of(count_x, count_y))
     vmem = pl.BlockSpec(memory_space=pltpu.VMEM)
-    smem = pl.BlockSpec(memory_space=pltpu.SMEM)
     anywhere = pl.BlockSpec(memory_space=pl.ANY)
     dma = pltpu.SemaphoreType.DMA
 
@@ -960,11 +977,10 @@
     def body(*refs):
         newton_kernel((count_x, count_y, lanes, n_macro, n_micro), *refs)
 
-    return tuple(
-        pl.pallas_call(
+    outputs = pl.pallas_call(
             body,
             out_shape=[jax.ShapeDtypeStruct(load.shape, jnp.float32)] * 2,
-            in_specs=[anywhere] * 8 + [smem] * 2,
+            in_specs=[anywhere] * 8 + [vmem] * 2,
             out_specs=[vmem, vmem],
             scratch_shapes=[
                 held(*displacement.shape),
@@ -996,33 +1012,25 @@
                 held(ITERS, 3, rows, lanes),
                 held(ITERS, len(AROUND), side, lanes),
                 held(ITERS, len(AROUND), side, lanes),
-                held(16, 128),
-                held(n_micro, 16, 128),
-                held(16, 128),
-                held(n_macro, 16, 128),
+                held(8, 128),
+                held(n_micro, 8, 128),
+                held(8, 128),
+                held(n_macro, 8, 128),
                 held(1, 128),
                 held(total, 1, 128),
                 dma((8,)),
                 dma((3,)),
                 dma((3,)),
+                dma((1,)),
                 dma((n_micro,)),
+                dma((1,)),
                 dma((n_micro,)),
-                dma((n_micro,)),
-                dma((n_micro,)),
-                dma((sides,)),
-                dma((sides,)),
-                dma((ITERS, len(AROUND))),
-                dma((ITERS, len(AROUND))),
-                dma((n_micro - 1,)),
-                dma((n_micro - 1,)),
-                dma((n_macro - 1,)),
-                dma((n_macro - 1,)),
-                dma((total,)),
-                dma((total,)),
-                dma((len(AROUND),)),
-                dma((len(AROUND),)),
-                dma((strips,)),
-                dma((strips,)),
+                dma((3,)),
+                dma((3,)),
+                dma((2, len(AROUND))),
+                dma((2, len(AROUND))),
+                dma((3,)),
+                dma((3,)),
             ],
             compiler_params=pltpu.CompilerParams(collective_id=0, has_side_effects=True),
             name="newton_step",
@@ -1035,9 +1043,17 @@
             precond[0],
             forcing[0],
             coupling[0].T,
-            lame_first,
-            lame_shear,
-        )
+            lame_first.reshape(1, 1),
+            lame_shear.reshape(1, 1),
+        )
+    return tuple(
+        pl.pallas_call(
+            hand_over,
+            out_shape=[jax.ShapeDtypeStruct(load.shape, jnp.float32)] * 2,
+            in_specs=[vmem, vmem],
+            out_specs=[vmem, vmem],
+            name="hand_over",
+        )(*outputs)
     )
 
 

time: 58 us -> 55.5 us (0.957)
  local copies, waits for them, and re-layouts: 1.92 us -> 0 us
  Pallas kernels: 53.9 us -> 53.3 us
    unnamed x4 -> x0, local copies, waits for them, and re-layouts: 1.92 us -> none
    pallas_call x1, Pallas kernels: 53.9 us -> 52 us  [shards(): pl.pallas_call(body, out_shape=[jax.ShapeDtypeStruct(load.shape, jnp.floa...]
    pallas_call x0 -> x1, Pallas kernels: none -> 1.33 us  [shards(): pl.pallas_call(hand_over, out_shape=[jax.ShapeDtypeStruct(load.shape, jnp...]
where the time goes in v9:
time: 55.5 us; the launch traced here: 55.3 us
  Pallas kernels  53.3 us (96%)
  between operations  1.93 us (3%)
    pallas_call x1, Pallas kernels, shards(): pl.pallas_call(body, out_shape=[jax.ShapeDtypeStruct(load.shape, jnp.floa...  52 us
    pallas_call x1, Pallas kernels, shards(): pl.pallas_call(hand_over, out_shape=[jax.ShapeDtypeStruct(load.shape, jnp...  1.33 us

profile of v9, /device:TPU:0, one launch (start us, length us, event | category | flops | bytes accessed | tf_op | source)
XLA Modules:
  0.0 55.3 jit_solution(5988196567450466540)
XLA Ops:
  1.9 52.0 %newton_step.1 = (f32[3,2,2,256]{3,2,1,0:T(2,128)}, f32[3,2,2,256]{3,2,1,0:T(2,128)}) custom-call(f32[3,2,2,256]{3,2,1,0:T(2,128)} %refs_0_.1, f32[3,2,2,256]{3,2,1,0:T(2,128)} %refs_1_.1, s32[8,128]{1,0:T(8,128)} %bitcast.16, s32[8,128]{1,0:T(8,128)} %bitcast.17, bf16[512,512]{1,0:T(8,128)(2,1)} %bitcast.12, bf16[512,512]{1,0:T(8,128)(2,1)} %bitcast.13, ...), custom_call_target="tpu_custom_call" | custom-call | tf_op jit(solution)/shard_map/newton_step/pallas_call | solution.py:980
  53.9 1.3 %hand_over.1 = (f32[3,2,2,256]{3,2,1,0:T(2,128)}, f32[3,2,2,256]{3,2,1,0:T(2,128)}) custom-call(f32[3,2,2,256]{3,2,1,0:T(2,128)} %get-tuple-element.4.inc_in, f32[3,2,2,256]{3,2,1,0:T(2,128)} %get-tuple-element.5.res_in), custom_call_target="tpu_custom_call" | custom-call | tf_op jit(solution)/shard_map/hand_over/pallas_call | solution.py:1050

commit v10 on v9

--- a/solution.py
+++ b/solution.py
@@ -213,7 +213,6 @@
         inputs[name].wait()
     force = force_ref[...].astype(jnp.float32)
     force = jnp.concatenate([force, jnp.zeros((2, size), jnp.float32)], axis=0)
-    load_map = force.T
     wide_products[...] = jnp.zeros((tall, size), jnp.float32)
     coupling = couple_ref[...].astype(jnp.float32)
     wide_products[pl.ds(0, 6)] = coupling
@@ -244,12 +243,16 @@
     rank = jnp.zeros((groups, 128), jnp.float32)
     for owner in range(n_micro):
         rank = jnp.where(route == owner, ranks[owner * groups : (owner + 1) * groups], rank)
+    slot_type = jnp.bfloat16 if slots <= 256 else jnp.float32
     slot_at = lax.broadcasted_iota(jnp.int32, (slots, 128), 0).astype(jnp.float32)
+    slot_at = slot_at.astype(slot_type)
 
     def spot(owner, carry):
         local = jnp.where(route == owner, rank, -1.0)
         for g in range(groups):
-            hit = jnp.where(local[g : g + 1] == slot_at, 1.0, 0.0)
+            near_slot = jnp.broadcast_to(local[g : g + 1], (16, 128)).astype(slot_type)
+            near_slot = jnp.concatenate([near_slot] * (slots // 16), axis=0)
+            hit = jnp.where(near_slot == slot_at, slot_type(1), slot_type(0))
             low = pl.multiple_of(owner * slots, slots)
             spots[pl.ds(low, slots), g * 128 : (g + 1) * 128] = hit.astype(jnp.bfloat16)
         return carry
@@ -293,17 +296,20 @@
         inputs[name].wait()
 
     def split(exact):
-        high = exact.astype(jnp.bfloat16)
-        return jnp.concatenate([high, (exact - high.astype(jnp.float32)).astype(jnp.bfloat16)], axis=1)
+        high = exact.astype(jnp.bfloat16).astype(jnp.float32)
+        return jnp.concatenate([high, exact - high], axis=0)
 
     def through(matrix, exact):
-        moved = jnp.dot(matrix[...], split(exact), preferred_element_type=jnp.float32)
-        return moved[:, :8] + moved[:, 8:]
-
-    first_map = OMEGA * through(pre, load_map)
-    misfit_map = through(stiff, first_map) - load_map
-    for at, exact in enumerate((first_map, misfit_map, load_map)):
-        maps[pl.ds(at * size, size)] = split(exact)
+        moved = jnp.dot(
+            split(exact).astype(jnp.bfloat16), matrix[...], preferred_element_type=jnp.float32
+        )
+        return moved[:8] + moved[8:]
+
+    first_map = OMEGA * through(pre, force)
+    misfit_map = through(stiff, first_map) - force
+    turned = jnp.concatenate([split(first_map), split(misfit_map), split(force)], axis=0).T
+    for at in range(3):
+        maps[pl.ds(at * size, size)] = turned[:, at * 16 : (at + 1) * 16].astype(jnp.bfloat16)
     for c in range(3):
         for i, j in owned:
             basis[0, c, pl.ds((i + 1) * wide + j + 1, 1)] = disp_ref[c, i, j : j + 1]
@@ -734,19 +740,42 @@
             value = jnp.where(tile_row == at, piece, value)
         return value
 
+    def spread(at, src, dst, mine, row, column):
+        pltpu.make_async_remote_copy(
+            src_ref=src,
+            dst_ref=dst.at[mine],
+            send_sem=sum_send.at[at],
+            recv_sem=sum_recv.at[at],
+            device_id=(row, column),
+            device_id_type=MESH,
+        ).start()
+
     def gather_start(at, src, dst, count, mine, device):
-        def send(step):
-            pltpu.make_async_remote_copy(
-                src_ref=src,
-                dst_ref=dst.at[mine],
-                send_sem=sum_send.at[at],
-                recv_sem=sum_recv.at[at],
-                device_id=device(lax.rem(mine + step, count)),
-                device_id_type=MESH,
-            ).start()
-
-        every(count, send)
+        every(
+            count, lambda step: spread(at, src, dst, mine, *device(lax.rem(mine + step, count)))
+        )
         dst[mine] = src[...]
+
+    def gather_all(at, src, dst):
+        columns = [lax.rem(b + step, n_micro) for step in range(n_micro)] if total <= 32 else None
+        for step in range(n_macro - 1, -1, -1):
+            row = lax.rem(a + step, n_macro)
+            if columns is None:
+                lax.fori_loop(
+                    0 if step else 1,
+                    n_micro,
+                    lambda k, carry: (
+                        spread(at, src, dst, me, row, lax.rem(b + k, n_micro)),
+                        carry,
+                    )[1],
+                    0,
+                )
+            else:
+                order = sorted(range(n_micro), key=lambda k: -min(k, n_micro - k))
+                for k in order:
+                    if step or k:
+                        spread(at, src, dst, me, row, columns[k])
+        dst[me] = src[...]
 
     def gather_finish(at, dst, count, device, mine):
         others = dst.at[pl.ds(0, count - 1)]
@@ -868,7 +897,7 @@
     )
     last_part[...] = jnp.sum(jnp.where(diagonal, sums, 0.0), axis=0, keepdims=True)
 
-    gather_start(2, last_part, last_all, total, me, device)
+    gather_all(2, last_part, last_all)
     gather_finish(2, last_all, total, device, me)
     totals = jnp.sum(last_all[...], axis=0)
     held = [totals[:, k : k + 1] for k in range(2 * ITERS)]

time: 55.5 us -> 55.5 us (level)
  no operation moved by 1% of the time
where the time goes in v10:
time: 55.5 us; the launch traced here: 55.3 us
  Pallas kernels  53.3 us (96%)
  between operations  1.93 us (3%)
    pallas_call x1, Pallas kernels, shards(): pl.pallas_call(body, out_shape=[jax.ShapeDtypeStruct(load.shape, jnp.floa...  52 us
    pallas_call x1, Pallas kernels, shards(): pl.pallas_call(hand_over, out_shape=[jax.ShapeDtypeStruct(load.shape, jnp...  1.33 us

profile of v10, /device:TPU:0, one launch (start us, length us, event | category | flops | bytes accessed | tf_op | source)
XLA Modules:
  0.0 55.3 jit_solution(292541420331837443)
XLA Ops:
  1.9 52.0 %newton_step.1 = (f32[3,2,2,256]{3,2,1,0:T(2,128)}, f32[3,2,2,256]{3,2,1,0:T(2,128)}) custom-call(f32[3,2,2,256]{3,2,1,0:T(2,128)} %refs_0_.1, f32[3,2,2,256]{3,2,1,0:T(2,128)} %refs_1_.1, s32[8,128]{1,0:T(8,128)} %bitcast.16, s32[8,128]{1,0:T(8,128)} %bitcast.17, bf16[512,512]{1,0:T(8,128)(2,1)} %bitcast.12, bf16[512,512]{1,0:T(8,128)(2,1)} %bitcast.13, ...), custom_call_target="tpu_custom_call" | custom-call | tf_op jit(solution)/shard_map/newton_step/pallas_call | solution.py:1009
  53.9 1.3 %hand_over.1 = (f32[3,2,2,256]{3,2,1,0:T(2,128)}, f32[3,2,2,256]{3,2,1,0:T(2,128)}) custom-call(f32[3,2,2,256]{3,2,1,0:T(2,128)} %get-tuple-element.4.inc_in, f32[3,2,2,256]{3,2,1,0:T(2,128)} %get-tuple-element.5.res_in), custom_call_target="tpu_custom_call" | custom-call | tf_op jit(solution)/shard_map/hand_over/pallas_call | solution.py:1079

commit v11 on v10

--- a/solution.py
+++ b/solution.py
@@ -655,12 +655,15 @@
         dx, dy = AROUND[at]
         return [i * wide + j for i in pick(dx, count_x) for j in pick(dy, count_y)]
 
+    def filled(at):
+        return 3 * len(places(at, near))
+
     def hop(it, at):
         dx, dy = AROUND[at]
         other = len(AROUND) - 1 - at
         return pltpu.make_async_remote_copy(
-            src_ref=send_halo.at[it, at],
-            dst_ref=halo.at[it, other],
+            src_ref=send_halo.at[it, at, pl.ds(0, filled(at))],
+            dst_ref=halo.at[it, other, pl.ds(0, filled(at))],
             send_sem=send_sem.at[(it - 1) % 2, at],
             recv_sem=recv_sem.at[(it - 1) % 2, other],
             device_id=(a + dx, b + dy),
@@ -685,8 +688,8 @@
             def _():
                 hop(it, at).wait_send()
                 pltpu.make_async_remote_copy(
-                    src_ref=send_halo.at[it, at],
-                    dst_ref=halo.at[it, at],
+                    src_ref=send_halo.at[it, at, pl.ds(0, filled(at))],
+                    dst_ref=halo.at[it, at, pl.ds(0, filled(at))],
                     send_sem=send_sem.at[(it - 1) % 2, at],
                     recv_sem=recv_sem.at[(it - 1) % 2, at],
                     device_id=(a + dx, b + dy),
@@ -858,14 +861,24 @@
     middle[...] = jnp.sum(got_micro[...], axis=0)
     gather_start(1, middle, got_macro, n_macro, a, along_macro)
     halo_finish(2)
+    grown = applied(2)
+    for c in range(3):
+        basis[3, c] = grown[c]
+    halo_start(3)
     gather_finish(1, got_macro, n_macro, along_macro, a)
     totals = jnp.sum(jnp.sum(got_macro[...], axis=0), axis=1, keepdims=True)
     shift = jnp.sqrt(totals[1:2] / totals[0:1])
     scale = 1.0 / shift
+    halo_finish(3)
     for c in range(3):
-        u0, w1, w2 = basis[0, c], basis[1, c] * scale, basis[2, c] * (scale * scale)
-        basis[1, c] = w1 - u0
-        basis[2, c] = (w2 - w1) - (w1 - u0)
+        powers = [basis[0, c]]
+        factor = scale
+        for k in range(1, 4):
+            powers.append(basis[k, c] * factor)
+            factor = factor * scale
+        for k in range(1, 4):
+            powers = [later - sooner for sooner, later in zip(powers, powers[1:])]
+            basis[k, c] = powers[0]
 
     def field(it):
         return [basis[it, c] for c in range(3)]
@@ -875,19 +888,15 @@
         return [grown[c] * scale - jnp.where(own, basis[it, c], 0.0) for c in range(3)]
 
     moments = []
-    for it in range(2, ITERS):
+    for it in range(3, ITERS):
         grown = step(it)
         if it + 1 < ITERS:
             for c in range(3):
                 basis[it + 1, c] = grown[c]
             halo_start(it + 1)
-            if it == 2:
-                for k in range(3):
-                    moments.append(product(field(k), field(k)))
-                    moments.append(product(field(k), field(k + 1)))
-            else:
-                moments.append(product(field(it), field(it)))
-                moments.append(product(field(it), field(it + 1)))
+            for k in range(len(moments) // 2, it + 1):
+                moments.append(product(field(k), field(k)))
+                moments.append(product(field(k), field(k + 1)))
             halo_finish(it + 1)
     moments.append(product(field(ITERS - 1), field(ITERS - 1)))
     moments.append(product(field(ITERS - 1), grown))

time: 55.5 us -> 54.8 us (0.987)
  Pallas kernels: 53.3 us -> 52.6 us
    pallas_call x1, Pallas kernels: 52 us -> 51.3 us  [shards(): pl.pallas_call(body, out_shape=[jax.ShapeDtypeStruct(load.shape, jnp.floa...]
where the time goes in v11:
time: 54.8 us; the launch traced here: 54.6 us
  Pallas kernels  52.6 us (96%)
  between operations  1.93 us (4%)
    pallas_call x1, Pallas kernels, shards(): pl.pallas_call(body, out_shape=[jax.ShapeDtypeStruct(load.shape, jnp.floa...  51.3 us
    pallas_call x1, Pallas kernels, shards(): pl.pallas_call(hand_over, out_shape=[jax.ShapeDtypeStruct(load.shape, jnp...  1.33 us

profile of v11, /device:TPU:0, one launch (start us, length us, event | category | flops | bytes accessed | tf_op | source)
XLA Modules:
  0.0 54.6 jit_solution(7565326685433206150)
XLA Ops:
  1.9 51.3 %newton_step.1 = (f32[3,2,2,256]{3,2,1,0:T(2,128)}, f32[3,2,2,256]{3,2,1,0:T(2,128)}) custom-call(f32[3,2,2,256]{3,2,1,0:T(2,128)} %refs_0_.1, f32[3,2,2,256]{3,2,1,0:T(2,128)} %refs_1_.1, s32[8,128]{1,0:T(8,128)} %bitcast.16, s32[8,128]{1,0:T(8,128)} %bitcast.17, bf16[512,512]{1,0:T(8,128)(2,1)} %bitcast.12, bf16[512,512]{1,0:T(8,128)(2,1)} %bitcast.13, ...), custom_call_target="tpu_custom_call" | custom-call | tf_op jit(solution)/shard_map/newton_step/pallas_call | solution.py:1018
  53.2 1.3 %hand_over.1 = (f32[3,2,2,256]{3,2,1,0:T(2,128)}, f32[3,2,2,256]{3,2,1,0:T(2,128)}) custom-call(f32[3,2,2,256]{3,2,1,0:T(2,128)} %get-tuple-element.4.inc_in, f32[3,2,2,256]{3,2,1,0:T(2,128)} %get-tuple-element.5.res_in), custom_call_target="tpu_custom_call" | custom-call | tf_op jit(solution)/shard_map/hand_over/pallas_call | solution.py:1088

commit v12 on v11

--- a/solution.py
+++ b/solution.py
@@ -219,7 +219,7 @@
     couple[...] = wide_products[...].astype(jnp.bfloat16)
     wide_products[pl.ds(0, 6)] = jnp.zeros((6, size), jnp.float32)
     for at, (first, second) in enumerate(PAIRS):
-        wide_products[pl.ds(6 + at, 1)] = coupling[first : first + 1] * coupling[second : second + 1]
+        wide_products[pl.ds(8 + at, 1)] = coupling[first : first + 1] * coupling[second : second + 1]
     products[...] = wide_products[...].astype(jnp.bfloat16)
 
     route = routes_ref[...]
@@ -442,7 +442,7 @@
             amount = lame_first
         else:
             continue
-        base = jnp.where(tall_at == 6 + at, amount, base)
+        base = jnp.where(tall_at == 8 + at, amount, base)
 
     def back_copy(other, mine):
         return pltpu.make_async_remote_copy(
@@ -535,14 +535,18 @@
 
     lax.fori_loop(0, pairs, take_back, 0)
 
-    def side_copy(at):
+    even = len(PAIRS) // 8 * 8
+    parts = [part for part in ((0, even), (even, len(PAIRS) - even)) if part[1] > 0]
+
+    def side_copy(at, part):
         (dx, dy), place, _ = handed[at]
+        first, count = parts[part]
         low = column_at[place] * lanes
         return pltpu.make_async_remote_copy(
-            src_ref=values.at[pl.ds(8, tall - 8), pl.ds(low, lanes)],
-            dst_ref=beside.at[at],
-            send_sem=side_send.at[after.index((dx, dy))],
-            recv_sem=side_recv.at[after.index((dx, dy))],
+            src_ref=values.at[pl.ds(8 + first, count), pl.ds(low, lanes)],
+            dst_ref=beside.at[at, pl.ds(first, count)],
+            send_sem=side_send.at[part, after.index((dx, dy))],
+            recv_sem=side_recv.at[part, after.index((dx, dy))],
             device_id=(a + dx, b + dy),
             device_id_type=MESH,
         )
@@ -555,8 +559,8 @@
         way = AROUND.index((dx, dy))
         other = len(AROUND) - 1 - way
         return pltpu.make_async_remote_copy(
-            src_ref=values.at[pl.ds(0, 8), columns],
-            dst_ref=near_stress.at[other, pl.ds(0, 8), columns],
+            src_ref=values.at[pl.ds(0, 6), columns],
+            dst_ref=near_stress.at[other, pl.ds(0, 6), columns],
             send_sem=send_sem.at[1, way],
             recv_sem=recv_sem.at[1, other],
             device_id=(a + dx, b + dy),
@@ -567,7 +571,7 @@
         dx, dy = AROUND[way]
         offset = (dx, dy) if sent else (-dx, -dy)
         count = sum(count for place, _, count in strips if place == offset)
-        columns = near_stress.at[way, pl.ds(0, 8), pl.ds(0, count * lanes)]
+        columns = near_stress.at[way, pl.ds(0, 6), pl.ds(0, count * lanes)]
         return pltpu.make_async_remote_copy(
             src_ref=columns,
             dst_ref=columns,
@@ -594,7 +598,8 @@
 
         @pl.when(inside(dx, dy))
         def _():
-            side_copy(at).start()
+            for part in range(len(parts)):
+                side_copy(at, part).start()
 
     def span(step, count, below):
         if step == 0:
@@ -619,14 +624,15 @@
         for v in range(6):
             outer[v, pl.ds((i + 2) * broad + j + 2, 1)] = read(v)
 
-    def put_tangent(read, row, first=6):
-        for v in range(first, 6 + len(PAIRS)):
+    def put_tangent(read, row):
+        for v in range(len(PAIRS)):
             elem[v, pl.ds(row, 1)] = read(v)
 
     for at, (i, j) in enumerate(owned):
         put_stress(lambda v: values[v : v + 1, at * lanes : (at + 1) * lanes], i, j)
         put_tangent(
-            lambda v: values[v : v + 1, at * lanes : (at + 1) * lanes], (i + 1) * wide + j + 1
+            lambda v: values[8 + v : 9 + v, at * lanes : (at + 1) * lanes],
+            (i + 1) * wide + j + 1,
         )
     for at, (dx, dy) in enumerate(AROUND):
 
@@ -640,11 +646,6 @@
             for j, from_j in span(dy, count_y, 2):
                 low = column_at[from_i, from_j] * lanes
                 put_stress(lambda v: near_stress[at, v : v + 1, low : low + lanes], i, j)
-    for at, ((dx, dy), place, (i, j)) in enumerate(handed):
-        low = column_at[place] * lanes
-        source = AROUND.index((-dx, -dy))
-        for v in (6, 7):
-            elem[v, pl.ds(i * wide + j, 1)] = near_stress[source, v : v + 1, low : low + lanes]
     def near(step, count):
         return {0: list(range(1, count + 1)), -1: [1], 1: [count]}[step]
 
@@ -717,7 +718,7 @@
         for i in range(6):
             value = None
             for j in range(6):
-                term = elem[6 + PAIR_AT[(min(i, j), max(i, j))]] * strain[j]
+                term = elem[PAIR_AT[(min(i, j), max(i, j))]] * strain[j]
                 value = term if value is None else value + term
             stress.append(value)
         return [
@@ -822,28 +823,34 @@
             low = (i + 1) * broad + 1
             basis[0, c, pl.ds(i * wide, wide)] = pushed[low : low + wide]
         basis[0, c] = jnp.where(real, loads[c] - basis[0, c], 0.0)
-    for way, (dx, dy) in enumerate(after):
+    def sides_moved(way, part):
+        dx, dy = after[way]
         mine = [at for at, (offset, _, _) in enumerate(handed) if offset == (dx, dy)]
-        landed = beside.at[pl.ds(mine[0], len(mine))]
-        moved = pltpu.make_async_remote_copy(
+        first, count = parts[part]
+        landed = beside.at[pl.ds(mine[0], len(mine)), pl.ds(first, count)]
+        return pltpu.make_async_remote_copy(
             src_ref=landed,
             dst_ref=landed,
-            send_sem=side_send.at[way],
-            recv_sem=side_recv.at[way],
+            send_sem=side_send.at[part, way],
+            recv_sem=side_recv.at[part, way],
             device_id=(a + dx, b + dy),
             device_id_type=MESH,
         )
 
+    for way, (dx, dy) in enumerate(after):
+
         @pl.when(inside(dx, dy))
         def _():
-            moved.wait_send()
+            for part in range(len(parts)):
+                sides_moved(way, part).wait_send()
 
         @pl.when(inside(-dx, -dy))
         def _():
-            moved.wait_recv()
+            for part in range(len(parts)):
+                sides_moved(way, part).wait_recv()
 
     for at, (_, _, (i, j)) in enumerate(handed):
-        put_tangent(lambda v: beside[at, v - 8 : v - 7], i * wide + j, 8)
+        put_tangent(lambda v: beside[at, v : v + 1], i * wide + j)
 
     grown = applied(0)
     for c in range(3):
@@ -996,7 +1003,7 @@
     capacity = max(2, 2 * points // n_micro)
     slots = -(-capacity // 128) * 128
     size = stiffness.shape[1]
-    tall = -(-(6 + len(PAIRS)) // 8) * 8
+    tall = -(-(8 + len(PAIRS)) // 8) * 8
     rows = -(-(count_x + 2) * (count_y + 2) // 8) * 8
     side = -(-3 * max(count_x, count_y) // 8) * 8
     total = n_macro * n_micro
@@ -1046,7 +1053,7 @@
                 held(n_micro, tall, slots),
                 held(tall, points),
                 held(sides, tall - 8, lanes),
-                held(6 + len(PAIRS), rows, lanes),
+                held(len(PAIRS), rows, lanes),
                 held(ITERS, 3, rows, lanes),
                 held(ITERS, len(AROUND), side, lanes),
                 held(ITERS, len(AROUND), side, lanes),
@@ -1063,8 +1070,8 @@
                 dma((n_micro,)),
                 dma((1,)),
                 dma((n_micro,)),
-                dma((3,)),
-                dma((3,)),
+                dma((2, 3)),
+                dma((2, 3)),
                 dma((2, len(AROUND))),
                 dma((2, len(AROUND))),
                 dma((3,)),

time: 54.8 us -> 54.1 us (0.987)
  Pallas kernels: 52.6 us -> 52 us
    pallas_call x1, Pallas kernels: 51.3 us -> 50.6 us  [shards(): pl.pallas_call(body, out_shape=[jax.ShapeDtypeStruct(load.shape, jnp.floa...]
where the time goes in v12:
time: 54.1 us; the launch traced here: 53.9 us
  Pallas kernels  52 us (96%)
  between operations  1.93 us (4%)
    pallas_call x1, Pallas kernels, shards(): pl.pallas_call(body, out_shape=[jax.ShapeDtypeStruct(load.shape, jnp.floa...  50.6 us
    pallas_call x1, Pallas kernels, shards(): pl.pallas_call(hand_over, out_shape=[jax.ShapeDtypeStruct(load.shape, jnp...  1.33 us

profile of v12, /device:TPU:0, one launch (start us, length us, event | category | flops | bytes accessed | tf_op | source)
XLA Modules:
  0.0 53.9 jit_solution(2098163954909844843)
XLA Ops:
  1.9 50.6 %newton_step.1 = (f32[3,2,2,256]{3,2,1,0:T(2,128)}, f32[3,2,2,256]{3,2,1,0:T(2,128)}) custom-call(f32[3,2,2,256]{3,2,1,0:T(2,128)} %refs_0_.1, f32[3,2,2,256]{3,2,1,0:T(2,128)} %refs_1_.1, s32[8,128]{1,0:T(8,128)} %bitcast.16, s32[8,128]{1,0:T(8,128)} %bitcast.17, bf16[512,512]{1,0:T(8,128)(2,1)} %bitcast.12, bf16[512,512]{1,0:T(8,128)(2,1)} %bitcast.13, ...), custom_call_target="tpu_custom_call" | custom-call | tf_op jit(solution)/shard_map/newton_step/pallas_call | solution.py:1025
  52.6 1.3 %hand_over.1 = (f32[3,2,2,256]{3,2,1,0:T(2,128)}, f32[3,2,2,256]{3,2,1,0:T(2,128)}) custom-call(f32[3,2,2,256]{3,2,1,0:T(2,128)} %get-tuple-element.4.inc_in, f32[3,2,2,256]{3,2,1,0:T(2,128)} %get-tuple-element.5.res_in), custom_call_target="tpu_custom_call" | custom-call | tf_op jit(solution)/shard_map/hand_over/pallas_call | solution.py:1095

commit v13 on v12

--- a/solution.py
+++ b/solution.py
@@ -52,7 +52,7 @@
     pre,
     force_ref,
     couple_ref,
-    maps,
+    force_t,
     couple,
     products,
     wide_products,
@@ -295,21 +295,7 @@
     for name in ("pre", "stiff"):
         inputs[name].wait()
 
-    def split(exact):
-        high = exact.astype(jnp.bfloat16).astype(jnp.float32)
-        return jnp.concatenate([high, exact - high], axis=0)
-
-    def through(matrix, exact):
-        moved = jnp.dot(
-            split(exact).astype(jnp.bfloat16), matrix[...], preferred_element_type=jnp.float32
-        )
-        return moved[:8] + moved[8:]
-
-    first_map = OMEGA * through(pre, force)
-    misfit_map = through(stiff, first_map) - force
-    turned = jnp.concatenate([split(first_map), split(misfit_map), split(force)], axis=0).T
-    for at in range(3):
-        maps[pl.ds(at * size, size)] = turned[:, at * 16 : (at + 1) * 16].astype(jnp.bfloat16)
+    force_t[...] = force.T.astype(jnp.bfloat16)
     for c in range(3):
         for i, j in owned:
             basis[0, c, pl.ds((i + 1) * wide + j + 1, 1)] = disp_ref[c, i, j : j + 1]
@@ -467,22 +453,17 @@
             taken.append(route_in[other])
         points_in = jnp.concatenate(taken, axis=1)
         sweeps = points_in[6:7]
-        strain_in = points_in.astype(jnp.bfloat16)
-        strain_in = jnp.concatenate([strain_in, strain_in], axis=0)
-
-        def mapped(at):
-            return jnp.dot(
-                maps[pl.ds(at * size, size)], strain_in, preferred_element_type=jnp.float32
+        modal_load = jnp.dot(
+            force_t[...], points_in.astype(jnp.bfloat16), preferred_element_type=jnp.float32
+        )
+        modes = -OMEGA * jnp.dot(
+            pre[...], (-modal_load).astype(jnp.bfloat16), preferred_element_type=jnp.float32
+        )
+        for sweep in range(1, ITMAX):
+            misfit = jnp.dot(
+                stiff[...], modes.astype(jnp.bfloat16), preferred_element_type=jnp.float32
             )
-
-        modes, misfit, modal_load = mapped(0), mapped(1), mapped(2)
-        for sweep in range(1, ITMAX):
-            if sweep > 1:
-                misfit = jnp.dot(
-                    stiff[...], modes.astype(jnp.bfloat16), preferred_element_type=jnp.float32
-                )
-                misfit = misfit - modal_load
-            misfit = (misfit + BETA * jnp.tanh(modes)).astype(jnp.bfloat16)
+            misfit = (misfit + BETA * jnp.tanh(modes) - modal_load).astype(jnp.bfloat16)
             change = jnp.dot(pre[...], misfit, preferred_element_type=jnp.float32)
             modes = modes - jnp.where(sweeps > sweep, OMEGA, 0.0) * change
         bent = jnp.tanh(modes)
@@ -1036,7 +1017,7 @@
                 half(size, size),
                 half(6, size),
                 half(6, size),
-                half(3 * size, 16),
+                half(size, 8),
                 half(tall, size),
                 half(tall, size),
                 held(tall, size),

time: 54.1 us -> 55.8 us (1.031)
  Pallas kernels: 52 us -> 53.6 us
    pallas_call x1, Pallas kernels: 50.6 us -> 52.3 us  [shards(): pl.pallas_call(body, out_shape=[jax.ShapeDtypeStruct(load.shape, jnp.floa...]
where the time goes in v13:
time: 55.8 us; the launch traced here: 55.5 us
  Pallas kernels  53.6 us (96%)
  between operations  1.93 us (3%)
    pallas_call x1, Pallas kernels, shards(): pl.pallas_call(body, out_shape=[jax.ShapeDtypeStruct(load.shape, jnp.floa...  52.3 us
    pallas_call x1, Pallas kernels, shards(): pl.pallas_call(hand_over, out_shape=[jax.ShapeDtypeStruct(load.shape, jnp...  1.33 us

profile of v13, /device:TPU:0, one launch (start us, length us, event | category | flops | bytes accessed | tf_op | source)
XLA Modules:
  0.0 55.5 jit_solution(6680993506776668787)
XLA Ops:
  1.9 52.3 %newton_step.1 = (f32[3,2,2,256]{3,2,1,0:T(2,128)}, f32[3,2,2,256]{3,2,1,0:T(2,128)}) custom-call(f32[3,2,2,256]{3,2,1,0:T(2,128)} %refs_0_.1, f32[3,2,2,256]{3,2,1,0:T(2,128)} %refs_1_.1, s32[8,128]{1,0:T(8,128)} %bitcast.16, s32[8,128]{1,0:T(8,128)} %bitcast.17, bf16[512,512]{1,0:T(8,128)(2,1)} %bitcast.12, bf16[512,512]{1,0:T(8,128)(2,1)} %bitcast.13, ...), custom_call_target="tpu_custom_call" | custom-call | tf_op jit(solution)/shard_map/newton_step/pallas_call | solution.py:1006
  54.2 1.3 %hand_over.1 = (f32[3,2,2,256]{3,2,1,0:T(2,128)}, f32[3,2,2,256]{3,2,1,0:T(2,128)}) custom-call(f32[3,2,2,256]{3,2,1,0:T(2,128)} %get-tuple-element.4.inc_in, f32[3,2,2,256]{3,2,1,0:T(2,128)} %get-tuple-element.5.res_in), custom_call_target="tpu_custom_call" | custom-call | tf_op jit(solution)/shard_map/hand_over/pallas_call | solution.py:1076
